TPU v7x, 128 devices: a whole 4x4x4 slice. The times are simulated.
128 devices in a mesh: tx: 16 (over y, x), ty: 8 (over z, core).
Axes of the slice: x: 4, y: 4, z: 4, core: 2. Of those that a mesh axis runs over, the one named last changes fastest.
Arguments:
- potential: float32 [32768, 768], P(('tx', 'ty')), may hold values from -3 to 3
- gating: float32 [32768, 768], P(('tx', 'ty')), may hold values from -3 to 3
- ecs_start: float32 [512, 256, 32], P('tx', 'ty'), may hold values from -6 to 6
- templates: bfloat16 [10, 768, 768], replicated, may hold values from -0.21875 to 0.21875
- template_id: int32 [32768], P(('tx', 'ty')), may hold values from 0 to 9
- patch_src: int32 [131072], P(('tx', 'ty')), may hold values from 0 to 3071
- patch_dev: int32 [131072, 1], P(('tx', 'ty')), may hold values from 0 to 127; in each aligned block of 1024 rows (0 to 1023, 1024 to 2047, ...) at most 16 rows name the same one
- patch_dst: int32 [131072], P(('tx', 'ty')), may hold values from 0 to 3071
- patch_conduct: float32 [131072], P(('tx', 'ty')), may hold values from 0.5 to 2
- memb_point: int32 [393216], P(('tx', 'ty')), may hold values from 0 to 32767
Outputs:
- final_potential: float32 [32768, 768], P(('tx', 'ty'))
- final_ecs: float32 [512, 256, 32], P('tx', 'ty')
Inputs may be any that keep to these rules, and one draw needn't show every extreme that they name: `patch_dev`: among the 1024 gap junctions listed on one device, at most 16 have their target on any one device, and some device receives exactly 16 from some device.
All inputs are finite; a program needn't handle non-finite values.
Results may differ from a plain program's by a relative error of at most 0.0003.
Values sent between devices are 32-bit elements; how exact they have to be, the bound alone decides.
No kernel may reach another device: no remote copies, remote signals or barrier semaphores. Data moves between devices by JAX's collectives and lax.ppermute only.
A program may use at most 128 MiB of HBM per device.

v0:
```python
import functools

import jax
import jax.numpy as jnp
from jax import lax
from jax.experimental import pallas as pl
from jax.experimental.pallas import tpu as pltpu
from jax.sharding import PartitionSpec as P

BLOCK = 64
SWEEPS = 4
STEPS = 2
CELLS = 256
NODES = 768
PER = 12
DEVS = 128
CAP = 16
TILE = 32
HALO = 4
F32 = jnp.float32
BF16 = jnp.bfloat16
I32 = jnp.int32
AXES = ("tx", "ty")
VMEM = pl.BlockSpec(memory_space=pltpu.VMEM)
SMEM = pl.BlockSpec(memory_space=pltpu.SMEM)


def iota(shape, dim):
    return lax.broadcasted_iota(I32, shape, dim)


def low_half(rows):
    return iota((rows, 128), 1) < 64


def regroup(number):
    value = number.astype(F32)
    cell = jnp.floor((value + 0.5) * (1.0 / PER))
    return (value - PER * cell) * CELLS + cell


def split2(x):
    hi = x.astype(BF16).astype(F32)
    return hi, x - hi


def tables(by_lane):
    def rows(at):
        hi = by_lane[16 * at : 16 * at + 16, :]
        lo = by_lane[16 * at + 16 : 16 * at + 32, :]
        return (hi * 64.0 + lo).astype(I32)

    conduct = by_lane[64:80, :] + by_lane[80:96, :] + by_lane[96:112, :]
    return rows(0), rows(2), conduct


def setup_kernel(dev_ref, src_ref, dst_ref, conduct_ref, table_ref, own_ref, own_conduct_ref):
    device = iota((128, 128), 0)
    before = (device < iota((128, 128), 1)).astype(F32).astype(BF16)
    slots = iota((16, 128), 0)
    count = jnp.zeros((128, 1), F32)
    table = jnp.zeros((128, 128), F32)
    for q in range(8):
        hit = (dev_ref[q : q + 1, :] == device).astype(F32)
        hit_bf = hit.astype(BF16)
        running = jnp.dot(hit_bf, before, preferred_element_type=F32) + count
        rank = jnp.sum(hit * running, axis=0, keepdims=True)
        count = count + jnp.sum(hit, axis=1, keepdims=True)
        here = rank.astype(I32) == slots
        parts = []
        for ref in (dst_ref, src_ref):
            number = regroup(ref[q : q + 1, :])
            hi = jnp.floor(number * (1.0 / 64.0))
            parts += [hi, number - 64.0 * hi]
        first, rest = split2(conduct_ref[q : q + 1, :])
        second, third = split2(rest)
        parts += [first, second, third, jnp.zeros((1, 128), F32)]
        values = jnp.concatenate([jnp.where(here, part, 0.0) for part in parts], axis=0)
        table = table + lax.dot_general(
            hit_bf, values.astype(BF16), (((1,), (1,)), ((), ())), preferred_element_type=F32
        )
    table_ref[...] = table
    _, own, conduct = tables(table.T)
    own_ref[...] = own
    own_conduct_ref[...] = conduct


def doubled(volt, rows_ref):
    low = low_half(CELLS)
    for j in range(PER // 2):
        pair = volt[:, 128 * j : 128 * j + 128]
        turned = pltpu.roll(pair, 64, 1)
        rows_ref[512 * j : 512 * j + 256, :] = jnp.where(low, pair, turned)
        rows_ref[512 * j + 256 : 512 * j + 512, :] = jnp.where(low, turned, pair)


def gather_rows(rows_ref, index_ref, conduct_ref, out_ref, offset, stride):
    low = low_half(1)

    def body(d, carry):
        for p in range(8):
            a = index_ref[2 * p, d]
            b = index_ref[2 * p + 1, d]
            scale = jnp.where(low, conduct_ref[2 * p, d], conduct_ref[2 * p + 1, d])
            row = jnp.where(low, rows_ref[pl.ds(a, 1), :], rows_ref[pl.ds(b, 1), :])
            out_ref[pl.ds(d * stride + offset + p, 1), :] = row * scale
        return carry

    lax.fori_loop(0, DEVS, body, 0)


def first_gather_kernel(own_ref, conduct_ref, volt_ref, out_ref, rows_ref):
    doubled(volt_ref[...], rows_ref)
    gather_rows(rows_ref, own_ref, conduct_ref, out_ref, 0, 8)


def second_gather_kernel(
    table_ref, volt_ref, sent_ref, out_ref, into_ref, into_conduct_ref, rows_ref, index_sm, conduct_sm, sem
):
    into, _, conduct = tables(table_ref[...].T)
    into_ref[...] = into
    into_conduct_ref[...] = conduct
    one = pltpu.make_async_copy(into_ref, index_sm, sem.at[0])
    two = pltpu.make_async_copy(into_conduct_ref, conduct_sm, sem.at[1])
    one.start()
    two.start()
    doubled(volt_ref[...], rows_ref)
    for d in range(DEVS):
        out_ref[16 * d : 16 * d + 8, :] = sent_ref[8 * d : 8 * d + 8, :]
    one.wait()
    two.wait()
    gather_rows(rows_ref, index_sm, conduct_sm, out_ref, 8, 16)


def degree_kernel(into_ref, into_conduct_ref, own_ref, own_conduct_ref, out_ref):
    cell = iota((CELLS, 128), 0)
    kind = iota((16, 128), 0)
    total = jnp.zeros((CELLS, 48), F32)
    for index_ref, conduct_ref in ((into_ref, into_conduct_ref), (own_ref, own_conduct_ref)):
        for s in range(CAP):
            number = index_ref[s : s + 1, :]
            hit = ((number & 255) == cell).astype(F32).astype(BF16)
            here = (number >> 8) == kind
            first, rest = split2(conduct_ref[s : s + 1, :])
            second, third = split2(rest)
            values = jnp.concatenate([jnp.where(here, x, 0.0) for x in (first, second, third)], axis=0)
            total = total + lax.dot_general(
                hit, values.astype(BF16), (((1,), (1,)), ((), ())), preferred_element_type=F32
            )
    out_ref[...] = total[:, 0:16] + total[:, 16:32] + total[:, 32:48]


def base_kernel(volt_ref, recov_ref, id_ref, degree_ref, template_ref, out_ref, volt_bf):
    index = pl.program_id(0)

    @pl.when(index == 0)
    def _():
        volt_bf[...] = volt_ref[...].astype(BF16)
        out_ref[...] = jnp.zeros_like(out_ref)

    masked = jnp.where(id_ref[...] == index, volt_bf[...], jnp.zeros((), BF16))
    out_ref[...] += jnp.dot(masked, template_ref[0], preferred_element_type=F32)

    @pl.when(index == pl.num_programs(0) - 1)
    def _():
        low = low_half(CELLS)
        for j in range(PER // 2):
            cut = slice(128 * j, 128 * j + 128)
            volt = volt_ref[:, cut]
            ion = volt - volt * volt * volt * (1.0 / 3.0) - recov_ref[:, cut]
            degree = jnp.where(low, degree_ref[:, 2 * j : 2 * j + 1], degree_ref[:, 2 * j + 1 : 2 * j + 2])
            out_ref[:, cut] += degree * volt - ion


def grid_row(point):
    return ((point >> 7) & 7) * TILE + (point >> 10)


def gap_kernel(
    into_ref,
    own_ref,
    got_ref,
    base_ref,
    point_col_ref,
    point_row_ref,
    phi_ref,
    current_ref,
    deposit_ref,
    x_low_ref,
    x_high_ref,
    y_low_ref,
    y_high_ref,
    ll_ref,
    lh_ref,
    hl_ref,
    hh_ref,
    even_in,
    odd_in,
    even_out,
    odd_out,
):
    for ref in (even_in, odd_in, even_out, odd_out):
        ref[...] = jnp.zeros_like(ref)

    def body(d, carry):
        for p in range(8):
            row = got_ref[pl.ds(d * 16 + p, 1), :]
            back = got_ref[pl.ds(d * 16 + 8 + p, 1), :]
            even_in[pl.ds(into_ref[2 * p, d], 1), :] += row
            odd_in[pl.ds(into_ref[2 * p + 1, d], 1), :] += row
            even_out[pl.ds(own_ref[2 * p, d], 1), :] += back
            odd_out[pl.ds(own_ref[2 * p + 1, d], 1), :] += back
        return carry

    lax.fori_loop(0, DEVS, body, 0)

    low = low_half(CELLS)
    lane = iota((CELLS, 128), 1)
    row_of = iota((CELLS, CELLS), 0)
    total = jnp.zeros((CELLS, 256), F32)
    for j in range(PER // 2):
        sums = []
        for k in (2 * j, 2 * j + 1):
            cut = slice(CELLS * k, CELLS * k + CELLS)
            even = even_in[cut, :] + even_out[cut, :]
            odd = odd_in[cut, :] + odd_out[cut, :]
            both = jnp.where(low, even, odd)
            sums.append(both + pltpu.roll(both, 64, 1))
        cut = slice(128 * j, 128 * j + 128)
        current = base_ref[:, cut] - jnp.where(low, sums[0], sums[1])
        current_ref[:, cut] = current
        for k, part in ((2 * j, jnp.where(low, current, 0.0)), (2 * j + 1, jnp.where(low, 0.0, current))):
            mean = jnp.sum(part, axis=1, keepdims=True) * (1.0 / BLOCK)
            hi, lo = split2(mean)
            here = (point_col_ref[:, k : k + 1] & 127) == lane
            spread = jnp.concatenate([jnp.where(here, hi, 0.0), jnp.where(here, lo, 0.0)], axis=1)
            hit = (grid_row(point_row_ref[k : k + 1, :]) == row_of).astype(F32).astype(BF16)
            total = total + jnp.dot(hit, spread.astype(BF16), preferred_element_type=F32)
    total = total[:, 0:128] + total[:, 128:256]
    for t in range(8):
        deposit_ref[:, 128 * t : 128 * t + 128] = total[TILE * t : TILE * t + TILE, :]
    far = TILE - HALO
    for array, at in ((phi_ref, 0), (deposit_ref, HALO)):
        x_low_ref[at : at + HALO, :] = array[0:HALO, :]
        x_high_ref[at : at + HALO, :] = array[far:TILE, :]
        y_low_ref[8 * at : 8 * at + TILE, :] = array[:, 0:128]
        y_high_ref[8 * at : 8 * at + TILE, :] = array[:, 896:1024]
        ll_ref[at : at + HALO, :] = array[0:HALO, 0:128]
        lh_ref[at : at + HALO, :] = array[0:HALO, 896:1024]
        hl_ref[at : at + HALO, :] = array[far:TILE, 0:128]
        hh_ref[at : at + HALO, :] = array[far:TILE, 896:1024]


def sweep_kernel(last, *refs):
    (
        place_ref,
        phi_ref,
        deposit_ref,
        x_before_ref,
        x_after_ref,
        y_before_ref,
        y_after_ref,
        bb_ref,
        ba_ref,
        ab_ref,
        aa_ref,
        current_ref,
        volt_ref,
        point_col_ref,
    ) = refs[:14]
    if last:
        volt_out, phi_out, wide_phi, wide_deposit = refs[14:]
    else:
        (
            recov_ref,
            into_ref,
            into_conduct_ref,
            own_ref,
            own_conduct_ref,
            volt_out,
            phi_out,
            recov_out,
            send_out,
            wide_phi,
            wide_deposit,
            rows_ref,
        ) = refs[14:]
    high = TILE + HALO
    for wide, at in ((wide_phi, 0), (wide_deposit, HALO)):
        wide[0:HALO, 128:1152] = x_before_ref[at : at + HALO, :]
        wide[high : high + HALO, 128:1152] = x_after_ref[at : at + HALO, :]
        wide[HALO:high, 0:128] = y_before_ref[8 * at : 8 * at + TILE, :]
        wide[HALO:high, 1152:1280] = y_after_ref[8 * at : 8 * at + TILE, :]
        wide[0:HALO, 0:128] = bb_ref[at : at + HALO, :]
        wide[0:HALO, 1152:1280] = ba_ref[at : at + HALO, :]
        wide[high : high + HALO, 0:128] = ab_ref[at : at + HALO, :]
        wide[high : high + HALO, 1152:1280] = aa_ref[at : at + HALO, :]
    wide_phi[HALO:high, 128:1152] = phi_ref[...]
    wide_deposit[HALO:high, 128:1152] = deposit_ref[...]
    shape = (TILE + 2 * HALO, 1280)
    row = iota(shape, 0)
    lane = iota(shape, 1)
    first_row = jnp.where(place_ref[0] == 0, HALO, 0)
    last_row = jnp.where(place_ref[0] == place_ref[2] - 1, high, high + HALO)
    first_lane = jnp.where(place_ref[1] == 0, 128, 0)
    last_lane = jnp.where(place_ref[1] == place_ref[3] - 1, 1152, 1280)
    inside = (row >= first_row) & (row < last_row) & (lane >= first_lane) & (lane < last_lane)
    depth = lane & (TILE - 1)
    wide_phi[...] = jnp.where(inside, wide_phi[...], 0.0)
    for sweep in range(SWEEPS):
        phi = wide_phi[...]
        total = wide_deposit[...] + pltpu.roll(phi, 1, 0) + pltpu.roll(phi, shape[0] - 1, 0)
        total = total + pltpu.roll(phi, 32, 1) + pltpu.roll(phi, shape[1] - 32, 1)
        total = total + jnp.where(depth == 0, 0.0, pltpu.roll(phi, 1, 1))
        total = total + jnp.where(depth == TILE - 1, 0.0, pltpu.roll(phi, shape[1] - 1, 1))
        wide_phi[...] = jnp.where(inside, total * (1.0 / 6.5), 0.0)
    phi = wide_phi[HALO:high, 128:1152]
    phi_out[...] = phi
    stacked = jnp.concatenate([phi[:, 128 * t : 128 * t + 128] for t in range(8)], axis=0)
    hi, lo = split2(stacked)
    pieces = jnp.concatenate([hi, lo], axis=1).astype(BF16)
    low = low_half(CELLS)
    lane = iota((CELLS, 128), 1)
    column = iota((CELLS, CELLS), 1)
    for j in range(PER // 2):
        at_patch = []
        for k in (2 * j, 2 * j + 1):
            point = point_col_ref[:, k : k + 1]
            hit = (grid_row(point) == column).astype(F32).astype(BF16)
            found = jnp.dot(hit, pieces, preferred_element_type=F32)
            found = found[:, 0:128] + found[:, 128:256]
            at_patch.append(jnp.sum(jnp.where((point & 127) == lane, found, 0.0), axis=1, keepdims=True))
        cut = slice(128 * j, 128 * j + 128)
        volt = volt_ref[:, cut]
        fresh = volt - 0.05 * (current_ref[:, cut] + jnp.where(low, at_patch[0], at_patch[1]))
        volt_out[:, cut] = fresh
        if not last:
            recov = recov_ref[:, cut]
            recov_out[:, cut] = recov + 0.05 * 0.08 * (volt + 0.7 - 0.8 * recov)
            turned = pltpu.roll(fresh, 64, 1)
            rows_ref[512 * j : 512 * j + 256, :] = jnp.where(low, fresh, turned)
            rows_ref[512 * j + 256 : 512 * j + 512, :] = jnp.where(low, turned, fresh)
    if not last:
        gather_rows(rows_ref, own_ref, own_conduct_ref, send_out, 0, 16)
        gather_rows(rows_ref, into_ref, into_conduct_ref, send_out, 8, 16)


def shaped(*shape, dtype=F32):
    return jax.ShapeDtypeStruct(shape, dtype)


def exchange(x):
    return lax.all_to_all(x, AXES, split_axis=0, concat_axis=0, tiled=True)


def send(x, by_x, by_y):
    size_x = lax.axis_size("tx")
    size_y = lax.axis_size("ty")
    if by_y == 0:
        return lax.ppermute(x, "tx", [(i, (i + by_x) % size_x) for i in range(size_x)])
    if by_x == 0:
        return lax.ppermute(x, "ty", [(i, (i + by_y) % size_y) for i in range(size_y)])
    moves = [
        (i * size_y + j, (i + by_x) % size_x * size_y + (j + by_y) % size_y)
        for i in range(size_x)
        for j in range(size_y)
    ]
    return lax.ppermute(x, AXES, moves)


def on_device(
    potential,
    gating,
    ecs_start,
    templates,
    template_id,
    patch_src,
    patch_dev,
    patch_dst,
    patch_conduct,
    memb_point,
):
    flat = (8, 128)
    table, own, own_conduct = pl.pallas_call(
        setup_kernel,
        out_shape=(shaped(128, 128), shaped(CAP, 128, dtype=I32), shaped(CAP, 128)),
        in_specs=[VMEM] * 4,
        out_specs=(VMEM,) * 3,
        name="setup",
    )(
        patch_dev.reshape(flat),
        patch_src.reshape(flat),
        patch_dst.reshape(flat),
        patch_conduct.reshape(flat),
    )
    got_table = exchange(table)
    rows_scratch = pltpu.VMEM((PER * CELLS, 128), F32)
    sent = pl.pallas_call(
        first_gather_kernel,
        out_shape=shaped(DEVS * 8, 128),
        in_specs=[SMEM, SMEM, VMEM],
        out_specs=VMEM,
        scratch_shapes=[rows_scratch],
        name="gather_source",
    )(own, own_conduct, potential)
    outgoing, into, into_conduct = pl.pallas_call(
        second_gather_kernel,
        out_shape=(shaped(DEVS * 16, 128), shaped(CAP, 128, dtype=I32), shaped(CAP, 128)),
        in_specs=[VMEM] * 3,
        out_specs=(VMEM,) * 3,
        scratch_shapes=[
            rows_scratch,
            pltpu.SMEM((CAP, 128), I32),
            pltpu.SMEM((CAP, 128), F32),
            pltpu.SemaphoreType.DMA((2,)),
        ],
        name="gather_target",
    )(got_table, potential, sent)
    degree = pl.pallas_call(
        degree_kernel,
        out_shape=shaped(CELLS, 16),
        in_specs=[VMEM] * 4,
        out_specs=VMEM,
        name="degree",
    )(into, into_conduct, own, own_conduct)

    place = jnp.stack([lax.axis_index("tx"), lax.axis_index("ty"), lax.axis_size("tx"), lax.axis_size("ty")])
    place = place.astype(I32)
    point_col = memb_point.reshape(CELLS, PER)
    point_row = point_col.T
    id_col = template_id.reshape(CELLS, 1)
    volt = potential
    recov = gating
    phi = ecs_start.reshape(TILE, TILE * TILE)
    whole = lambda *shape: pl.BlockSpec(shape, lambda i: (0,) * len(shape))
    for step in range(STEPS):
        last = step == STEPS - 1
        got = exchange(outgoing.reshape(DEVS, 16, 128)).reshape(DEVS * 16, 128)
        base = pl.pallas_call(
            base_kernel,
            grid=(templates.shape[0],),
            out_shape=shaped(CELLS, NODES),
            in_specs=[
                whole(CELLS, NODES),
                whole(CELLS, NODES),
                whole(CELLS, 1),
                whole(CELLS, 16),
                pl.BlockSpec((1, NODES, NODES), lambda i: (i, 0, 0)),
            ],
            out_specs=whole(CELLS, NODES),
            scratch_shapes=[pltpu.VMEM((CELLS, NODES), BF16)],
            cost_estimate=pl.CostEstimate(flops=3_000_000_000, bytes_accessed=14_000_000, transcendentals=0),
            name="base",
        )(volt, recov, id_col, degree, templates)
        accumulator = pltpu.VMEM((PER * CELLS, 128), F32)
        slabs = (shaped(8, 1024),) * 2 + (shaped(64, 128),) * 2 + (shaped(8, 128),) * 4
        current, deposit, *edges = pl.pallas_call(
            gap_kernel,
            out_shape=(shaped(CELLS, NODES), shaped(TILE, 1024)) + slabs,
            in_specs=[SMEM] * 2 + [VMEM] * 5,
            out_specs=(VMEM,) * 10,
            scratch_shapes=[accumulator] * 4,
            name="gap",
        )(into, own, got, base, point_col, point_row, phi)
        ways = ((-1, 0), (1, 0), (0, -1), (0, 1), (-1, -1), (-1, 1), (1, -1), (1, 1))
        came = [send(edge, *way) for edge, way in zip(edges, ways)]
        x_after, x_before, y_after, y_before, aa, ab, ba, bb = came
        operands = [place, phi, deposit, x_before, x_after, y_before, y_after, bb, ba, ab, aa, current, volt, point_col]
        specs = [SMEM] + [VMEM] * 13
        wide = [pltpu.VMEM((TILE + 2 * HALO, 1280), F32)] * 2
        outs = (shaped(CELLS, NODES), shaped(TILE, 1024))
        if last:
            volt, phi = pl.pallas_call(
                functools.partial(sweep_kernel, True),
                out_shape=outs,
                in_specs=specs,
                out_specs=(VMEM,) * 2,
                scratch_shapes=wide,
                name="sweep_last",
            )(*operands)
        else:
            volt, phi, recov, outgoing = pl.pallas_call(
                functools.partial(sweep_kernel, False),
                out_shape=outs + (shaped(CELLS, NODES), shaped(DEVS * 16, 128)),
                in_specs=specs + [VMEM] + [SMEM] * 4,
                out_specs=(VMEM,) * 4,
                scratch_shapes=wide + [rows_scratch],
                name="sweep",
            )(*operands, recov, into, into_conduct, own, own_conduct)
    return (volt, phi.reshape(TILE, TILE, TILE))


def solution(mesh):
    return jax.shard_map(
        on_device,
        mesh=mesh,
        in_specs=(
            P(("tx", "ty"), None),
            P(("tx", "ty"), None),
            P("tx", "ty", None),
            P(),
            P(("tx", "ty")),
            P(("tx", "ty")),
            P(("tx", "ty"), None),
            P(("tx", "ty")),
            P(("tx", "ty")),
            P(("tx", "ty")),
        ),
        out_specs=(P(("tx", "ty"), None), P("tx", "ty", None)),
        check_vma=False,
    )
```

profile of v0, /device:TPU:31, one launch (start us, length us, event | category | flops | bytes accessed | tf_op | source)
XLA Modules:
  0.0 183.5 jit_solution(15479723428492135321)
XLA Ops:
  0.6 2.1 %setup.1 = (f32[128,128]{1,0:T(8,128)}, s32[16,128]{1,0:T(8,128)}, f32[16,128]{1,0:T(8,128)}) custom-call(s32[8,128]{1,0:T(8,128)} %bitcast.24, s32[8,128]{1,0:T(8,128)} %bitcast.25, s32[8,128]{1,0:T(8,128)} %bitcast.26, f32[8,128]{1,0:T(8,128)} %bitcast.27), custom_call_target="tpu_custom_call" | custom-call | tf_op jit(solution)/shard_map/setup/pallas_call | solution.py:384
  2.8 10.5 %all-to-all-start = ((f32[128,1,128]{2,1,0:T(1,128)}), f32[128,1,128]{2,1,0:T(1,128)S(1)}, u32[]{:S(2)}, u32[]{:S(2)}) async-start(f32[128,1,128]{2,1,0:T(1,128)} %bitcast.23), calls=%async_computation | async-start | bytes 131072 | tf_op jit(solution)/shard_map/all_to_all | solution.py:353
  13.3 5.7 %gather_source.1.sent_ref = f32[1024,128]{1,0:T(8,128)} custom-call(s32[16,128]{1,0:T(8,128)} %get-tuple-element.35.own_ref.refs_17_, f32[16,128]{1,0:T(8,128)} %get-tuple-element.36.conduct_ref.own_conduct_ref.refs_18_, f32[256,768]{1,0:T(8,128)} %refs_12_.1), custom_call_target="tpu_custom_call" | custom-call | tf_op jit(solution)/shard_map/gather_source/pallas_call | solution.py:398
  20.2 6.7 %gather_target.1 = (f32[2048,128]{1,0:T(8,128)}, s32[16,128]{1,0:T(8,128)}, f32[16,128]{1,0:T(8,128)}) custom-call(f32[128,128]{1,0:T(8,128)} %bitcast.20, f32[256,768]{1,0:T(8,128)} %refs_12_.1, f32[1024,128]{1,0:T(8,128)} %gather_source.1.sent_ref), custom_call_target="tpu_custom_call" | custom-call | tf_op jit(solution)/shard_map/gather_target/pallas_call | solution.py:406
  26.9 9.2 %all-to-all-start.1 = ((f32[128,16,128]{2,1,0:T(8,128)}), f32[128,16,128]{2,1,0:T(8,128)S(1)}, u32[]{:S(2)}, u32[]{:S(2)}) async-start(f32[128,16,128]{2,1,0:T(8,128)} %bitcast.19), calls=%async_computation.1 | async-start | bytes 2097152 | tf_op jit(solution)/shard_map/all_to_all | solution.py:353
  37.7 1.9 %reshape.42.phi_ref.refs_1_ = f32[32,1024]{1,0:T(8,128)} reshape(f32[32,32,32]{2,1,0:T(8,128)} %param.12) | data formatting | bytes 262144 | tf_op jit(solution)/shard_map/reshape | solution.py:434
  41.1 2.2 %degree.1.degree_ref = f32[256,16]{1,0:T(8,128)} custom-call(s32[16,128]{1,0:T(8,128)} %get-tuple-element.37.into_ref.refs_15_, f32[16,128]{1,0:T(8,128)} %get-tuple-element.39.into_conduct_ref.refs_16_, s32[16,128]{1,0:T(8,128)} %get-tuple-element.35.own_ref.refs_17_, f32[16,128]{1,0:T(8,128)} %get-tuple-element.36.conduct_ref.own_conduct_ref.refs_18_), custom_call_target="tpu_custom_call" | custom-call | tf_op jit(solution)/shard_map/degree/pallas_call | solution.py:419
  43.3 11.9 %base.2.base_ref = f32[256,768]{1,0:T(8,128)} custom-call(f32[256,768]{1,0:T(8,128)} %refs_12_.1, f32[256,768]{1,0:T(8,128)} %refs_14_.1, s32[256,1]{1,0:T(8,128)} %copy.18.id_ref, f32[256,16]{1,0:T(8,128)} %degree.1.degree_ref, bf16[10,768,768]{2,1,0:T(8,128)(2,1)} %template_ref.3), custom_call_target="tpu_custom_call" | custom-call | flops 3000000000 | bytes 14000000 | tf_op jit(solution)/shard_map/base/pallas_call | solution.py:439
  56.2 11.5 %gap.2 = (f32[256,768]{1,0:T(8,128)}, f32[32,1024]{1,0:T(8,128)}, f32[8,1024]{1,0:T(8,128)}, f32[8,1024]{1,0:T(8,128)}, f32[64,128]{1,0:T(8,128)}, /*index=5*/f3...) custom-call(s32[16,128]{1,0:T(8,128)} %get-tuple-element.37.into_ref.refs_15_, ...), custom_call_target="tpu_custom_call" | custom-call | tf_op jit(solution)/shard_map/gap/pallas_call | solution.py:457
  69.0 2.4 %collective-permute-start.6 = (f32[8,128]{1,0:T(8,128)}, f32[8,128]{1,0:T(8,128)S(1)}, u32[]{:S(2)}, u32[]{:S(2)}) collective-permute-start(f32[8,128]{1,0:T(8,128)} %get-tuple-element.47), channel_id=1, source_target_pairs={{0,121},{1,122},{2,123},{3,124},{4,125},{5,126},{6,127},{7,120},{8... | collective-permute-start | bytes 12296 | tf_op jit(solution)/shard_map/ppermute | solution.py:368
  72.4 3.9 %collective-permute-start = (f32[8,1024]{1,0:T(8,128)}, f32[8,1024]{1,0:T(8,128)S(1)}, u32[]{:S(2)}, u32[]{:S(2)}) collective-permute-start(f32[8,1024]{1,0:T(8,128)} %get-tuple-element.41), channel_id=1, source_target_pairs={{0,8},{8,16},{16,24},{24,32},{32,40},{40,48},{48,56},{56,64},{64,7... | collective-permute-start | bytes 98312 | tf_op jit(solution)/shard_map/ppermute | solution.py:360
  78.0 2.3 %collective-permute-start.3 = (f32[64,128]{1,0:T(8,128)}, f32[64,128]{1,0:T(8,128)S(1)}, u32[]{:S(2)}, u32[]{:S(2)}) collective-permute-start(f32[64,128]{1,0:T(8,128)} %get-tuple-element.44), channel_id=1, source_target_pairs={{0,7},{1,0},{2,1},{3,2},{4,3},{5,4},{6,5},{7,6},{8,15},{9,8},{10,9... | collective-permute-start | bytes 98312 | tf_op jit(solution)/shard_map/ppermute | solution.py:362
  83.3 15.1 %sweep.1 = (f32[256,768]{1,0:T(8,128)}, f32[32,1024]{1,0:T(8,128)}, f32[256,768]{1,0:T(8,128)}, f32[2048,128]{1,0:T(8,128)}) custom-call(s32[4]{0:T(128)} %pad_add_fusion.refs_0_, f32[32,1024]{1,0:T(8,128)} %reshape.42.phi_ref.refs_1_, f32[32,1024]{1,0:T(8,128)} %get-tuple-element.40.refs_2_, f32[8,1024]{1,0:T(8,128)} %copy-done.6, f32[8,1024]{1,0:T(8,128)} %copy-done.9, ...), custom_call_target="tpu_custom_call" | custom-call | tf_op jit(solution)/shard_map/sweep/pallas_call | solution.py:482
  98.4 11.0 %all-to-all-start.2 = ((f32[128,16,128]{2,1,0:T(8,128)}), f32[128,16,128]{2,1,0:T(8,128)S(1)}, u32[]{:S(2)}, u32[]{:S(2)}) async-start(f32[128,16,128]{2,1,0:T(8,128)} %bitcast.18), calls=%async_computation.2 | async-start | bytes 2097152 | tf_op jit(solution)/shard_map/all_to_all | solution.py:353
  109.4 11.9 %base.3.base_ref = f32[256,768]{1,0:T(8,128)} custom-call(f32[256,768]{1,0:T(8,128)} %get-tuple-element.52.volt_ref.refs_12_, f32[256,768]{1,0:T(8,128)} %get-tuple-element.53.recov_ref, s32[256,1]{1,0:T(8,128)} %copy.18.id_ref, f32[256,16]{1,0:T(8,128)} %degree.1.degree_ref, bf16[10,768,768]{2,1,0:T(8,128)(2,1)} %template_ref.3), custom_call_target="tpu_custom_call" | custom-call | flops 3000000000 | bytes 14000000 | tf_op jit(solution)/shard_map/base/pallas_call | solution.py:439
  121.3 3.6 %all-to-all-done.2 = f32[128,16,128]{2,1,0:T(8,128)S(1)} async-done(((f32[128,16,128]{2,1,0:T(8,128)}), f32[128,16,128]{2,1,0:T(8,128)S(1)}, u32[]{:S(2)}, u32[]{:S(2)}) %all-to-all-start.2) | async-done | bytes 1048608 | tf_op jit(solution)/shard_map/all_to_all | solution.py:353
  125.9 11.5 %gap.3 = (f32[256,768]{1,0:T(8,128)}, f32[32,1024]{1,0:T(8,128)}, f32[8,1024]{1,0:T(8,128)}, f32[8,1024]{1,0:T(8,128)}, f32[64,128]{1,0:T(8,128)}, /*index=5*/f3...) custom-call(s32[16,128]{1,0:T(8,128)} %get-tuple-element.37.into_ref.refs_15_, ...), custom_call_target="tpu_custom_call" | custom-call | tf_op jit(solution)/shard_map/gap/pallas_call | solution.py:457
  137.4 3.2 %collective-permute-start.8 = (f32[8,1024]{1,0:T(8,128)}, f32[8,1024]{1,0:T(8,128)S(1)}, u32[]{:S(2)}, u32[]{:S(2)}) collective-permute-start(f32[8,1024]{1,0:T(8,128)} %get-tuple-element.55), channel_id=1, source_target_pairs={{0,8},{8,16},{16,24},{24,32},{32,40},{40,48},{48,56},{56,64},{64,7... | collective-permute-start | bytes 98312 | tf_op jit(solution)/shard_map/ppermute | solution.py:360
  142.2 6.3 %collective-permute-start.12 = (f32[8,128]{1,0:T(8,128)}, f32[8,128]{1,0:T(8,128)S(1)}, u32[]{:S(2)}, u32[]{:S(2)}) collective-permute-start(f32[8,128]{1,0:T(8,128)} %get-tuple-element.59), channel_id=1, source_target_pairs={{0,9},{1,10},{2,11},{3,12},{4,13},{5,14},{6,15},{7,8},{8,17},{9,18... | collective-permute-start | bytes 12296 | tf_op jit(solution)/shard_map/ppermute | solution.py:368
  149.5 9.3 %collective-permute-start.13 = (f32[8,128]{1,0:T(8,128)}, f32[8,128]{1,0:T(8,128)S(1)}, u32[]{:S(2)}, u32[]{:S(2)}) collective-permute-start(f32[8,128]{1,0:T(8,128)} %get-tuple-element.60), channel_id=1, source_target_pairs={{0,15},{1,8},{2,9},{3,10},{4,11},{5,12},{6,13},{7,14},{8,23},{9,16... | collective-permute-start | bytes 12296 | tf_op jit(solution)/shard_map/ppermute | solution.py:368
  159.7 7.1 %collective-permute-done.14.refs_9_ = f32[8,128]{1,0:T(8,128)S(1)} collective-permute-done((f32[8,128]{1,0:T(8,128)}, f32[8,128]{1,0:T(8,128)S(1)}, u32[]{:S(2)}, u32[]{:S(2)}) %collective-permute-start.14) | collective-permute-done | bytes 4128 | tf_op jit(solution)/shard_map/ppermute | solution.py:368
  166.8 7.5 %collective-permute-done.15.refs_10_ = f32[8,128]{1,0:T(8,128)S(1)} collective-permute-done((f32[8,128]{1,0:T(8,128)}, f32[8,128]{1,0:T(8,128)S(1)}, u32[]{:S(2)}, u32[]{:S(2)}) %collective-permute-start.15) | collective-permute-done | bytes 4128 | tf_op jit(solution)/shard_map/ppermute | solution.py:368
  174.9 6.7 %sweep_last.1 = (f32[256,768]{1,0:T(8,128)}, f32[32,1024]{1,0:T(8,128)}) custom-call(s32[4]{0:T(128)} %pad_add_fusion.refs_0_, f32[32,1024]{1,0:T(8,128)} %get-tuple-element.50.phi_ref.refs_1_, f32[32,1024]{1,0:T(8,128)} %get-tuple-element.54.refs_2_, f32[8,1024]{1,0:T(8,128)} %copy-done.4, f32[8,1024]{1,0:T(8,128)} %copy-done.5, f32[64,128]{1,0:T(8,128)} %copy-done.7, ...), custom_call_target="tpu_custom_call" | custom-call | tf_op jit(solution)/shard_map/sweep_last/pallas_call | solution.py:473
  181.6 1.9 %reshape.53 = f32[32,32,32]{2,1,0:T(8,128)} reshape(f32[32,1024]{1,0:T(8,128)} %get-tuple-element.65) | data formatting | bytes 262144 | tf_op jit(solution)/shard_map/reshape | solution.py:490
  (70 shorter events, 17.0 us)
Async XLA Ops:
  2.8 16.8 %all-to-all-start = ((f32[128,1,128]{2,1,0:T(1,128)}), f32[128,1,128]{2,1,0:T(1,128)S(1)}, u32[]{:S(2)}, u32[]{:S(2)}) async-start(f32[128,1,128]{2,1,0:T(1,128)} %bitcast.23), calls=%async_computation | async-start | bytes 131072 | tf_op jit(solution)/shard_map/all_to_all | solution.py:353
  26.9 28.2 %all-to-all-start.1 = ((f32[128,16,128]{2,1,0:T(8,128)}), f32[128,16,128]{2,1,0:T(8,128)S(1)}, u32[]{:S(2)}, u32[]{:S(2)}) async-start(f32[128,16,128]{2,1,0:T(8,128)} %bitcast.19), calls=%async_computation.1 | async-start | bytes 2097152 | tf_op jit(solution)/shard_map/all_to_all | solution.py:353
  37.0 18.1 %copy-start = (s32[256,12]{1,0:T(8,128)}, s32[256,12]{1,0:T(8,128)S(1)}, u32[]{:S(2)}) copy-start(s32[256,12]{1,0:T(8,128)S(1)} %reshape.50.point_col_ref.refs_13_) | copy-start | bytes 36868
  67.7 8.7 %collective-permute-start.4 = (f32[8,128]{1,0:T(8,128)}, f32[8,128]{1,0:T(8,128)S(1)}, u32[]{:S(2)}, u32[]{:S(2)}) collective-permute-start(f32[8,128]{1,0:T(8,128)} %get-tuple-element.45), channel_id=1, source_target_pairs={{0,9},{1,10},{2,11},{3,12},{4,13},{5,14},{6,15},{7,8},{8,17},{9,18... | collective-permute-start | bytes 12296 | tf_op jit(solution)/shard_map/ppermute | solution.py:368
  68.8 7.6 %collective-permute-start.5 = (f32[8,128]{1,0:T(8,128)}, f32[8,128]{1,0:T(8,128)S(1)}, u32[]{:S(2)}, u32[]{:S(2)}) collective-permute-start(f32[8,128]{1,0:T(8,128)} %get-tuple-element.46), channel_id=1, source_target_pairs={{0,15},{1,8},{2,9},{3,10},{4,11},{5,12},{6,13},{7,14},{8,23},{9,16... | collective-permute-start | bytes 12296 | tf_op jit(solution)/shard_map/ppermute | solution.py:368
  69.0 9.0 %collective-permute-start.6 = (f32[8,128]{1,0:T(8,128)}, f32[8,128]{1,0:T(8,128)S(1)}, u32[]{:S(2)}, u32[]{:S(2)}) collective-permute-start(f32[8,128]{1,0:T(8,128)} %get-tuple-element.47), channel_id=1, source_target_pairs={{0,121},{1,122},{2,123},{3,124},{4,125},{5,126},{6,127},{7,120},{8... | collective-permute-start | bytes 12296 | tf_op jit(solution)/shard_map/ppermute | solution.py:368
  71.5 9.5 %collective-permute-start.7 = (f32[8,128]{1,0:T(8,128)}, f32[8,128]{1,0:T(8,128)S(1)}, u32[]{:S(2)}, u32[]{:S(2)}) collective-permute-start(f32[8,128]{1,0:T(8,128)} %get-tuple-element.48), channel_id=1, source_target_pairs={{0,127},{1,120},{2,121},{3,122},{4,123},{5,124},{6,125},{7,126},{8... | collective-permute-start | bytes 12296 | tf_op jit(solution)/shard_map/ppermute | solution.py:368
  72.4 8.5 %collective-permute-start = (f32[8,1024]{1,0:T(8,128)}, f32[8,1024]{1,0:T(8,128)S(1)}, u32[]{:S(2)}, u32[]{:S(2)}) collective-permute-start(f32[8,1024]{1,0:T(8,128)} %get-tuple-element.41), channel_id=1, source_target_pairs={{0,8},{8,16},{16,24},{24,32},{32,40},{40,48},{48,56},{56,64},{64,7... | collective-permute-start | bytes 98312 | tf_op jit(solution)/shard_map/ppermute | solution.py:360
  76.4 6.3 %copy-start.12 = (f32[8,128]{1,0:T(8,128)}, f32[8,128]{1,0:T(8,128)S(1)}, u32[]{:S(2)}) copy-start(f32[8,128]{1,0:T(8,128)S(1)} %collective-permute-done.4.refs_7_) | copy-start | bytes 12292
  76.4 6.3 %collective-permute-start.1 = (f32[8,1024]{1,0:T(8,128)}, f32[8,1024]{1,0:T(8,128)S(1)}, u32[]{:S(2)}, u32[]{:S(2)}) collective-permute-start(f32[8,1024]{1,0:T(8,128)} %get-tuple-element.42), channel_id=1, source_target_pairs={{0,120},{8,0},{16,8},{24,16},{32,24},{40,32},{48,40},{56,48},{64,5... | collective-permute-start | bytes 98312 | tf_op jit(solution)/shard_map/ppermute | solution.py:360
  76.4 6.3 %collective-permute-start.2 = (f32[64,128]{1,0:T(8,128)}, f32[64,128]{1,0:T(8,128)S(1)}, u32[]{:S(2)}, u32[]{:S(2)}) collective-permute-start(f32[64,128]{1,0:T(8,128)} %get-tuple-element.43), channel_id=1, source_target_pairs={{0,1},{1,2},{2,3},{3,4},{4,5},{5,6},{6,7},{7,0},{8,9},{9,10},{10,1... | collective-permute-start | bytes 98312 | tf_op jit(solution)/shard_map/ppermute | solution.py:362
  78.0 4.6 %collective-permute-start.3 = (f32[64,128]{1,0:T(8,128)}, f32[64,128]{1,0:T(8,128)S(1)}, u32[]{:S(2)}, u32[]{:S(2)}) collective-permute-start(f32[64,128]{1,0:T(8,128)} %get-tuple-element.44), channel_id=1, source_target_pairs={{0,7},{1,0},{2,1},{3,2},{4,3},{5,4},{6,5},{7,6},{8,15},{9,8},{10,9... | collective-permute-start | bytes 98312 | tf_op jit(solution)/shard_map/ppermute | solution.py:362
  98.4 26.5 %all-to-all-start.2 = ((f32[128,16,128]{2,1,0:T(8,128)}), f32[128,16,128]{2,1,0:T(8,128)S(1)}, u32[]{:S(2)}, u32[]{:S(2)}) async-start(f32[128,16,128]{2,1,0:T(8,128)} %bitcast.18), calls=%async_computation.2 | async-start | bytes 2097152 | tf_op jit(solution)/shard_map/all_to_all | solution.py:353
  137.4 36.8 %collective-permute-start.8 = (f32[8,1024]{1,0:T(8,128)}, f32[8,1024]{1,0:T(8,128)S(1)}, u32[]{:S(2)}, u32[]{:S(2)}) collective-permute-start(f32[8,1024]{1,0:T(8,128)} %get-tuple-element.55), channel_id=1, source_target_pairs={{0,8},{8,16},{16,24},{24,32},{32,40},{40,48},{48,56},{56,64},{64,7... | collective-permute-start | bytes 98312 | tf_op jit(solution)/shard_map/ppermute | solution.py:360
  140.6 33.7 %collective-permute-start.9 = (f32[8,1024]{1,0:T(8,128)}, f32[8,1024]{1,0:T(8,128)S(1)}, u32[]{:S(2)}, u32[]{:S(2)}) collective-permute-start(f32[8,1024]{1,0:T(8,128)} %get-tuple-element.56), channel_id=1, source_target_pairs={{0,120},{8,0},{16,8},{24,16},{32,24},{40,32},{48,40},{56,48},{64,5... | collective-permute-start | bytes 98312 | tf_op jit(solution)/shard_map/ppermute | solution.py:360
  140.6 33.7 %collective-permute-start.10 = (f32[64,128]{1,0:T(8,128)}, f32[64,128]{1,0:T(8,128)S(1)}, u32[]{:S(2)}, u32[]{:S(2)}) collective-permute-start(f32[64,128]{1,0:T(8,128)} %get-tuple-element.57), channel_id=1, source_target_pairs={{0,1},{1,2},{2,3},{3,4},{4,5},{5,6},{6,7},{7,0},{8,9},{9,10},{10,1... | collective-permute-start | bytes 98312 | tf_op jit(solution)/shard_map/ppermute | solution.py:362
  142.0 32.3 %collective-permute-start.11 = (f32[64,128]{1,0:T(8,128)}, f32[64,128]{1,0:T(8,128)S(1)}, u32[]{:S(2)}, u32[]{:S(2)}) collective-permute-start(f32[64,128]{1,0:T(8,128)} %get-tuple-element.58), channel_id=1, source_target_pairs={{0,7},{1,0},{2,1},{3,2},{4,3},{5,4},{6,5},{7,6},{8,15},{9,8},{10,9... | collective-permute-start | bytes 98312 | tf_op jit(solution)/shard_map/ppermute | solution.py:362
  142.2 7.3 %collective-permute-start.12 = (f32[8,128]{1,0:T(8,128)}, f32[8,128]{1,0:T(8,128)S(1)}, u32[]{:S(2)}, u32[]{:S(2)}) collective-permute-start(f32[8,128]{1,0:T(8,128)} %get-tuple-element.59), channel_id=1, source_target_pairs={{0,9},{1,10},{2,11},{3,12},{4,13},{5,14},{6,15},{7,8},{8,17},{9,18... | collective-permute-start | bytes 12296 | tf_op jit(solution)/shard_map/ppermute | solution.py:368
  149.5 24.9 %copy-start.16 = (f32[8,128]{1,0:T(8,128)}, f32[8,128]{1,0:T(8,128)S(1)}, u32[]{:S(2)}) copy-start(f32[8,128]{1,0:T(8,128)S(1)} %collective-permute-done.12.refs_7_) | copy-start | bytes 12292
  149.5 10.2 %collective-permute-start.13 = (f32[8,128]{1,0:T(8,128)}, f32[8,128]{1,0:T(8,128)S(1)}, u32[]{:S(2)}, u32[]{:S(2)}) collective-permute-start(f32[8,128]{1,0:T(8,128)} %get-tuple-element.60), channel_id=1, source_target_pairs={{0,15},{1,8},{2,9},{3,10},{4,11},{5,12},{6,13},{7,14},{8,23},{9,16... | collective-permute-start | bytes 12296 | tf_op jit(solution)/shard_map/ppermute | solution.py:368
  159.7 14.6 %copy-start.17 = (f32[8,128]{1,0:T(8,128)}, f32[8,128]{1,0:T(8,128)S(1)}, u32[]{:S(2)}) copy-start(f32[8,128]{1,0:T(8,128)S(1)} %collective-permute-done.13.refs_8_) | copy-start | bytes 12292
  159.7 7.1 %collective-permute-start.14 = (f32[8,128]{1,0:T(8,128)}, f32[8,128]{1,0:T(8,128)S(1)}, u32[]{:S(2)}, u32[]{:S(2)}) collective-permute-start(f32[8,128]{1,0:T(8,128)} %get-tuple-element.61), channel_id=1, source_target_pairs={{0,121},{1,122},{2,123},{3,124},{4,125},{5,126},{6,127},{7,120},{8... | collective-permute-start | bytes 12296 | tf_op jit(solution)/shard_map/ppermute | solution.py:368
  166.8 7.6 %copy-start.18 = (f32[8,128]{1,0:T(8,128)}, f32[8,128]{1,0:T(8,128)S(1)}, u32[]{:S(2)}) copy-start(f32[8,128]{1,0:T(8,128)S(1)} %collective-permute-done.14.refs_9_) | copy-start | bytes 12292
  166.8 7.5 %collective-permute-start.15 = (f32[8,128]{1,0:T(8,128)}, f32[8,128]{1,0:T(8,128)S(1)}, u32[]{:S(2)}, u32[]{:S(2)}) collective-permute-start(f32[8,128]{1,0:T(8,128)} %get-tuple-element.62), channel_id=1, source_target_pairs={{0,127},{1,120},{2,121},{3,122},{4,123},{5,124},{6,125},{7,126},{8... | collective-permute-start | bytes 12296 | tf_op jit(solution)/shard_map/ppermute | solution.py:368
  (15 other events, 22.0 us)
where the time goes:
time: 185 us; the launch traced here: 184 us
  Pallas kernels  85.4 us (46%)
  starting transfers between devices  63.7 us (34%)
  waiting for transfers between devices  22.4 us (12%)
  local copies, waits for them, and re-layouts  10.6 us (6%)
    all_to_all x3, starting transfers between devices, exchange(): return lax.all_to_all(x, AXES, split_axis=0, concat_axis=0, tiled=True)  30.7 us
    pallas_call x2, Pallas kernels, on_device(): pl.pallas_call(base_kernel, grid=(templates.shape[0],), out_shape=shaped(...  23.8 us
    pallas_call x2, Pallas kernels, on_device(): pl.pallas_call(gap_kernel, out_shape=(shaped(CELLS, NODES), shaped(TILE,...  23 us
    ppermute x8, starting transfers between devices, send(): return lax.ppermute(x, AXES, moves)  20.3 us
    ppermute x8, waiting for transfers between devices, send(): return lax.ppermute(x, AXES, moves)  16.5 us
    pallas_call x1, Pallas kernels, on_device(): pl.pallas_call(functools.partial(sweep_kernel, False), out_shape=outs + (...  15.1 us
    ppermute x4, starting transfers between devices, send(): lax.ppermute(x, 'tx', [(i, (i + by_x) % size_x) for i in range(size_x)])  7.13 us
    pallas_call x1, Pallas kernels, on_device(): pl.pallas_call(second_gather_kernel, out_shape=(shaped(DEVS * 16, 128), s...  6.74 us
  transfers between devices with their start and end apart: 19, of which 7 were waited for; matrix products, arithmetic and copies ran while one was open for 3% of the time, Pallas kernels for 17%

commit v1 on v0

v1 whole, which is shorter than its diff:
```python
import functools

import jax
import jax.numpy as jnp
from jax import lax
from jax.experimental import pallas as pl
from jax.experimental.pallas import tpu as pltpu
from jax.sharding import PartitionSpec as P

BLOCK = 64
SWEEPS = 4
STEPS = 2
CELLS = 256
NODES = 768
PER = 12
DEVS = 128
CAP = 16
TILE = 32
HALO = 4
TILES = 8
F32 = jnp.float32
BF16 = jnp.bfloat16
I32 = jnp.int32
AXES = ("tx", "ty")
VMEM = pl.BlockSpec(memory_space=pltpu.VMEM)
SMEM = pl.BlockSpec(memory_space=pltpu.SMEM)
NT = (((1,), (1,)), ((), ()))
TN = (((0,), (0,)), ((), ()))


def iota(shape, dim):
    return lax.broadcasted_iota(I32, shape, dim)


def low_half(rows):
    return iota((rows, 128), 1) < 64


def flag(condition):
    return condition.astype(F32).astype(BF16)


def regroup(number):
    value = number.astype(F32)
    cell = jnp.floor((value + 0.5) * (1.0 / PER))
    return (value - PER * cell) * CELLS + cell


def split2(x):
    hi = x.astype(BF16).astype(F32)
    return hi, x - hi


def setup_kernel(dev_ref, src_ref, dst_ref, conduct_ref, table_ref):
    device = iota((128, 128), 0)
    before = flag(device < iota((128, 128), 1))
    slots = iota((16, 128), 0)
    count = jnp.zeros((128, 1), F32)
    table = jnp.zeros((128, 128), F32)
    for q in range(8):
        hit = (dev_ref[q : q + 1, :] == device).astype(F32)
        hit_bf = hit.astype(BF16)
        running = jnp.dot(hit_bf, before, preferred_element_type=F32) + count
        rank = jnp.sum(hit * running, axis=0, keepdims=True)
        count = count + jnp.sum(hit, axis=1, keepdims=True)
        here = rank.astype(I32) == slots
        parts = []
        for ref in (dst_ref, src_ref):
            number = regroup(ref[q : q + 1, :])
            hi = jnp.floor(number * (1.0 / 64.0))
            parts += [hi, number - 64.0 * hi]
        first, rest = split2(conduct_ref[q : q + 1, :])
        second, third = split2(rest)
        parts += [first, second, third, jnp.zeros((1, 128), F32)]
        values = jnp.concatenate([jnp.where(here, part, 0.0) for part in parts], axis=0)
        table = table + lax.dot_general(hit_bf, values.astype(BF16), NT, preferred_element_type=F32)
    table_ref[...] = table


def decode(table, first_lane, scratch):
    scratch[...] = table
    lane = iota((16, 128), 1)
    out = jnp.zeros((16, 128), F32)
    for dl in range(8):
        rows = scratch[pl.ds(dl, 16, stride=8), :]
        out = jnp.where((lane >> 4) == dl, pltpu.roll(rows, (16 * dl - first_lane) % 128, 1), out)
    return out


def doubled(volt, rows_ref):
    low = low_half(CELLS)
    for j in range(PER // 2):
        pair = volt[:, 128 * j : 128 * j + 128]
        turned = pltpu.roll(pair, 64, 1)
        rows_ref[512 * j : 512 * j + 256, :] = jnp.where(low, pair, turned)
        rows_ref[512 * j + 256 : 512 * j + 512, :] = jnp.where(low, turned, pair)


def gather_rows(rows_ref, index_ref, scale_ref, out_ref, offset, stride):
    low = low_half(1)

    def body(r, carry):
        scale_base = pl.multiple_of(r * 64, 64)
        out_base = pl.multiple_of(r * (8 * stride), 8 * stride)
        for m in range(64):
            a = index_ref[r, 2 * m]
            b = index_ref[r, 2 * m + 1]
            row = jnp.where(low, rows_ref[pl.ds(a, 1), :], rows_ref[pl.ds(b, 1), :])
            place = (m // 8) * stride + offset + m % 8
            out_ref[pl.ds(out_base + place, 1), :] = row * scale_ref[pl.ds(scale_base + m, 1), :]
        return carry

    lax.fori_loop(0, DEVS // 8, body, 0)


def gather_kernel(incoming, *refs):
    if incoming:
        table_ref, volt_ref, sent_ref, out_ref = refs[:4]
    else:
        table_ref, volt_ref, out_ref = refs[:3]
    index_ref, conduct_ref, scale_ref, rows_ref, scratch, index_sm, sem = refs[-7:]
    table = table_ref[...]
    numbers = 64.0 * table + pltpu.roll(table, 112, 1)
    index_ref[...] = decode(numbers, 0 if incoming else 32, scratch).astype(I32)
    copy = pltpu.make_async_copy(index_ref, index_sm, sem)
    copy.start()
    conducts = table + pltpu.roll(table, 112, 1) + pltpu.roll(table, 96, 1)
    conduct_ref[...] = decode(conducts, 64, scratch)
    part = iota((128, 1024), 0)
    lane = iota((128, 1024), 1)
    spread = flag((part >= 64) & (part < 112) & ((part & 15) == (lane >> 6)))
    scale = jnp.dot(table.astype(BF16), spread, preferred_element_type=F32)
    for p in range(8):
        scale_ref[pl.ds(p, DEVS, stride=8), :] = scale[:, 128 * p : 128 * p + 128]
    doubled(volt_ref[...], rows_ref)
    if incoming:
        for d in range(DEVS):
            out_ref[16 * d : 16 * d + 8, :] = sent_ref[8 * d : 8 * d + 8, :]
    copy.wait()
    if incoming:
        gather_rows(rows_ref, index_sm, scale_ref, out_ref, 8, 16)
    else:
        gather_rows(rows_ref, index_sm, scale_ref, out_ref, 0, 8)


def expander(rows, j):
    return (iota((rows, 128), 0) & 15) == 2 * j + (iota((rows, 128), 1) >> 6)


def prepare_kernel(into_ref, into_conduct_ref, own_ref, own_conduct_ref, id_ref, ecs_ref, degree_ref, id_out, phi_out):
    cell = iota((CELLS, 128), 0)
    kind = iota((16, 128), 0)
    total = jnp.zeros((48, CELLS), F32)
    for index_ref, conduct_ref in ((into_ref, into_conduct_ref), (own_ref, own_conduct_ref)):
        for s in range(CAP):
            number = index_ref[s : s + 1, :]
            hit = flag((number & 255) == cell)
            here = (number >> 8) == kind
            first, rest = split2(conduct_ref[s : s + 1, :])
            second, third = split2(rest)
            values = jnp.concatenate([jnp.where(here, x, 0.0) for x in (first, second, third)], axis=0)
            total = total + lax.dot_general(values.astype(BF16), hit, NT, preferred_element_type=F32)
    total = total[0:16, :] + total[16:32, :] + total[32:48, :]
    first, rest = split2(total)
    second, third = split2(rest)
    pieces = jnp.concatenate([first, second, third], axis=0).astype(BF16)
    for j in range(PER // 2):
        degree_ref[:, 128 * j : 128 * j + 128] = lax.dot_general(
            pieces, flag(expander(48, j)), TN, preferred_element_type=F32
        )
    number = iota((16, 128), 0).astype(F32).astype(BF16)
    for half in range(2):
        hit = flag(id_ref[half : half + 1, :] == kind)
        id_out[128 * half : 128 * half + 128, :] = lax.dot_general(hit, number, TN, preferred_element_type=F32)
    for t in range(TILES):
        for y in range(4):
            rows = ecs_ref[pl.ds(4 * t + y, TILE, stride=TILE), :]
            phi_out[TILE * t : TILE * t + TILE, 32 * y : 32 * y + 32] = rows


def base_kernel(volt_ref, recov_ref, id_ref, degree_ref, template_ref, out_ref, volt_bf):
    index = pl.program_id(0)

    @pl.when(index == 0)
    def _():
        volt_bf[...] = volt_ref[...].astype(BF16)
        out_ref[...] = jnp.zeros_like(out_ref)

    mine = id_ref[...] == index.astype(F32)
    masked = jnp.concatenate(
        [
            jnp.where(mine, volt_bf[:, 128 * j : 128 * j + 128], jnp.zeros((), BF16))
            for j in range(PER // 2)
        ],
        axis=1,
    )
    out_ref[...] += jnp.dot(masked, template_ref[0], preferred_element_type=F32)

    @pl.when(index == pl.num_programs(0) - 1)
    def _():
        volt = volt_ref[...]
        ion = volt - volt * volt * volt * (1.0 / 3.0) - recov_ref[...]
        out_ref[...] += degree_ref[...] * volt - ion


def grid_row(point):
    return ((point >> 7) & 7) * TILE + (point >> 10)


def gap_kernel(
    into_ref,
    own_ref,
    got_ref,
    base_ref,
    point_ref,
    phi_ref,
    current_ref,
    deposit_ref,
    x_low_ref,
    x_high_ref,
    y_low_ref,
    y_high_ref,
    even_in,
    odd_in,
    even_out,
    odd_out,
):
    for ref in (even_in, odd_in, even_out, odd_out):
        ref[...] = jnp.zeros_like(ref)

    def body(r, carry):
        base = pl.multiple_of(r * 128, 128)
        for m in range(64):
            at = (m // 8) * 16 + m % 8
            row = got_ref[pl.ds(base + at, 1), :]
            back = got_ref[pl.ds(base + (at + 8), 1), :]
            even_in[pl.ds(into_ref[r, 2 * m], 1), :] += row
            odd_in[pl.ds(into_ref[r, 2 * m + 1], 1), :] += row
            even_out[pl.ds(own_ref[r, 2 * m], 1), :] += back
            odd_out[pl.ds(own_ref[r, 2 * m + 1], 1), :] += back
        return carry

    lax.fori_loop(0, DEVS // 8, body, 0)

    low = low_half(CELLS)
    means = jnp.zeros((16, CELLS), F32)
    for j in range(PER // 2):
        sums = []
        for k in (2 * j, 2 * j + 1):
            cut = slice(CELLS * k, CELLS * k + CELLS)
            even = even_in[cut, :] + even_out[cut, :]
            odd = odd_in[cut, :] + odd_out[cut, :]
            both = jnp.where(low, even, odd)
            sums.append(both + pltpu.roll(both, 64, 1))
        cut = slice(128 * j, 128 * j + 128)
        current = base_ref[:, cut] - jnp.where(low, sums[0], sums[1])
        current_ref[:, cut] = current
        weights = jnp.where(expander(16, j), 1.0 / BLOCK, 0.0).astype(BF16)
        for part in split2(current):
            means = means + lax.dot_general(weights, part.astype(BF16), NT, preferred_element_type=F32)
    mean_hi, mean_lo = split2(means)
    row_of = iota((CELLS, CELLS), 0)
    column_of = iota((128, CELLS), 0)
    total = jnp.zeros((CELLS, 256), F32)
    for k in range(PER):
        point = point_ref[k : k + 1, :]
        hit = flag(grid_row(point) == row_of)
        here = (point & 127) == column_of
        spread = [jnp.where(here, x[k : k + 1, :], 0.0) for x in (mean_hi, mean_lo)]
        spread = jnp.concatenate(spread, axis=0).astype(BF16)
        total = total + lax.dot_general(hit, spread, NT, preferred_element_type=F32)
    deposit_ref[...] = total[:, 0:128] + total[:, 128:256]
    for array, at, across in ((phi_ref, 0, 0), (deposit_ref, HALO, TILE)):
        for t in range(TILES):
            start = TILE * t
            x_low_ref[8 * t + at : 8 * t + at + HALO, :] = array[start : start + HALO, :]
            x_high_ref[8 * t + at : 8 * t + at + HALO, :] = array[start + TILE - HALO : start + TILE, :]
        y_low_ref[across : across + TILE, :] = array[0:TILE, :]
        y_high_ref[across : across + TILE, :] = array[TILE * (TILES - 1) :, :]


ROWS = TILE + 2 * HALO
LEAD = 8


def sweep_kernel(last, *refs):
    place_ref, phi_ref, deposit_ref, x_before_ref, x_after_ref, y_before_ref, y_after_ref = refs[:7]
    current_ref, volt_ref, point_ref = refs[7:10]
    if last:
        volt_out, phi_out, wide_phi, wide_deposit, found_ref = refs[10:]
    else:
        recov_ref, into_ref, into_scale_ref, own_ref, own_scale_ref = refs[10:15]
        volt_out, phi_out, recov_out, send_out, wide_phi, wide_deposit, found_ref, rows_ref = refs[15:]
    end = LEAD + ROWS
    high = LEAD + HALO + TILE
    for wide, array, at, across in ((wide_phi, phi_ref, 0, 0), (wide_deposit, deposit_ref, HALO, TILE)):
        for t in range(TILES):
            wide[t + 1, LEAD : LEAD + HALO, :] = x_before_ref[8 * t + at : 8 * t + at + HALO, :]
            wide[t + 1, LEAD + HALO : high, :] = array[TILE * t : TILE * t + TILE, :]
            wide[t + 1, high:end, :] = x_after_ref[8 * t + at : 8 * t + at + HALO, :]
        for t, came in ((0, y_before_ref), (TILES + 1, y_after_ref)):
            wide[t, LEAD : LEAD + HALO, :] = came[at : at + HALO, :]
            wide[t, LEAD + HALO : high, :] = came[8 + across : 8 + across + TILE, :]
            wide[t, high:end, :] = came[72 + at : 72 + at + HALO, :]
    shape = (ROWS, 128)
    row = iota(shape, 0)
    lane = iota(shape, 1)
    depth = lane & (TILE - 1)
    first_row = jnp.where(place_ref[0] == 0, HALO, 0)
    last_row = jnp.where(place_ref[0] == place_ref[2] - 1, HALO + TILE, ROWS)
    inside = (row >= first_row) & (row < last_row)
    first_tile = jnp.where(place_ref[1] == 0, 1, 0)
    last_tile = jnp.where(place_ref[1] == place_ref[3] - 1, TILES + 1, TILES + 2)
    scale = jnp.where(inside, 1.0 / 6.5, 0.0)
    side = [jnp.where((t >= first_tile) & (t < last_tile), 1.0, 0.0) for t in (0, TILES + 1)]
    edge = {0: scale * side[0], TILES + 1: scale * side[1]}
    for t in range(TILES + 2):
        wide_phi[t, 0:LEAD, :] = jnp.zeros((LEAD, 128), F32)
        wide_phi[t, end : end + 8, :] = jnp.zeros((8, 128), F32)
        keep = jnp.where(inside, side[0 if t == 0 else 1], 0.0) if t in edge else jnp.where(inside, 1.0, 0.0)
        wide_phi[t, LEAD:end, :] = jnp.where(keep > 0.0, wide_phi[t, LEAD:end, :], 0.0)
    nothing = jnp.zeros(shape, F32)
    for sweep in range(SWEEPS):
        middle = [wide_phi[t, LEAD:end, :] for t in range(TILES + 2)]
        fresh = []
        ups = [pltpu.roll(x, 32, 1) for x in middle]
        downs = [pltpu.roll(x, 96, 1) for x in middle]
        for t in range(TILES + 2):
            total = wide_deposit[t, LEAD:end, :]
            total = total + wide_phi[t, LEAD - 1 : end - 1, :] + wide_phi[t, LEAD + 1 : end + 1, :]
            total = total + jnp.where(lane < 32, ups[t - 1] if t else nothing, ups[t])
            total = total + jnp.where(lane >= 96, downs[t + 1] if t <= TILES else nothing, downs[t])
            total = total + jnp.where(depth == 0, 0.0, pltpu.roll(middle[t], 1, 1))
            total = total + jnp.where(depth == TILE - 1, 0.0, pltpu.roll(middle[t], 127, 1))
            fresh.append(jnp.where(edge.get(t, scale) > 0.0, total * (1.0 / 6.5), 0.0))
        for t in range(TILES + 2):
            wide_phi[t, LEAD:end, :] = fresh[t]
    tiles = [wide_phi[t + 1, LEAD + HALO : high, :] for t in range(TILES)]
    if last:
        for t in range(TILES):
            for y in range(4):
                turned = tiles[t] if y == 0 else pltpu.roll(tiles[t], 128 - 32 * y, 1)
                phi_out[pl.ds(4 * t + y, TILE, stride=TILE), :] = turned[:, 0:TILE]
    else:
        for t in range(TILES):
            phi_out[TILE * t : TILE * t + TILE, :] = tiles[t]
    turned = jnp.concatenate(tiles, axis=0).T
    pieces = jnp.concatenate(split2(turned), axis=0).astype(BF16)
    row_of = iota((CELLS, CELLS), 0)
    column_of = iota((128, CELLS), 0)
    found_ref[...] = jnp.zeros_like(found_ref)
    for k in range(PER):
        point = point_ref[k : k + 1, :]
        hit = flag(grid_row(point) == row_of)
        found = jnp.dot(pieces, hit, preferred_element_type=F32)
        found = found[0:128, :] + found[128:256, :]
        here = (point & 127) == column_of
        found_ref[k : k + 1, :] = jnp.sum(jnp.where(here, found, 0.0), axis=0, keepdims=True)
    found = jnp.concatenate(split2(found_ref[...]), axis=0).astype(BF16)
    low = low_half(CELLS)
    for j in range(PER // 2):
        cut = slice(128 * j, 128 * j + 128)
        at_node = lax.dot_general(found, flag(expander(32, j)), TN, preferred_element_type=F32)
        volt = volt_ref[:, cut]
        fresh = volt - 0.05 * (current_ref[:, cut] + at_node)
        volt_out[:, cut] = fresh
        if not last:
            recov = recov_ref[:, cut]
            recov_out[:, cut] = recov + 0.05 * 0.08 * (volt + 0.7 - 0.8 * recov)
            turned = pltpu.roll(fresh, 64, 1)
            rows_ref[512 * j : 512 * j + 256, :] = jnp.where(low, fresh, turned)
            rows_ref[512 * j + 256 : 512 * j + 512, :] = jnp.where(low, turned, fresh)
    if not last:
        gather_rows(rows_ref, own_ref, own_scale_ref, send_out, 0, 16)
        gather_rows(rows_ref, into_ref, into_scale_ref, send_out, 8, 16)


def shaped(*shape, dtype=F32):
    return jax.ShapeDtypeStruct(shape, dtype)


def exchange(x):
    return lax.all_to_all(x, AXES, split_axis=0, concat_axis=0, tiled=True)


def shift(x, axis, by):
    size = lax.axis_size(axis)
    return lax.ppermute(x, axis, [(i, (i + by) % size) for i in range(size)])


def on_device(
    potential,
    gating,
    ecs_start,
    templates,
    template_id,
    patch_src,
    patch_dev,
    patch_dst,
    patch_conduct,
    memb_point,
):
    flat = (8, 128)
    table = pl.pallas_call(
        setup_kernel,
        out_shape=shaped(128, 128),
        in_specs=[VMEM] * 4,
        out_specs=VMEM,
        name="setup",
    )(
        patch_dev.reshape(flat),
        patch_src.reshape(flat),
        patch_dst.reshape(flat),
        patch_conduct.reshape(flat),
    )
    got_table = exchange(table)
    rows_scratch = pltpu.VMEM((PER * CELLS, 128), F32)
    tables_out = (shaped(16, 128, dtype=I32), shaped(16, 128), shaped(DEVS * 8, 128))
    gather_scratch = [
        rows_scratch,
        pltpu.VMEM((128, 128), F32),
        pltpu.SMEM((16, 128), I32),
        pltpu.SemaphoreType.DMA,
    ]
    sent, own, own_conduct, own_scale = pl.pallas_call(
        functools.partial(gather_kernel, False),
        out_shape=(shaped(DEVS * 8, 128),) + tables_out,
        in_specs=[VMEM] * 2,
        out_specs=(VMEM,) * 4,
        scratch_shapes=gather_scratch,
        name="gather_source",
    )(table, potential)
    outgoing, into, into_conduct, into_scale = pl.pallas_call(
        functools.partial(gather_kernel, True),
        out_shape=(shaped(DEVS * 16, 128),) + tables_out,
        in_specs=[VMEM] * 3,
        out_specs=(VMEM,) * 4,
        scratch_shapes=gather_scratch,
        name="gather_target",
    )(got_table, potential, sent)
    degree, id_wide, phi = pl.pallas_call(
        prepare_kernel,
        out_shape=(shaped(CELLS, NODES), shaped(CELLS, 128), shaped(TILE * TILES, 128)),
        in_specs=[VMEM] * 6,
        out_specs=(VMEM,) * 3,
        name="prepare",
    )(into, into_conduct, own, own_conduct, template_id.reshape(2, 128), ecs_start.reshape(TILE * TILE, TILE))

    place = jnp.stack([lax.axis_index("tx"), lax.axis_index("ty"), lax.axis_size("tx"), lax.axis_size("ty")])
    place = place.astype(I32)
    points = memb_point.reshape(CELLS, PER).T
    volt = potential
    recov = gating
    whole = lambda *shape: pl.BlockSpec(shape, lambda i: (0,) * len(shape))
    for step in range(STEPS):
        last = step == STEPS - 1
        got = exchange(outgoing.reshape(DEVS, 16, 128)).reshape(DEVS * 16, 128)
        base = pl.pallas_call(
            base_kernel,
            grid=(templates.shape[0],),
            out_shape=shaped(CELLS, NODES),
            in_specs=[
                whole(CELLS, NODES),
                whole(CELLS, NODES),
                whole(CELLS, 128),
                whole(CELLS, NODES),
                pl.BlockSpec((1, NODES, NODES), lambda i: (i, 0, 0)),
            ],
            out_specs=whole(CELLS, NODES),
            scratch_shapes=[pltpu.VMEM((CELLS, NODES), BF16)],
            cost_estimate=pl.CostEstimate(flops=3_000_000_000, bytes_accessed=14_000_000, transcendentals=0),
            name="base",
        )(volt, recov, id_wide, degree, templates)
        accumulator = pltpu.VMEM((PER * CELLS, 128), F32)
        current, deposit, x_low, x_high, y_low, y_high = pl.pallas_call(
            gap_kernel,
            out_shape=(shaped(CELLS, NODES), shaped(TILE * TILES, 128)) + (shaped(64, 128),) * 4,
            in_specs=[SMEM] * 2 + [VMEM] * 4,
            out_specs=(VMEM,) * 6,
            scratch_shapes=[accumulator] * 4,
            name="gap",
        )(into, own, got, base, points, phi)
        x_before = shift(x_high, "tx", 1)
        x_after = shift(x_low, "tx", -1)
        y_low = jnp.concatenate([x_before[0:8], y_low, x_after[0:8]])
        y_high = jnp.concatenate([x_before[56:64], y_high, x_after[56:64]])
        y_before = shift(y_high, "ty", 1)
        y_after = shift(y_low, "ty", -1)
        operands = [place, phi, deposit, x_before, x_after, y_before, y_after, current, volt, points]
        specs = [SMEM] + [VMEM] * 9
        wide = [pltpu.VMEM((TILES + 2, LEAD + ROWS + 8, 128), F32)] * 2 + [pltpu.VMEM((16, CELLS), F32)]
        if last:
            volt, phi = pl.pallas_call(
                functools.partial(sweep_kernel, True),
                out_shape=(shaped(CELLS, NODES), shaped(TILE * TILE, TILE)),
                in_specs=specs,
                out_specs=(VMEM,) * 2,
                scratch_shapes=wide,
                name="sweep_last",
            )(*operands)
        else:
            volt, phi, recov, outgoing = pl.pallas_call(
                functools.partial(sweep_kernel, False),
                out_shape=(
                    shaped(CELLS, NODES),
                    shaped(TILE * TILES, 128),
                    shaped(CELLS, NODES),
                    shaped(DEVS * 16, 128),
                ),
                in_specs=specs + [VMEM, SMEM, VMEM, SMEM, VMEM],
                out_specs=(VMEM,) * 4,
                scratch_shapes=wide + [rows_scratch],
                name="sweep",
            )(*operands, recov, into, into_scale, own, own_scale)
    return (volt, phi.reshape(TILE, TILE, TILE))


def solution(mesh):
    return jax.shard_map(
        on_device,
        mesh=mesh,
        in_specs=(
            P(("tx", "ty"), None),
            P(("tx", "ty"), None),
            P("tx", "ty", None),
            P(),
            P(("tx", "ty")),
            P(("tx", "ty")),
            P(("tx", "ty"), None),
            P(("tx", "ty")),
            P(("tx", "ty")),
            P(("tx", "ty")),
        ),
        out_specs=(P(("tx", "ty"), None), P("tx", "ty", None)),
        check_vma=False,
    )
```

time: 185 us -> 149 us (0.81)
  starting transfers between devices: 63.7 us -> 38.6 us
  Pallas kernels: 85.4 us -> 73.9 us
  local copies, waits for them, and re-layouts: 10.6 us -> 5.35 us
  other arithmetic: 0.58 us -> 3.65 us
  waiting for transfers between devices: 22.4 us -> 24.3 us
    ppermute x16 -> x8, starting transfers between devices: 33 us -> 10.6 us  [shift(): return lax.ppermute(x, axis, [(i, (i + by) % size) for i in range(size)])]
    pallas_call x8, Pallas kernels: 61.6 us -> 50.7 us  [the longest x2 21 us: on_device(): pl.pallas_call(gap_kernel, out_shape=(shaped(CELLS, NODES), shaped(TILE *...]
    reshape x5 -> x2, local copies, waits for them, and re-layouts: 6.78 us -> 1.52 us  [on_device(): points = memb_point.reshape(CELLS, PER).T]
    concatenate x0 -> x4, other arithmetic: none -> 3.07 us  [the longest x2 1.55 us: on_device(): y_high = jnp.concatenate([x_before[56:64], y_high, x_after[56:64]])]
    all_to_all x3, starting transfers between devices: 30.7 us -> 27.9 us  [exchange(): return lax.all_to_all(x, AXES, split_axis=0, concat_axis=0, tiled=True)]
    ppermute x16 -> x8, waiting for transfers between devices: 18.2 us -> 18.8 us  [shift(): return lax.ppermute(x, axis, [(i, (i + by) % size) for i in range(size)])]
    unnamed x40 -> x22, local copies, waits for them, and re-layouts: 3.81 us -> 3.82 us
  transfers between devices with their start and end apart: 19 -> 11, of which waited for: 7 -> 9; matrix products, arithmetic and copies ran while one was open for 3% -> 2% of each run, Pallas kernels for 17% -> 21%
where the time goes in v1:
time: 149 us; the launch traced here: 146 us
  Pallas kernels  73.9 us (50%)
  starting transfers between devices  38.6 us (26%)
  waiting for transfers between devices  24.3 us (16%)
  local copies, waits for them, and re-layouts  5.35 us (4%)
  other arithmetic  3.65 us (2%)
    all_to_all x3, starting transfers between devices, exchange(): return lax.all_to_all(x, AXES, split_axis=0, concat_axis=0, tiled=True)  27.9 us
    pallas_call x2, Pallas kernels, on_device(): pl.pallas_call(base_kernel, grid=(templates.shape[0],), out_shape=shaped(...  23.2 us
    pallas_call x2, Pallas kernels, on_device(): pl.pallas_call(gap_kernel, out_shape=(shaped(CELLS, NODES), shaped(TILE *...  21 us
    ppermute x8, waiting for transfers between devices, shift(): return lax.ppermute(x, axis, [(i, (i + by) % size) for i in range(size)])  18.8 us
    ppermute x8, starting transfers between devices, shift(): return lax.ppermute(x, axis, [(i, (i + by) % size) for i in range(size)])  10.6 us
    pallas_call x1, Pallas kernels, on_device(): pl.pallas_call(functools.partial(sweep_kernel, False), out_shape=(shaped(...  9.44 us
    all_to_all x3, waiting for transfers between devices, exchange(): return lax.all_to_all(x, AXES, split_axis=0, concat_axis=0, tiled=True)  5.45 us
    pallas_call x1, Pallas kernels, on_device(): pl.pallas_call(functools.partial(gather_kernel, True), out_shape=(shaped(...  5.12 us
  transfers between devices with their start and end apart: 11, of which 9 were waited for; matrix products, arithmetic and copies ran while one was open for 2% of the time, Pallas kernels for 21%

profile of v1, /device:TPU:31, one launch (start us, length us, event | category | flops | bytes accessed | tf_op | source)
XLA Modules:
  0.0 146.5 jit_solution(2124637660057383150)
XLA Ops:
  0.6 2.1 %setup.1.refs_0_ = f32[128,128]{1,0:T(8,128)} custom-call(s32[8,128]{1,0:T(8,128)} %bitcast.29, s32[8,128]{1,0:T(8,128)} %bitcast.30, s32[8,128]{1,0:T(8,128)} %bitcast.31, f32[8,128]{1,0:T(8,128)} %bitcast.32), custom_call_target="tpu_custom_call" | custom-call | tf_op jit(solution)/shard_map/setup/pallas_call | solution.py:404
  2.7 10.5 %all-to-all-start = ((f32[128,1,128]{2,1,0:T(1,128)}), f32[128,1,128]{2,1,0:T(1,128)S(1)}, u32[]{:S(2)}, u32[]{:S(2)}) async-start(f32[128,1,128]{2,1,0:T(1,128)} %bitcast.22), calls=%async_computation | async-start | bytes 131072 | tf_op jit(solution)/shard_map/all_to_all | solution.py:383
  13.3 4.7 %gather_source.1 = (f32[1024,128]{1,0:T(8,128)}, s32[16,128]{1,0:T(8,128)}, f32[16,128]{1,0:T(8,128)}, f32[1024,128]{1,0:T(8,128)}) custom-call(f32[128,128]{1,0:T(8,128)} %setup.1.refs_0_, f32[256,768]{1,0:T(8,128)} %refs_8_.1), custom_call_target="tpu_custom_call" | custom-call | tf_op jit(solution)/shard_map/gather_source/pallas_call | solution.py:425
  18.0 1.5 %all-to-all-done = f32[128,1,128]{2,1,0:T(1,128)S(1)} async-done(((f32[128,1,128]{2,1,0:T(1,128)}), f32[128,1,128]{2,1,0:T(1,128)S(1)}, u32[]{:S(2)}, u32[]{:S(2)}) %all-to-all-start) | async-done | bytes 65568 | tf_op jit(solution)/shard_map/all_to_all | solution.py:383
  20.1 5.1 %gather_target.1 = (f32[2048,128]{1,0:T(8,128)}, s32[16,128]{1,0:T(8,128)}, f32[16,128]{1,0:T(8,128)}, f32[1024,128]{1,0:T(8,128)}) custom-call(f32[128,128]{1,0:T(8,128)} %bitcast.28, f32[256,768]{1,0:T(8,128)} %refs_8_.1, f32[1024,128]{1,0:T(8,128)} %get-tuple-element.31.refs_2_), custom_call_target="tpu_custom_call" | custom-call | tf_op jit(solution)/shard_map/gather_target/pallas_call | solution.py:433
  25.3 8.3 %all-to-all-start.1 = ((f32[128,16,128]{2,1,0:T(8,128)}), f32[128,16,128]{2,1,0:T(8,128)S(1)}, u32[]{:S(2)}, u32[]{:S(2)}) async-start(f32[128,16,128]{2,1,0:T(8,128)} %bitcast.21), calls=%async_computation.1 | async-start | bytes 2097152 | tf_op jit(solution)/shard_map/all_to_all | solution.py:383
  35.1 3.4 %prepare.1 = (f32[256,768]{1,0:T(8,128)}, f32[256,128]{1,0:T(8,128)}, f32[256,128]{1,0:T(8,128)}) custom-call(s32[16,128]{1,0:T(8,128)} %get-tuple-element.32.into_ref.refs_11_, f32[16,128]{1,0:T(8,128)} %get-tuple-element.33.into_conduct_ref, s32[16,128]{1,0:T(8,128)} %get-tuple-element.34.own_ref.refs_13_, f32[16,128]{1,0:T(8,128)} %get-tuple-element.35.own_conduct_ref, ...), custom_call_target="tpu_custom_call" | custom-call | tf_op jit(solution)/shard_map/prepare/pallas_call | solution.py:441
  38.5 11.6 %base.2.base_ref = f32[256,768]{1,0:T(8,128)} custom-call(f32[256,768]{1,0:T(8,128)} %refs_8_.1, f32[256,768]{1,0:T(8,128)} %refs_10_.1, f32[256,128]{1,0:T(8,128)} %get-tuple-element.38.id_ref, f32[256,768]{1,0:T(8,128)} %get-tuple-element.39.degree_ref, bf16[10,768,768]{2,1,0:T(8,128)(2,1)} %template_ref.3), custom_call_target="tpu_custom_call" | custom-call | flops 3000000000 | bytes 14000000 | tf_op jit(solution)/shard_map/base/pallas_call | solution.py:458
  51.1 10.5 %gap.2 = (f32[256,768]{1,0:T(8,128)}, f32[256,128]{1,0:T(8,128)}, f32[64,128]{1,0:T(8,128)}, f32[64,128]{1,0:T(8,128)}, f32[64,128]{1,0:T(8,128)}, /*index=5*/f32[64,128]{1,0:T(8,128)}) custom-call(s32[16,128]{1,0:T(8,128)} %get-tuple-element.32.into_ref.refs_11_, s32[16,128]{1,0:T(8,128)} %get-tuple-element.34.own_ref.refs_13_, f32[2048,128]{1,0:T(8,128)} %bitcast.18, ...), custom_call_target="tpu_custom_call" | custom-call | tf_op jit(solution)/shard_map/gap/pallas_call | solution.py:475
  61.6 1.7 %collective-permute-start = (f32[64,128]{1,0:T(8,128)}, f32[64,128]{1,0:T(8,128)S(1)}, u32[]{:S(2)}, u32[]{:S(2)}) collective-permute-start(f32[64,128]{1,0:T(8,128)} %get-tuple-element.41), channel_id=1, source_target_pairs={{0,8},{8,16},{16,24},{24,32},{32,40},{40,48},{48,56},{56,64},{64,7... | collective-permute-start | bytes 98312 | tf_op jit(solution)/shard_map/ppermute | solution.py:388
  63.2 1.3 collective-permute-done.refs_3_
  64.6 5.0 %collective-permute-done.1.refs_4_ = f32[64,128]{1,0:T(8,128)S(1)} collective-permute-done((f32[64,128]{1,0:T(8,128)}, f32[64,128]{1,0:T(8,128)S(1)}, u32[]{:S(2)}, u32[]{:S(2)}) %collective-permute-start.1) | collective-permute-done | bytes 32800 | tf_op jit(solution)/shard_map/ppermute | solution.py:388
  70.3 3.2 %collective-permute-start.2 = (f32[80,128]{1,0:T(8,128)S(1)}, f32[80,128]{1,0:T(8,128)S(1)}, u32[]{:S(2)}, u32[]{:S(2)}) collective-permute-start(f32[80,128]{1,0:T(8,128)S(1)} %pad_maximum_fusion), channel_id=1, source_target_pairs={{0,1},{1,2},{2,3},{3,4},{4,5},{5,6},{6,7},{7,0},{8,9},{9,10},{10,1... | collective-permute-start | bytes 122888 | tf_op jit(solution)/shard_map/ppermute | solution.py:388
  74.8 2.8 %collective-permute-done.3.refs_6_ = f32[80,128]{1,0:T(8,128)S(1)} collective-permute-done((f32[80,128]{1,0:T(8,128)S(1)}, f32[80,128]{1,0:T(8,128)S(1)}, u32[]{:S(2)}, u32[]{:S(2)}) %collective-permute-start.3) | collective-permute-done | bytes 40992 | tf_op jit(solution)/shard_map/ppermute | solution.py:388
  78.3 9.4 %sweep.1 = (f32[256,768]{1,0:T(8,128)}, f32[256,128]{1,0:T(8,128)}, f32[256,768]{1,0:T(8,128)}, f32[2048,128]{1,0:T(8,128)}) custom-call(s32[4]{0:T(128)} %pad_add_fusion.refs_0_, f32[256,128]{1,0:T(8,128)} %get-tuple-element.36.phi_ref.refs_1_, f32[256,128]{1,0:T(8,128)} %get-tuple-element.40.refs_2_, f32[64,128]{1,0:T(8,128)} %copy-done.3, ...), custom_call_target="tpu_custom_call" | custom-call | tf_op jit(solution)/shard_map/sweep/pallas_call | solution.py:502
  87.7 9.1 %all-to-all-start.2 = ((f32[128,16,128]{2,1,0:T(8,128)}), f32[128,16,128]{2,1,0:T(8,128)S(1)}, u32[]{:S(2)}, u32[]{:S(2)}) async-start(f32[128,16,128]{2,1,0:T(8,128)} %bitcast.20), calls=%async_computation.2 | async-start | bytes 2097152 | tf_op jit(solution)/shard_map/all_to_all | solution.py:383
  96.8 11.6 %base.3.base_ref = f32[256,768]{1,0:T(8,128)} custom-call(f32[256,768]{1,0:T(8,128)} %get-tuple-element.50.volt_ref.refs_8_, f32[256,768]{1,0:T(8,128)} %get-tuple-element.51.recov_ref, f32[256,128]{1,0:T(8,128)} %get-tuple-element.38.id_ref, f32[256,768]{1,0:T(8,128)} %get-tuple-element.39.degree_ref, bf16[10,768,768]{2,1,0:T(8,128)(2,1)} %template_ref.3), custom_call_target="tpu_custom_call" | custom-call | flops 3000000000 | bytes 14000000 | tf_op jit(solution)/shard_map/base/pallas_call | solution.py:458
  108.4 3.9 %all-to-all-done.2 = f32[128,16,128]{2,1,0:T(8,128)S(1)} async-done(((f32[128,16,128]{2,1,0:T(8,128)}), f32[128,16,128]{2,1,0:T(8,128)S(1)}, u32[]{:S(2)}, u32[]{:S(2)}) %all-to-all-start.2) | async-done | bytes 1048608 | tf_op jit(solution)/shard_map/all_to_all | solution.py:383
  113.3 10.5 %gap.3 = (f32[256,768]{1,0:T(8,128)}, f32[256,128]{1,0:T(8,128)}, f32[64,128]{1,0:T(8,128)}, f32[64,128]{1,0:T(8,128)}, f32[64,128]{1,0:T(8,128)}, /*index=5*/f32[64,128]{1,0:T(8,128)}) custom-call(s32[16,128]{1,0:T(8,128)} %get-tuple-element.32.into_ref.refs_11_, s32[16,128]{1,0:T(8,128)} %get-tuple-element.34.own_ref.refs_13_, f32[2048,128]{1,0:T(8,128)} %bitcast.19, ...), custom_call_target="tpu_custom_call" | custom-call | tf_op jit(solution)/shard_map/gap/pallas_call | solution.py:475
  123.8 2.7 %collective-permute-start.4 = (f32[64,128]{1,0:T(8,128)}, f32[64,128]{1,0:T(8,128)S(1)}, u32[]{:S(2)}, u32[]{:S(2)}) collective-permute-start(f32[64,128]{1,0:T(8,128)} %get-tuple-element.53), channel_id=1, source_target_pairs={{0,8},{8,16},{16,24},{24,32},{32,40},{40,48},{48,56},{56,64},{64,7... | collective-permute-start | bytes 98312 | tf_op jit(solution)/shard_map/ppermute | solution.py:388
  127.8 5.0 %collective-permute-done.5.refs_4_ = f32[64,128]{1,0:T(8,128)S(1)} collective-permute-done((f32[64,128]{1,0:T(8,128)}, f32[64,128]{1,0:T(8,128)S(1)}, u32[]{:S(2)}, u32[]{:S(2)}) %collective-permute-start.5) | collective-permute-done | bytes 32800 | tf_op jit(solution)/shard_map/ppermute | solution.py:388
  133.5 3.2 %collective-permute-start.6 = (f32[80,128]{1,0:T(8,128)S(1)}, f32[80,128]{1,0:T(8,128)S(1)}, u32[]{:S(2)}, u32[]{:S(2)}) collective-permute-start(f32[80,128]{1,0:T(8,128)S(1)} %pad_maximum_fusion.2), channel_id=1, source_target_pairs={{0,1},{1,2},{2,3},{3,4},{4,5},{5,6},{6,7},{7,0},{8,9},{9,10},{10,1... | collective-permute-start | bytes 122888 | tf_op jit(solution)/shard_map/ppermute | solution.py:388
  137.8 3.1 %collective-permute-done.7.refs_6_ = f32[80,128]{1,0:T(8,128)S(1)} collective-permute-done((f32[80,128]{1,0:T(8,128)S(1)}, f32[80,128]{1,0:T(8,128)S(1)}, u32[]{:S(2)}, u32[]{:S(2)}) %collective-permute-start.7) | collective-permute-done | bytes 40992 | tf_op jit(solution)/shard_map/ppermute | solution.py:388
  141.5 4.9 %sweep_last.1 = (f32[256,768]{1,0:T(8,128)}, f32[1024,32]{1,0:T(8,128)}) custom-call(s32[4]{0:T(128)} %pad_add_fusion.refs_0_, f32[256,128]{1,0:T(8,128)} %get-tuple-element.48.phi_ref.refs_1_, f32[256,128]{1,0:T(8,128)} %get-tuple-element.52.refs_2_, f32[64,128]{1,0:T(8,128)} %copy-done.5, f32[64,128]{1,0:T(8,128)} %copy-done.6, f32[80,128]{1,0:T(8,128)} %copy-done.9, ...), custom_call_target="tpu_custom_call" | custom-call | tf_op jit(solution)/shard_map/sweep_last/pallas_call | solution.py:493
  (41 shorter events, 10.7 us)
Async XLA Ops:
  2.7 16.8 %all-to-all-start = ((f32[128,1,128]{2,1,0:T(1,128)}), f32[128,1,128]{2,1,0:T(1,128)S(1)}, u32[]{:S(2)}, u32[]{:S(2)}) async-start(f32[128,1,128]{2,1,0:T(1,128)} %bitcast.22), calls=%async_computation | async-start | bytes 131072 | tf_op jit(solution)/shard_map/all_to_all | solution.py:383
  19.5 0.6 copy-start.2
  25.3 24.8 %all-to-all-start.1 = ((f32[128,16,128]{2,1,0:T(8,128)}), f32[128,16,128]{2,1,0:T(8,128)S(1)}, u32[]{:S(2)}, u32[]{:S(2)}) async-start(f32[128,16,128]{2,1,0:T(8,128)} %bitcast.21), calls=%async_computation.1 | async-start | bytes 2097152 | tf_op jit(solution)/shard_map/all_to_all | solution.py:383
  50.1 1.0 copy-start
  61.6 3.0 %collective-permute-start = (f32[64,128]{1,0:T(8,128)}, f32[64,128]{1,0:T(8,128)S(1)}, u32[]{:S(2)}, u32[]{:S(2)}) collective-permute-start(f32[64,128]{1,0:T(8,128)} %get-tuple-element.41), channel_id=1, source_target_pairs={{0,8},{8,16},{16,24},{24,32},{32,40},{40,48},{48,56},{56,64},{64,7... | collective-permute-start | bytes 98312 | tf_op jit(solution)/shard_map/ppermute | solution.py:388
  63.2 6.3 %collective-permute-start.1 = (f32[64,128]{1,0:T(8,128)}, f32[64,128]{1,0:T(8,128)S(1)}, u32[]{:S(2)}, u32[]{:S(2)}) collective-permute-start(f32[64,128]{1,0:T(8,128)} %get-tuple-element.42), channel_id=1, source_target_pairs={{0,120},{8,0},{16,8},{24,16},{32,24},{40,32},{48,40},{56,48},{64,5... | collective-permute-start | bytes 98312 | tf_op jit(solution)/shard_map/ppermute | solution.py:388
  64.6 13.1 %copy-start.3 = (f32[64,128]{1,0:T(8,128)}, f32[64,128]{1,0:T(8,128)S(1)}, u32[]{:S(2)}) copy-start(f32[64,128]{1,0:T(8,128)S(1)} %collective-permute-done.refs_3_) | copy-start | bytes 98308
  69.5 8.1 %copy-start.4 = (f32[64,128]{1,0:T(8,128)}, f32[64,128]{1,0:T(8,128)S(1)}, u32[]{:S(2)}) copy-start(f32[64,128]{1,0:T(8,128)S(1)} %collective-permute-done.1.refs_4_) | copy-start | bytes 98308
  70.3 4.5 %collective-permute-start.2 = (f32[80,128]{1,0:T(8,128)S(1)}, f32[80,128]{1,0:T(8,128)S(1)}, u32[]{:S(2)}, u32[]{:S(2)}) collective-permute-start(f32[80,128]{1,0:T(8,128)S(1)} %pad_maximum_fusion), channel_id=1, source_target_pairs={{0,1},{1,2},{2,3},{3,4},{4,5},{5,6},{6,7},{7,0},{8,9},{9,10},{10,1... | collective-permute-start | bytes 122888 | tf_op jit(solution)/shard_map/ppermute | solution.py:388
  74.2 3.4 %collective-permute-start.3 = (f32[80,128]{1,0:T(8,128)S(1)}, f32[80,128]{1,0:T(8,128)S(1)}, u32[]{:S(2)}, u32[]{:S(2)}) collective-permute-start(f32[80,128]{1,0:T(8,128)S(1)} %pad_maximum_fusion.1), channel_id=1, source_target_pairs={{0,7},{1,0},{2,1},{3,2},{4,3},{5,4},{6,5},{7,6},{8,15},{9,8},{10,9... | collective-permute-start | bytes 122888 | tf_op jit(solution)/shard_map/ppermute | solution.py:388
  74.8 2.9 %copy-start.7 = (f32[80,128]{1,0:T(8,128)}, f32[80,128]{1,0:T(8,128)S(1)}, u32[]{:S(2)}) copy-start(f32[80,128]{1,0:T(8,128)S(1)} %collective-permute-done.2.refs_5_) | copy-start | bytes 122884
  77.6 0.6 copy-start.8
  87.7 24.6 %all-to-all-start.2 = ((f32[128,16,128]{2,1,0:T(8,128)}), f32[128,16,128]{2,1,0:T(8,128)S(1)}, u32[]{:S(2)}, u32[]{:S(2)}) async-start(f32[128,16,128]{2,1,0:T(8,128)} %bitcast.20), calls=%async_computation.2 | async-start | bytes 2097152 | tf_op jit(solution)/shard_map/all_to_all | solution.py:383
  112.4 1.0 copy-start.1
  123.8 4.0 %collective-permute-start.4 = (f32[64,128]{1,0:T(8,128)}, f32[64,128]{1,0:T(8,128)S(1)}, u32[]{:S(2)}, u32[]{:S(2)}) collective-permute-start(f32[64,128]{1,0:T(8,128)} %get-tuple-element.53), channel_id=1, source_target_pairs={{0,8},{8,16},{16,24},{24,32},{32,40},{40,48},{48,56},{56,64},{64,7... | collective-permute-start | bytes 98312 | tf_op jit(solution)/shard_map/ppermute | solution.py:388
  126.5 6.3 %collective-permute-start.5 = (f32[64,128]{1,0:T(8,128)}, f32[64,128]{1,0:T(8,128)S(1)}, u32[]{:S(2)}, u32[]{:S(2)}) collective-permute-start(f32[64,128]{1,0:T(8,128)} %get-tuple-element.54), channel_id=1, source_target_pairs={{0,120},{8,0},{16,8},{24,16},{32,24},{40,32},{48,40},{56,48},{64,5... | collective-permute-start | bytes 98312 | tf_op jit(solution)/shard_map/ppermute | solution.py:388
  127.8 13.1 %copy-start.5 = (f32[64,128]{1,0:T(8,128)}, f32[64,128]{1,0:T(8,128)S(1)}, u32[]{:S(2)}) copy-start(f32[64,128]{1,0:T(8,128)S(1)} %collective-permute-done.4.refs_3_) | copy-start | bytes 98308
  132.8 8.1 %copy-start.6 = (f32[64,128]{1,0:T(8,128)}, f32[64,128]{1,0:T(8,128)S(1)}, u32[]{:S(2)}) copy-start(f32[64,128]{1,0:T(8,128)S(1)} %collective-permute-done.5.refs_4_) | copy-start | bytes 98308
  133.5 4.3 %collective-permute-start.6 = (f32[80,128]{1,0:T(8,128)S(1)}, f32[80,128]{1,0:T(8,128)S(1)}, u32[]{:S(2)}, u32[]{:S(2)}) collective-permute-start(f32[80,128]{1,0:T(8,128)S(1)} %pad_maximum_fusion.2), channel_id=1, source_target_pairs={{0,1},{1,2},{2,3},{3,4},{4,5},{5,6},{6,7},{7,0},{8,9},{9,10},{10,1... | collective-permute-start | bytes 122888 | tf_op jit(solution)/shard_map/ppermute | solution.py:388
  137.5 3.4 %collective-permute-start.7 = (f32[80,128]{1,0:T(8,128)S(1)}, f32[80,128]{1,0:T(8,128)S(1)}, u32[]{:S(2)}, u32[]{:S(2)}) collective-permute-start(f32[80,128]{1,0:T(8,128)S(1)} %pad_maximum_fusion.3), channel_id=1, source_target_pairs={{0,7},{1,0},{2,1},{3,2},{4,3},{5,4},{6,5},{7,6},{8,15},{9,8},{10,9... | collective-permute-start | bytes 122888 | tf_op jit(solution)/shard_map/ppermute | solution.py:388
  137.8 3.1 %copy-start.9 = (f32[80,128]{1,0:T(8,128)}, f32[80,128]{1,0:T(8,128)S(1)}, u32[]{:S(2)}) copy-start(f32[80,128]{1,0:T(8,128)S(1)} %collective-permute-done.6.refs_5_) | copy-start | bytes 122884
  140.9 0.6 copy-start.10

commit v2 on v1

--- a/solution.py
+++ b/solution.py
@@ -26,6 +26,7 @@
 SMEM = pl.BlockSpec(memory_space=pltpu.SMEM)
 NT = (((1,), (1,)), ((), ()))
 TN = (((0,), (0,)), ((), ()))
+PARAMS = pltpu.CompilerParams(vmem_limit_bytes=67_043_328)
 
 
 def iota(shape, dim):
@@ -96,39 +97,54 @@
         rows_ref[512 * j + 256 : 512 * j + 512, :] = jnp.where(low, turned, pair)
 
 
-def gather_rows(rows_ref, index_ref, scale_ref, out_ref, offset, stride):
+def start_slots(index_ref, slots, sem):
+    copies = [
+        pltpu.make_async_copy(index_ref.at[pl.ds(s, 1), :], slot, sem.at[s]) for s, slot in enumerate(slots)
+    ]
+    for copy in copies:
+        copy.start()
+    return copies
+
+
+def gather_rows(rows_ref, slots, scale_ref, out_ref, offset, stride):
     low = low_half(1)
 
-    def body(r, carry):
-        scale_base = pl.multiple_of(r * 64, 64)
-        out_base = pl.multiple_of(r * (8 * stride), 8 * stride)
-        for m in range(64):
-            a = index_ref[r, 2 * m]
-            b = index_ref[r, 2 * m + 1]
-            row = jnp.where(low, rows_ref[pl.ds(a, 1), :], rows_ref[pl.ds(b, 1), :])
-            place = (m // 8) * stride + offset + m % 8
-            out_ref[pl.ds(out_base + place, 1), :] = row * scale_ref[pl.ds(scale_base + m, 1), :]
+    def body(i, carry):
+        for u in range(2):
+            d = 2 * i + u
+            scale_base = pl.multiple_of(d * 8, 8)
+            out_base = pl.multiple_of(d * stride, 8)
+            for p in range(8):
+                a = slots[p][0, d]
+                b = slots[p + 8][0, d]
+                row = jnp.where(low, rows_ref[pl.ds(a, 1), :], rows_ref[pl.ds(b, 1), :])
+                out_ref[pl.ds(out_base + (offset + p), 1), :] = row * scale_ref[pl.ds(scale_base + p, 1), :]
         return carry
 
-    lax.fori_loop(0, DEVS // 8, body, 0)
+    lax.fori_loop(0, DEVS // 2, body, 0)
 
 
 def gather_kernel(incoming, *refs):
     if incoming:
         table_ref, volt_ref, sent_ref, out_ref = refs[:4]
+        refs = refs[4:]
     else:
         table_ref, volt_ref, out_ref = refs[:3]
-    index_ref, conduct_ref, scale_ref, rows_ref, scratch, index_sm, sem = refs[-7:]
+        refs = refs[3:]
+    index_ref, number_ref, conduct_ref, scale_ref, rows_ref, scratch = refs[:6]
+    slots, sem = refs[6:22], refs[22]
+    first = 0 if incoming else 32
     table = table_ref[...]
     numbers = 64.0 * table + pltpu.roll(table, 112, 1)
-    index_ref[...] = decode(numbers, 0 if incoming else 32, scratch).astype(I32)
-    copy = pltpu.make_async_copy(index_ref, index_sm, sem)
-    copy.start()
+    index_ref[...] = numbers.T[first : first + 16, :].astype(I32)
+    copies = start_slots(index_ref, slots, sem)
+    number_ref[...] = decode(numbers, first, scratch).astype(I32)
     conducts = table + pltpu.roll(table, 112, 1) + pltpu.roll(table, 96, 1)
     conduct_ref[...] = decode(conducts, 64, scratch)
     part = iota((128, 1024), 0)
     lane = iota((128, 1024), 1)
-    spread = flag((part >= 64) & (part < 112) & ((part & 15) == (lane >> 6)))
+    slot = (lane >> 7) + 8 * ((lane >> 6) & 1)
+    spread = flag((part >= 64) & (part < 112) & ((part & 15) == slot))
     scale = jnp.dot(table.astype(BF16), spread, preferred_element_type=F32)
     for p in range(8):
         scale_ref[pl.ds(p, DEVS, stride=8), :] = scale[:, 128 * p : 128 * p + 128]
@@ -136,23 +152,46 @@
     if incoming:
         for d in range(DEVS):
             out_ref[16 * d : 16 * d + 8, :] = sent_ref[8 * d : 8 * d + 8, :]
-    copy.wait()
+    for copy in copies:
+        copy.wait()
     if incoming:
-        gather_rows(rows_ref, index_sm, scale_ref, out_ref, 8, 16)
+        gather_rows(rows_ref, slots, scale_ref, out_ref, 8, 16)
     else:
-        gather_rows(rows_ref, index_sm, scale_ref, out_ref, 0, 8)
+        gather_rows(rows_ref, slots, scale_ref, out_ref, 0, 8)
 
 
 def expander(rows, j):
     return (iota((rows, 128), 0) & 15) == 2 * j + (iota((rows, 128), 1) >> 6)
 
 
-def prepare_kernel(into_ref, into_conduct_ref, own_ref, own_conduct_ref, id_ref, ecs_ref, degree_ref, id_out, phi_out):
+def grid_row(point):
+    return ((point >> 7) & 7) * TILE + (point >> 10)
+
+
+def prepare_kernel(
+    into_ref,
+    into_conduct_ref,
+    own_ref,
+    own_conduct_ref,
+    id_ref,
+    ecs_ref,
+    point_ref,
+    degree_ref,
+    id_out,
+    phi_out,
+    slot_out,
+    place_ref,
+    found_ref,
+):
     cell = iota((CELLS, 128), 0)
     kind = iota((16, 128), 0)
+    place_ref[...] = jnp.zeros_like(place_ref)
+    place_ref[0:PER, :] = grid_row(point_ref[...]).astype(F32)
+    place_ref[16 : 16 + PER, :] = (point_ref[...] & 127).astype(F32)
+    places = place_ref[...].astype(BF16)
     total = jnp.zeros((48, CELLS), F32)
-    for index_ref, conduct_ref in ((into_ref, into_conduct_ref), (own_ref, own_conduct_ref)):
-        for s in range(CAP):
+    for side, (index_ref, conduct_ref) in enumerate(((into_ref, into_conduct_ref), (own_ref, own_conduct_ref))):
+        for s in range(16):
             number = index_ref[s : s + 1, :]
             hit = flag((number & 255) == cell)
             here = (number >> 8) == kind
@@ -160,6 +199,17 @@
             second, third = split2(rest)
             values = jnp.concatenate([jnp.where(here, x, 0.0) for x in (first, second, third)], axis=0)
             total = total + lax.dot_general(values.astype(BF16), hit, NT, preferred_element_type=F32)
+            found = jnp.dot(places, hit, preferred_element_type=F32)
+            for part in range(2):
+                picked = jnp.where(here, found[16 * part : 16 * part + 16, :], 0.0)
+                at = 32 * part + 16 * side + s
+                found_ref[at : at + 1, :] = jnp.sum(picked, axis=0, keepdims=True)
+    upper = (iota((16, 128), 1) & 8) != 0
+    for part in range(2):
+        into = found_ref[32 * part : 32 * part + 16, :]
+        own = found_ref[32 * part + 16 : 32 * part + 32, :]
+        slot_out[32 * part : 32 * part + 16, :] = jnp.where(upper, pltpu.roll(own, 8, 1), into).astype(I32)
+        slot_out[32 * part + 16 : 32 * part + 32, :] = jnp.where(upper, own, pltpu.roll(into, 120, 1)).astype(I32)
     total = total[0:16, :] + total[16:32, :] + total[32:48, :]
     first, rest = split2(total)
     second, third = split2(rest)
@@ -178,98 +228,77 @@
             phi_out[TILE * t : TILE * t + TILE, 32 * y : 32 * y + 32] = rows
 
 
-def base_kernel(volt_ref, recov_ref, id_ref, degree_ref, template_ref, out_ref, volt_bf):
-    index = pl.program_id(0)
-
-    @pl.when(index == 0)
-    def _():
-        volt_bf[...] = volt_ref[...].astype(BF16)
-        out_ref[...] = jnp.zeros_like(out_ref)
-
-    mine = id_ref[...] == index.astype(F32)
-    masked = jnp.concatenate(
-        [
-            jnp.where(mine, volt_bf[:, 128 * j : 128 * j + 128], jnp.zeros((), BF16))
-            for j in range(PER // 2)
-        ],
-        axis=1,
-    )
-    out_ref[...] += jnp.dot(masked, template_ref[0], preferred_element_type=F32)
-
-    @pl.when(index == pl.num_programs(0) - 1)
-    def _():
-        volt = volt_ref[...]
-        ion = volt - volt * volt * volt * (1.0 / 3.0) - recov_ref[...]
-        out_ref[...] += degree_ref[...] * volt - ion
-
-
-def grid_row(point):
-    return ((point >> 7) & 7) * TILE + (point >> 10)
-
-
-def gap_kernel(
-    into_ref,
-    own_ref,
-    got_ref,
-    base_ref,
-    point_ref,
-    phi_ref,
-    current_ref,
-    deposit_ref,
-    x_low_ref,
-    x_high_ref,
-    y_low_ref,
-    y_high_ref,
-    even_in,
-    odd_in,
-    even_out,
-    odd_out,
-):
-    for ref in (even_in, odd_in, even_out, odd_out):
-        ref[...] = jnp.zeros_like(ref)
-
-    def body(r, carry):
-        base = pl.multiple_of(r * 128, 128)
-        for m in range(64):
-            at = (m // 8) * 16 + m % 8
-            row = got_ref[pl.ds(base + at, 1), :]
-            back = got_ref[pl.ds(base + (at + 8), 1), :]
-            even_in[pl.ds(into_ref[r, 2 * m], 1), :] += row
-            odd_in[pl.ds(into_ref[r, 2 * m + 1], 1), :] += row
-            even_out[pl.ds(own_ref[r, 2 * m], 1), :] += back
-            odd_out[pl.ds(own_ref[r, 2 * m + 1], 1), :] += back
+def deposited(total, row, column, mean):
+    hit = flag(row == iota((CELLS, CELLS), 0))
+    here = column == iota((128, CELLS), 0)
+    spread = jnp.concatenate([jnp.where(here, x, 0.0) for x in split2(mean)], axis=0)
+    return total + lax.dot_general(hit, spread.astype(BF16), NT, preferred_element_type=F32)
+
+
+def base_kernel(volt_ref, recov_ref, id_ref, degree_ref, point_ref, template_ref, out_ref, deposit_ref, volt_bf, held, sem):
+    count = held.shape[0]
+    copies = [pltpu.make_async_copy(template_ref.at[i], held.at[i], sem.at[i]) for i in range(count)]
+    for copy in copies:
+        copy.start()
+    volt = volt_ref[...]
+    volt_bf[...] = volt.astype(BF16)
+    out_ref[...] = degree_ref[...] * volt - (volt - volt * volt * volt * (1.0 / 3.0) - recov_ref[...])
+
+    def body(i, carry):
+        parts = []
+        for u in range(2):
+            index = 2 * i + u
+            pltpu.make_async_copy(template_ref.at[index], held.at[index], sem.at[index]).wait()
+            mine = id_ref[...] == index.astype(F32)
+            parts += [
+                jnp.where(mine, volt_bf[:, 128 * j : 128 * j + 128], jnp.zeros((), BF16))
+                for j in range(PER // 2)
+            ]
+        both = held[pl.ds(2 * i, 2)].reshape(2 * NODES, NODES)
+        out_ref[...] += jnp.dot(jnp.concatenate(parts, axis=1), both, preferred_element_type=F32)
         return carry
 
-    lax.fori_loop(0, DEVS // 8, body, 0)
-
-    low = low_half(CELLS)
+    lax.fori_loop(0, count // 2, body, 0)
     means = jnp.zeros((16, CELLS), F32)
     for j in range(PER // 2):
-        sums = []
-        for k in (2 * j, 2 * j + 1):
-            cut = slice(CELLS * k, CELLS * k + CELLS)
-            even = even_in[cut, :] + even_out[cut, :]
-            odd = odd_in[cut, :] + odd_out[cut, :]
-            both = jnp.where(low, even, odd)
-            sums.append(both + pltpu.roll(both, 64, 1))
-        cut = slice(128 * j, 128 * j + 128)
-        current = base_ref[:, cut] - jnp.where(low, sums[0], sums[1])
-        current_ref[:, cut] = current
         weights = jnp.where(expander(16, j), 1.0 / BLOCK, 0.0).astype(BF16)
-        for part in split2(current):
+        for part in split2(out_ref[:, 128 * j : 128 * j + 128]):
             means = means + lax.dot_general(weights, part.astype(BF16), NT, preferred_element_type=F32)
-    mean_hi, mean_lo = split2(means)
-    row_of = iota((CELLS, CELLS), 0)
-    column_of = iota((128, CELLS), 0)
     total = jnp.zeros((CELLS, 256), F32)
     for k in range(PER):
         point = point_ref[k : k + 1, :]
-        hit = flag(grid_row(point) == row_of)
-        here = (point & 127) == column_of
-        spread = [jnp.where(here, x[k : k + 1, :], 0.0) for x in (mean_hi, mean_lo)]
-        spread = jnp.concatenate(spread, axis=0).astype(BF16)
-        total = total + lax.dot_general(hit, spread, NT, preferred_element_type=F32)
+        total = deposited(total, grid_row(point), point & 127, means[k : k + 1, :])
     deposit_ref[...] = total[:, 0:128] + total[:, 128:256]
+
+
+CHUNKS = 4
+
+
+def deposit_kernel(
+    got_any, base_ref, slot_ref, phi_ref, deposit_ref, x_low_ref, x_high_ref, y_low_ref, y_high_ref, got_ref, sem
+):
+    rows = got_ref.shape[0] // CHUNKS
+    copies = [
+        pltpu.make_async_copy(got_any.at[pl.ds(rows * i, rows), :], got_ref.at[pl.ds(rows * i, rows), :], sem.at[i])
+        for i in range(CHUNKS)
+    ]
+    for copy in copies:
+        copy.start()
+    lane = iota((16, 128), 1)
+    weights = jnp.where(iota((16, 128), 0) == (lane >> 6), 1.0 / BLOCK, 0.0).astype(BF16)
+    total = jnp.zeros((CELLS, 256), F32)
+    for r in range(16):
+        if r % (16 // CHUNKS) == 0:
+            copies[r // (16 // CHUNKS)].wait()
+        mean = jnp.zeros((16, 128), F32)
+        for part in split2(got_ref[128 * r : 128 * r + 128, :]):
+            mean = mean + lax.dot_general(weights, part.astype(BF16), NT, preferred_element_type=F32)
+
+        def both(at):
+            return jnp.concatenate([slot_ref[at + r : at + r + 1, :], slot_ref[at + 16 + r : at + 17 + r, :]], axis=1)
+
+        total = deposited(total, both(0), both(32), jnp.concatenate([mean[0:1, :], mean[1:2, :]], axis=1))
+    deposit_ref[...] = base_ref[...] - (total[:, 0:128] + total[:, 128:256])
     for array, at, across in ((phi_ref, 0, 0), (deposit_ref, HALO, TILE)):
         for t in range(TILES):
             start = TILE * t
@@ -279,6 +308,43 @@
         y_high_ref[across : across + TILE, :] = array[TILE * (TILES - 1) :, :]
 
 
+def collect_kernel(offset, index_ref, got_ref, base_ref, out_ref, *scratch):
+    lower, upper, slots, sem = scratch[0:2], scratch[2:4], scratch[4:20], scratch[20]
+    copies = start_slots(index_ref, slots, sem)
+    for ref in (*lower, *upper):
+        ref[...] = jnp.zeros_like(ref)
+    for copy in copies:
+        copy.wait()
+
+    def body(i, carry):
+        for u in range(2):
+            d = 2 * i + u
+            base = pl.multiple_of(d * 16, 16)
+            for p in range(8):
+                row = got_ref[pl.ds(base + (offset + p), 1), :]
+                lower[p % 2][pl.ds(slots[p][0, d], 1), :] += row
+                upper[p % 2][pl.ds(slots[p + 8][0, d], 1), :] += row
+        return carry
+
+    lax.fori_loop(0, DEVS // 2, body, 0)
+    low = low_half(CELLS)
+    for j in range(PER // 2):
+        sums = []
+        for k in (2 * j, 2 * j + 1):
+            cut = slice(CELLS * k, CELLS * k + CELLS)
+            both = jnp.where(low, lower[0][cut, :] + lower[1][cut, :], upper[0][cut, :] + upper[1][cut, :])
+            sums.append(both + pltpu.roll(both, 64, 1))
+        cut = slice(128 * j, 128 * j + 128)
+        out_ref[:, cut] = base_ref[:, cut] - jnp.where(low, sums[0], sums[1])
+
+
+def frame_kernel(before_ref, after_ref, y_low_ref, y_high_ref, low_ref, high_ref):
+    for middle_ref, out_ref, at in ((y_low_ref, low_ref, 0), (y_high_ref, high_ref, 8 * (TILES - 1))):
+        out_ref[0:8, :] = before_ref[at : at + 8, :]
+        out_ref[8:72, :] = middle_ref[...]
+        out_ref[72:80, :] = after_ref[at : at + 8, :]
+
+
 ROWS = TILE + 2 * HALO
 LEAD = 8
 
@@ -290,7 +356,9 @@
         volt_out, phi_out, wide_phi, wide_deposit, found_ref = refs[10:]
     else:
         recov_ref, into_ref, into_scale_ref, own_ref, own_scale_ref = refs[10:15]
-        volt_out, phi_out, recov_out, send_out, wide_phi, wide_deposit, found_ref, rows_ref = refs[15:]
+        volt_out, phi_out, recov_out, send_out, wide_phi, wide_deposit, found_ref, rows_ref = refs[15:23]
+        own_slots, into_slots, own_sem, into_sem = refs[23:39], refs[39:55], refs[55], refs[56]
+        copies = start_slots(own_ref, own_slots, own_sem) + start_slots(into_ref, into_slots, into_sem)
     end = LEAD + ROWS
     high = LEAD + HALO + TILE
     for wide, array, at, across in ((wide_phi, phi_ref, 0, 0), (wide_deposit, deposit_ref, HALO, TILE)):
@@ -320,7 +388,7 @@
         keep = jnp.where(inside, side[0 if t == 0 else 1], 0.0) if t in edge else jnp.where(inside, 1.0, 0.0)
         wide_phi[t, LEAD:end, :] = jnp.where(keep > 0.0, wide_phi[t, LEAD:end, :], 0.0)
     nothing = jnp.zeros(shape, F32)
-    for sweep in range(SWEEPS):
+    for _ in range(SWEEPS):
         middle = [wide_phi[t, LEAD:end, :] for t in range(TILES + 2)]
         fresh = []
         ups = [pltpu.roll(x, 32, 1) for x in middle]
@@ -371,8 +439,10 @@
             rows_ref[512 * j : 512 * j + 256, :] = jnp.where(low, fresh, turned)
             rows_ref[512 * j + 256 : 512 * j + 512, :] = jnp.where(low, turned, fresh)
     if not last:
-        gather_rows(rows_ref, own_ref, own_scale_ref, send_out, 0, 16)
-        gather_rows(rows_ref, into_ref, into_scale_ref, send_out, 8, 16)
+        for copy in copies:
+            copy.wait()
+        gather_rows(rows_ref, own_slots, own_scale_ref, send_out, 0, 16)
+        gather_rows(rows_ref, into_slots, into_scale_ref, send_out, 8, 16)
 
 
 def shaped(*shape, dtype=F32):
@@ -406,6 +476,7 @@
         out_shape=shaped(128, 128),
         in_specs=[VMEM] * 4,
         out_specs=VMEM,
+        compiler_params=PARAMS,
         name="setup",
     )(
         patch_dev.reshape(flat),
@@ -415,77 +486,106 @@
     )
     got_table = exchange(table)
     rows_scratch = pltpu.VMEM((PER * CELLS, 128), F32)
-    tables_out = (shaped(16, 128, dtype=I32), shaped(16, 128), shaped(DEVS * 8, 128))
-    gather_scratch = [
-        rows_scratch,
-        pltpu.VMEM((128, 128), F32),
-        pltpu.SMEM((16, 128), I32),
-        pltpu.SemaphoreType.DMA,
-    ]
-    sent, own, own_conduct, own_scale = pl.pallas_call(
+    slot_scratch = [pltpu.SMEM((1, 128), I32)] * CAP
+    slot_sem = pltpu.SemaphoreType.DMA((CAP,))
+    small = shaped(16, 128, dtype=I32)
+    tables_out = (small, small, shaped(16, 128), shaped(DEVS * 8, 128))
+    gather_scratch = [rows_scratch, pltpu.VMEM((128, 128), F32)] + slot_scratch + [slot_sem]
+    sent, own, own_number, own_conduct, own_scale = pl.pallas_call(
         functools.partial(gather_kernel, False),
         out_shape=(shaped(DEVS * 8, 128),) + tables_out,
         in_specs=[VMEM] * 2,
-        out_specs=(VMEM,) * 4,
+        out_specs=(VMEM,) * 5,
         scratch_shapes=gather_scratch,
+        compiler_params=PARAMS,
         name="gather_source",
     )(table, potential)
-    outgoing, into, into_conduct, into_scale = pl.pallas_call(
+    outgoing, into, into_number, into_conduct, into_scale = pl.pallas_call(
         functools.partial(gather_kernel, True),
         out_shape=(shaped(DEVS * 16, 128),) + tables_out,
         in_specs=[VMEM] * 3,
-        out_specs=(VMEM,) * 4,
+        out_specs=(VMEM,) * 5,
         scratch_shapes=gather_scratch,
+        compiler_params=PARAMS,
         name="gather_target",
     )(got_table, potential, sent)
-    degree, id_wide, phi = pl.pallas_call(
+    points = memb_point.reshape(CELLS, PER).T
+    degree, id_wide, phi, slot_points = pl.pallas_call(
         prepare_kernel,
-        out_shape=(shaped(CELLS, NODES), shaped(CELLS, 128), shaped(TILE * TILES, 128)),
-        in_specs=[VMEM] * 6,
-        out_specs=(VMEM,) * 3,
+        out_shape=(shaped(CELLS, NODES), shaped(CELLS, 128), shaped(TILE * TILES, 128), shaped(64, 128, dtype=I32)),
+        in_specs=[VMEM] * 7,
+        out_specs=(VMEM,) * 4,
+        scratch_shapes=[pltpu.VMEM((32, CELLS), F32), pltpu.VMEM((64, 128), F32)],
+        compiler_params=PARAMS,
         name="prepare",
-    )(into, into_conduct, own, own_conduct, template_id.reshape(2, 128), ecs_start.reshape(TILE * TILE, TILE))
+    )(
+        into_number,
+        into_conduct,
+        own_number,
+        own_conduct,
+        template_id.reshape(2, 128),
+        ecs_start.reshape(TILE * TILE, TILE),
+        points,
+    )
 
     place = jnp.stack([lax.axis_index("tx"), lax.axis_index("ty"), lax.axis_size("tx"), lax.axis_size("ty")])
     place = place.astype(I32)
-    points = memb_point.reshape(CELLS, PER).T
     volt = potential
     recov = gating
-    whole = lambda *shape: pl.BlockSpec(shape, lambda i: (0,) * len(shape))
+    anywhere = pl.BlockSpec(memory_space=pl.ANY)
     for step in range(STEPS):
         last = step == STEPS - 1
         got = exchange(outgoing.reshape(DEVS, 16, 128)).reshape(DEVS * 16, 128)
-        base = pl.pallas_call(
+        base, deposit_base = pl.pallas_call(
             base_kernel,
-            grid=(templates.shape[0],),
-            out_shape=shaped(CELLS, NODES),
-            in_specs=[
-                whole(CELLS, NODES),
-                whole(CELLS, NODES),
-                whole(CELLS, 128),
-                whole(CELLS, NODES),
-                pl.BlockSpec((1, NODES, NODES), lambda i: (i, 0, 0)),
+            out_shape=(shaped(CELLS, NODES), shaped(TILE * TILES, 128)),
+            in_specs=[VMEM] * 5 + [anywhere],
+            out_specs=(VMEM,) * 2,
+            scratch_shapes=[
+                pltpu.VMEM((CELLS, NODES), BF16),
+                pltpu.VMEM(templates.shape, BF16),
+                pltpu.SemaphoreType.DMA((templates.shape[0],)),
             ],
-            out_specs=whole(CELLS, NODES),
-            scratch_shapes=[pltpu.VMEM((CELLS, NODES), BF16)],
             cost_estimate=pl.CostEstimate(flops=3_000_000_000, bytes_accessed=14_000_000, transcendentals=0),
+            compiler_params=PARAMS,
             name="base",
-        )(volt, recov, id_wide, degree, templates)
-        accumulator = pltpu.VMEM((PER * CELLS, 128), F32)
-        current, deposit, x_low, x_high, y_low, y_high = pl.pallas_call(
-            gap_kernel,
-            out_shape=(shaped(CELLS, NODES), shaped(TILE * TILES, 128)) + (shaped(64, 128),) * 4,
-            in_specs=[SMEM] * 2 + [VMEM] * 4,
-            out_specs=(VMEM,) * 6,
-            scratch_shapes=[accumulator] * 4,
-            name="gap",
-        )(into, own, got, base, points, phi)
+        )(volt, recov, id_wide, degree, points, templates)
+        deposit, x_low, x_high, y_low, y_high = pl.pallas_call(
+            deposit_kernel,
+            out_shape=(shaped(TILE * TILES, 128),) + (shaped(64, 128),) * 4,
+            in_specs=[anywhere] + [VMEM] * 3,
+            out_specs=(VMEM,) * 5,
+            scratch_shapes=[pltpu.VMEM((DEVS * 16, 128), F32), pltpu.SemaphoreType.DMA((CHUNKS,))],
+            compiler_params=PARAMS,
+            name="deposit",
+        )(got, deposit_base, slot_points, phi)
+
+        def collect(offset, index, start):
+            return pl.pallas_call(
+                functools.partial(collect_kernel, offset),
+                out_shape=shaped(CELLS, NODES),
+                in_specs=[VMEM] * 3,
+                out_specs=VMEM,
+                scratch_shapes=[rows_scratch] * 4 + slot_scratch + [slot_sem],
+                cost_estimate=pl.CostEstimate(flops=1_000_000_000, bytes_accessed=10_000_000, transcendentals=0),
+                compiler_params=PARAMS,
+                name="collect_own" if offset else "collect_into",
+            )(index, got, start)
+
         x_before = shift(x_high, "tx", 1)
         x_after = shift(x_low, "tx", -1)
-        y_low = jnp.concatenate([x_before[0:8], y_low, x_after[0:8]])
-        y_high = jnp.concatenate([x_before[56:64], y_high, x_after[56:64]])
+        current = collect(0, into, base)
+        y_low, y_high = pl.pallas_call(
+            frame_kernel,
+            out_shape=(shaped(80, 128),) * 2,
+            in_specs=[VMEM] * 4,
+            out_specs=(VMEM,) * 2,
+            compiler_params=PARAMS,
+            name="frame",
+        )(x_before, x_after, y_low, y_high)
         y_before = shift(y_high, "ty", 1)
         y_after = shift(y_low, "ty", -1)
+        current = collect(8, own, current)
         operands = [place, phi, deposit, x_before, x_after, y_before, y_after, current, volt, points]
         specs = [SMEM] + [VMEM] * 9
         wide = [pltpu.VMEM((TILES + 2, LEAD + ROWS + 8, 128), F32)] * 2 + [pltpu.VMEM((16, CELLS), F32)]
@@ -496,6 +596,7 @@
                 in_specs=specs,
                 out_specs=(VMEM,) * 2,
                 scratch_shapes=wide,
+                compiler_params=PARAMS,
                 name="sweep_last",
             )(*operands)
         else:
@@ -507,9 +608,10 @@
                     shaped(CELLS, NODES),
                     shaped(DEVS * 16, 128),
                 ),
-                in_specs=specs + [VMEM, SMEM, VMEM, SMEM, VMEM],
+                in_specs=specs + [VMEM] * 5,
                 out_specs=(VMEM,) * 4,
-                scratch_shapes=wide + [rows_scratch],
+                scratch_shapes=wide + [rows_scratch] + slot_scratch * 2 + [slot_sem] * 2,
+                compiler_params=PARAMS,
                 name="sweep",
             )(*operands, recov, into, into_scale, own, own_scale)
     return (volt, phi.reshape(TILE, TILE, TILE))

time: 149 us -> 152 us (1.020)
  the two profiles are of different devices: /device:TPU:31 before, /device:TPU:0 now
where the time goes in v2:
time: 152 us; the launch traced here: 151 us
  Pallas kernels  90.6 us (60%)
  starting transfers between devices  40 us (26%)
  waiting for transfers between devices  17.5 us (12%)
  local copies, waits for them, and re-layouts  1.53 us (1%)
    pallas_call x4, Pallas kernels, collect(): pl.pallas_call(functools.partial(collect_kernel, offset), out_shape=shape...  27.7 us
    all_to_all x3, starting transfers between devices, exchange(): return lax.all_to_all(x, AXES, split_axis=0, concat_axis=0, tiled=True)  23.3 us
    pallas_call x2, Pallas kernels, on_device(): pl.pallas_call(base_kernel, out_shape=(shaped(CELLS, NODES), shaped(TILE...  19.1 us
    all_to_all x3, waiting for transfers between devices, exchange(): return lax.all_to_all(x, AXES, split_axis=0, concat_axis=0, tiled=True)  17.4 us
    ppermute x8, starting transfers between devices, shift(): return lax.ppermute(x, axis, [(i, (i + by) % size) for i in range(size)])  16.7 us
    pallas_call x1, Pallas kernels, on_device(): pl.pallas_call(functools.partial(sweep_kernel, False), out_shape=(shaped(...  10.2 us
    pallas_call x2, Pallas kernels, on_device(): pl.pallas_call(deposit_kernel, out_shape=(shaped(TILE * TILES, 128),) + (...  10.1 us
    pallas_call x1, Pallas kernels, on_device(): pl.pallas_call(functools.partial(gather_kernel, True), out_shape=(shaped(...  5.23 us
  transfers between devices with their start and end apart: 11, of which 3 were waited for; matrix products, arithmetic and copies ran while one was open for 1% of the time, Pallas kernels for 37%

profile of v2, /device:TPU:0, one launch (start us, length us, event | category | flops | bytes accessed | tf_op | source)
XLA Modules:
  0.0 151.1 jit_solution(10716181731199240398)
XLA Ops:
  0.6 2.1 %setup.1.refs_0_ = f32[128,128]{1,0:T(8,128)} custom-call(s32[8,128]{1,0:T(8,128)} %bitcast.27, s32[8,128]{1,0:T(8,128)} %bitcast.28, s32[8,128]{1,0:T(8,128)} %bitcast.29, f32[8,128]{1,0:T(8,128)} %bitcast.30), custom_call_target="tpu_custom_call" | custom-call | tf_op jit(solution)/shard_map/setup/pallas_call | solution.py:474
  2.7 11.7 %all-to-all-start = ((f32[128,1,128]{2,1,0:T(1,128)}), f32[128,1,128]{2,1,0:T(1,128)}, u32[]{:S(2)}, u32[]{:S(2)}) async-start(f32[128,1,128]{2,1,0:T(1,128)} %bitcast.20), calls=%async_computation | async-start | bytes 131072 | tf_op jit(solution)/shard_map/all_to_all | solution.py:453
  14.4 4.9 %gather_source.1 = (f32[1024,128]{1,0:T(8,128)}, s32[16,128]{1,0:T(8,128)}, s32[16,128]{1,0:T(8,128)}, f32[16,128]{1,0:T(8,128)}, f32[1024,128]{1,0:T(8,128)}) custom-call(f32[128,128]{1,0:T(8,128)} %setup.1.refs_0_, f32[256,768]{1,0:T(8,128)} %refs_8_.1), custom_call_target="tpu_custom_call" | custom-call | tf_op jit(solution)/shard_map/gather_source/pallas_call | solution.py:494
  19.3 4.6 %all-to-all-done = f32[128,1,128]{2,1,0:T(1,128)} async-done(((f32[128,1,128]{2,1,0:T(1,128)}), f32[128,1,128]{2,1,0:T(1,128)}, u32[]{:S(2)}, u32[]{:S(2)}) %all-to-all-start) | async-done | bytes 65568 | tf_op jit(solution)/shard_map/all_to_all | solution.py:453
  23.9 5.2 %gather_target.1 = (f32[2048,128]{1,0:T(8,128)}, s32[16,128]{1,0:T(8,128)}, s32[16,128]{1,0:T(8,128)}, f32[16,128]{1,0:T(8,128)}, f32[1024,128]{1,0:T(8,128)}) custom-call(f32[128,128]{1,0:T(8,128)} %bitcast.8.refs_0_, f32[256,768]{1,0:T(8,128)} %refs_8_.1, f32[1024,128]{1,0:T(8,128)} %get-tuple-element.40.refs_2_), custom_call_target="tpu_custom_call" | custom-call | tf_op jit(solution)/shard_map/gather_target/pallas_call | solution.py:503
  29.2 5.8 %all-to-all-start.1 = ((f32[128,16,128]{2,1,0:T(8,128)}), f32[128,16,128]{2,1,0:T(8,128)}, u32[]{:S(2)}, u32[]{:S(2)}) async-start(f32[128,16,128]{2,1,0:T(8,128)} %bitcast.18), calls=%async_computation.1 | async-start | bytes 2097152 | tf_op jit(solution)/shard_map/all_to_all | solution.py:453
  37.1 3.5 %prepare.1 = (f32[256,768]{1,0:T(8,128)}, f32[256,128]{1,0:T(8,128)}, f32[256,128]{1,0:T(8,128)}, s32[64,128]{1,0:T(8,128)}) custom-call(s32[16,128]{1,0:T(8,128)} %get-tuple-element.41.into_ref, f32[16,128]{1,0:T(8,128)} %get-tuple-element.42.into_conduct_ref, s32[16,128]{1,0:T(8,128)} %get-tuple-element.43.own_ref, ...), custom_call_target="tpu_custom_call" | custom-call | tf_op jit(solution)/shard_map/prepare/pallas_call | solution.py:513
  40.6 9.6 %base.2 = (f32[256,768]{1,0:T(8,128)}, f32[256,128]{1,0:T(8,128)}) custom-call(f32[256,768]{1,0:T(8,128)} %refs_8_.1, f32[256,768]{1,0:T(8,128)} %refs_10_.1, f32[256,128]{1,0:T(8,128)} %get-tuple-element.47.id_ref, f32[256,768]{1,0:T(8,128)} %get-tuple-element.48.degree_ref, s32[12,256]{1,0:T(8,128)} %bitcast.22, bf16[10,768,768]{2,1,0:T(8,128)(2,1)} %template_ref.3), custom_call_target="tpu_custom_call" | custom-call | flops 3000000000 | bytes 14000000 | tf_op jit(solution)/shard_map/base/pallas_call | solution.py:539
  50.2 3.6 %all-to-all-done.1 = f32[128,16,128]{2,1,0:T(8,128)} async-done(((f32[128,16,128]{2,1,0:T(8,128)}), f32[128,16,128]{2,1,0:T(8,128)}, u32[]{:S(2)}, u32[]{:S(2)}) %all-to-all-start.1) | async-done | bytes 1048608 | tf_op jit(solution)/shard_map/all_to_all | solution.py:453
  53.8 5.1 %deposit.2 = (f32[256,128]{1,0:T(8,128)}, f32[64,128]{1,0:T(8,128)}, f32[64,128]{1,0:T(8,128)}, f32[64,128]{1,0:T(8,128)}, f32[64,128]{1,0:T(8,128)}) custom-call(f32[2048,128]{1,0:T(8,128)} %bitcast.13.got_any.got_ref, f32[256,128]{1,0:T(8,128)} %get-tuple-element.49.base_ref, s32[64,128]{1,0:T(8,128)} %get-tuple-element.50.slot_ref, ...), custom_call_target="tpu_custom_call" | custom-call | tf_op jit(solution)/shard_map/deposit/pallas_call | solution.py:553
  59.6 4.7 %collective-permute-start.1 = (f32[64,128]{1,0:T(8,128)}, f32[64,128]{1,0:T(8,128)}, u32[]{:S(2)}, u32[]{:S(2)}) collective-permute-start(f32[64,128]{1,0:T(8,128)} %get-tuple-element.53), channel_id=1, source_target_pairs={{0,120},{8,0},{16,8},{24,16},{32,24},{40,32},{48,40},{56,48},{64,5... | collective-permute-start | bytes 98312 | tf_op jit(solution)/shard_map/ppermute | solution.py:458
  64.3 6.9 %collect_into.2.base_ref = f32[256,768]{1,0:T(8,128)} custom-call(s32[16,128]{1,0:T(8,128)} %get-tuple-element.59.index_ref.refs_11_, f32[2048,128]{1,0:T(8,128)} %bitcast.13.got_any.got_ref, f32[256,768]{1,0:T(8,128)} %get-tuple-element.60.base_ref), custom_call_target="tpu_custom_call" | custom-call | flops 1000000000 | bytes 10000000 | tf_op jit(solution)/shard_map/collect_into/pallas_call | solution.py:564
  72.7 3.0 %collective-permute-start.3 = (f32[80,128]{1,0:T(8,128)}, f32[80,128]{1,0:T(8,128)}, u32[]{:S(2)}, u32[]{:S(2)}) collective-permute-start(f32[80,128]{1,0:T(8,128)} %get-tuple-element.57), channel_id=1, source_target_pairs={{0,7},{1,0},{2,1},{3,2},{4,3},{5,4},{6,5},{7,6},{8,15},{9,8},{10,9... | collective-permute-start | bytes 122888 | tf_op jit(solution)/shard_map/ppermute | solution.py:458
  75.6 6.9 %collect_own.2.refs_7_ = f32[256,768]{1,0:T(8,128)} custom-call(s32[16,128]{1,0:T(8,128)} %get-tuple-element.58.index_ref.refs_13_, f32[2048,128]{1,0:T(8,128)} %bitcast.13.got_any.got_ref, f32[256,768]{1,0:T(8,128)} %collect_into.2.base_ref), custom_call_target="tpu_custom_call" | custom-call | flops 1000000000 | bytes 10000000 | tf_op jit(solution)/shard_map/collect_own/pallas_call | solution.py:564
  82.6 10.2 %sweep.1 = (f32[256,768]{1,0:T(8,128)}, f32[256,128]{1,0:T(8,128)}, f32[256,768]{1,0:T(8,128)}, f32[2048,128]{1,0:T(8,128)}) custom-call(s32[4]{0:T(128)} %pad_add_fusion.refs_0_, f32[256,128]{1,0:T(8,128)} %get-tuple-element.45.phi_ref.refs_1_, f32[256,128]{1,0:T(8,128)} %get-tuple-element.51.refs_2_, f32[64,128]{1,0:T(8,128)} %collective-permute-done.before_ref.refs_3_, ...), custom_call_target="tpu_custom_call" | custom-call | tf_op jit(solution)/shard_map/sweep/pallas_call | solution.py:603
  92.7 5.8 %all-to-all-start.2 = ((f32[128,16,128]{2,1,0:T(8,128)}), f32[128,16,128]{2,1,0:T(8,128)}, u32[]{:S(2)}, u32[]{:S(2)}) async-start(f32[128,16,128]{2,1,0:T(8,128)} %bitcast.19), calls=%async_computation.2 | async-start | bytes 2097152 | tf_op jit(solution)/shard_map/all_to_all | solution.py:453
  98.5 9.6 %base.3 = (f32[256,768]{1,0:T(8,128)}, f32[256,128]{1,0:T(8,128)}) custom-call(f32[256,768]{1,0:T(8,128)} %get-tuple-element.65.volt_ref.refs_8_, f32[256,768]{1,0:T(8,128)} %get-tuple-element.66.recov_ref, f32[256,128]{1,0:T(8,128)} %get-tuple-element.47.id_ref, f32[256,768]{1,0:T(8,128)} %get-tuple-element.48.degree_ref, s32[12,256]{1,0:T(8,128)} %bitcast.24, ...), custom_call_target="tpu_custom_call" | custom-call | flops 3000000000 | bytes 14000000 | tf_op jit(solution)/shard_map/base/pallas_call | solution.py:539
  108.1 9.3 %all-to-all-done.2 = f32[128,16,128]{2,1,0:T(8,128)} async-done(((f32[128,16,128]{2,1,0:T(8,128)}), f32[128,16,128]{2,1,0:T(8,128)}, u32[]{:S(2)}, u32[]{:S(2)}) %all-to-all-start.2) | async-done | bytes 1048608 | tf_op jit(solution)/shard_map/all_to_all | solution.py:453
  117.4 5.0 %deposit.3 = (f32[256,128]{1,0:T(8,128)}, f32[64,128]{1,0:T(8,128)}, f32[64,128]{1,0:T(8,128)}, f32[64,128]{1,0:T(8,128)}, f32[64,128]{1,0:T(8,128)}) custom-call(f32[2048,128]{1,0:T(8,128)} %bitcast.15.got_any.got_ref, f32[256,128]{1,0:T(8,128)} %get-tuple-element.67.base_ref, s32[64,128]{1,0:T(8,128)} %get-tuple-element.50.slot_ref, ...), custom_call_target="tpu_custom_call" | custom-call | tf_op jit(solution)/shard_map/deposit/pallas_call | solution.py:553
  123.1 4.7 %collective-permute-start.5 = (f32[64,128]{1,0:T(8,128)}, f32[64,128]{1,0:T(8,128)}, u32[]{:S(2)}, u32[]{:S(2)}) collective-permute-start(f32[64,128]{1,0:T(8,128)} %get-tuple-element.70), channel_id=1, source_target_pairs={{0,120},{8,0},{16,8},{24,16},{32,24},{40,32},{48,40},{56,48},{64,5... | collective-permute-start | bytes 98312 | tf_op jit(solution)/shard_map/ppermute | solution.py:458
  127.8 6.9 %collect_into.3.base_ref = f32[256,768]{1,0:T(8,128)} custom-call(s32[16,128]{1,0:T(8,128)} %get-tuple-element.59.index_ref.refs_11_, f32[2048,128]{1,0:T(8,128)} %bitcast.15.got_any.got_ref, f32[256,768]{1,0:T(8,128)} %get-tuple-element.75.base_ref), custom_call_target="tpu_custom_call" | custom-call | flops 1000000000 | bytes 10000000 | tf_op jit(solution)/shard_map/collect_into/pallas_call | solution.py:564
  136.2 3.0 %collective-permute-start.7 = (f32[80,128]{1,0:T(8,128)}, f32[80,128]{1,0:T(8,128)}, u32[]{:S(2)}, u32[]{:S(2)}) collective-permute-start(f32[80,128]{1,0:T(8,128)} %get-tuple-element.74), channel_id=1, source_target_pairs={{0,7},{1,0},{2,1},{3,2},{4,3},{5,4},{6,5},{7,6},{8,15},{9,8},{10,9... | collective-permute-start | bytes 122888 | tf_op jit(solution)/shard_map/ppermute | solution.py:458
  139.2 6.9 %collect_own.3.refs_7_ = f32[256,768]{1,0:T(8,128)} custom-call(s32[16,128]{1,0:T(8,128)} %get-tuple-element.58.index_ref.refs_13_, f32[2048,128]{1,0:T(8,128)} %bitcast.15.got_any.got_ref, f32[256,768]{1,0:T(8,128)} %collect_into.3.base_ref), custom_call_target="tpu_custom_call" | custom-call | flops 1000000000 | bytes 10000000 | tf_op jit(solution)/shard_map/collect_own/pallas_call | solution.py:564
  146.1 5.0 %sweep_last.1 = (f32[256,768]{1,0:T(8,128)}, f32[1024,32]{1,0:T(8,128)}) custom-call(s32[4]{0:T(128)} %pad_add_fusion.refs_0_, f32[256,128]{1,0:T(8,128)} %get-tuple-element.63.phi_ref.refs_1_, f32[256,128]{1,0:T(8,128)} %get-tuple-element.68.refs_2_, f32[64,128]{1,0:T(8,128)} %collective-permute-done.4.before_ref.refs_3_, ...), custom_call_target="tpu_custom_call" | custom-call | tf_op jit(solution)/shard_map/sweep_last/pallas_call | solution.py:593
  (17 shorter events, 6.5 us)
Async XLA Ops:
  2.7 21.2 %all-to-all-start = ((f32[128,1,128]{2,1,0:T(1,128)}), f32[128,1,128]{2,1,0:T(1,128)}, u32[]{:S(2)}, u32[]{:S(2)}) async-start(f32[128,1,128]{2,1,0:T(1,128)} %bitcast.20), calls=%async_computation | async-start | bytes 131072 | tf_op jit(solution)/shard_map/all_to_all | solution.py:453
  29.2 24.6 %all-to-all-start.1 = ((f32[128,16,128]{2,1,0:T(8,128)}), f32[128,16,128]{2,1,0:T(8,128)}, u32[]{:S(2)}, u32[]{:S(2)}) async-start(f32[128,16,128]{2,1,0:T(8,128)} %bitcast.18), calls=%async_computation.1 | async-start | bytes 2097152 | tf_op jit(solution)/shard_map/all_to_all | solution.py:453
  58.9 12.4 %collective-permute-start = (f32[64,128]{1,0:T(8,128)}, f32[64,128]{1,0:T(8,128)}, u32[]{:S(2)}, u32[]{:S(2)}) collective-permute-start(f32[64,128]{1,0:T(8,128)} %get-tuple-element.52), channel_id=1, source_target_pairs={{0,8},{8,16},{16,24},{24,32},{32,40},{40,48},{48,56},{56,64},{64,7... | collective-permute-start | bytes 98312 | tf_op jit(solution)/shard_map/ppermute | solution.py:458
  59.6 11.6 %collective-permute-start.1 = (f32[64,128]{1,0:T(8,128)}, f32[64,128]{1,0:T(8,128)}, u32[]{:S(2)}, u32[]{:S(2)}) collective-permute-start(f32[64,128]{1,0:T(8,128)} %get-tuple-element.53), channel_id=1, source_target_pairs={{0,120},{8,0},{16,8},{24,16},{32,24},{40,32},{48,40},{56,48},{64,5... | collective-permute-start | bytes 98312 | tf_op jit(solution)/shard_map/ppermute | solution.py:458
  72.7 9.9 %collective-permute-start.2 = (f32[80,128]{1,0:T(8,128)}, f32[80,128]{1,0:T(8,128)}, u32[]{:S(2)}, u32[]{:S(2)}) collective-permute-start(f32[80,128]{1,0:T(8,128)} %get-tuple-element.56), channel_id=1, source_target_pairs={{0,1},{1,2},{2,3},{3,4},{4,5},{5,6},{6,7},{7,0},{8,9},{9,10},{10,1... | collective-permute-start | bytes 122888 | tf_op jit(solution)/shard_map/ppermute | solution.py:458
  72.7 9.9 %collective-permute-start.3 = (f32[80,128]{1,0:T(8,128)}, f32[80,128]{1,0:T(8,128)}, u32[]{:S(2)}, u32[]{:S(2)}) collective-permute-start(f32[80,128]{1,0:T(8,128)} %get-tuple-element.57), channel_id=1, source_target_pairs={{0,7},{1,0},{2,1},{3,2},{4,3},{5,4},{6,5},{7,6},{8,15},{9,8},{10,9... | collective-permute-start | bytes 122888 | tf_op jit(solution)/shard_map/ppermute | solution.py:458
  92.7 24.6 %all-to-all-start.2 = ((f32[128,16,128]{2,1,0:T(8,128)}), f32[128,16,128]{2,1,0:T(8,128)}, u32[]{:S(2)}, u32[]{:S(2)}) async-start(f32[128,16,128]{2,1,0:T(8,128)} %bitcast.19), calls=%async_computation.2 | async-start | bytes 2097152 | tf_op jit(solution)/shard_map/all_to_all | solution.py:453
  122.4 12.4 %collective-permute-start.4 = (f32[64,128]{1,0:T(8,128)}, f32[64,128]{1,0:T(8,128)}, u32[]{:S(2)}, u32[]{:S(2)}) collective-permute-start(f32[64,128]{1,0:T(8,128)} %get-tuple-element.69), channel_id=1, source_target_pairs={{0,8},{8,16},{16,24},{24,32},{32,40},{40,48},{48,56},{56,64},{64,7... | collective-permute-start | bytes 98312 | tf_op jit(solution)/shard_map/ppermute | solution.py:458
  123.1 11.6 %collective-permute-start.5 = (f32[64,128]{1,0:T(8,128)}, f32[64,128]{1,0:T(8,128)}, u32[]{:S(2)}, u32[]{:S(2)}) collective-permute-start(f32[64,128]{1,0:T(8,128)} %get-tuple-element.70), channel_id=1, source_target_pairs={{0,120},{8,0},{16,8},{24,16},{32,24},{40,32},{48,40},{56,48},{64,5... | collective-permute-start | bytes 98312 | tf_op jit(solution)/shard_map/ppermute | solution.py:458
  136.2 9.9 %collective-permute-start.6 = (f32[80,128]{1,0:T(8,128)}, f32[80,128]{1,0:T(8,128)}, u32[]{:S(2)}, u32[]{:S(2)}) collective-permute-start(f32[80,128]{1,0:T(8,128)} %get-tuple-element.73), channel_id=1, source_target_pairs={{0,1},{1,2},{2,3},{3,4},{4,5},{5,6},{6,7},{7,0},{8,9},{9,10},{10,1... | collective-permute-start | bytes 122888 | tf_op jit(solution)/shard_map/ppermute | solution.py:458
  136.2 9.9 %collective-permute-start.7 = (f32[80,128]{1,0:T(8,128)}, f32[80,128]{1,0:T(8,128)}, u32[]{:S(2)}, u32[]{:S(2)}) collective-permute-start(f32[80,128]{1,0:T(8,128)} %get-tuple-element.74), channel_id=1, source_target_pairs={{0,7},{1,0},{2,1},{3,2},{4,3},{5,4},{6,5},{7,6},{8,15},{9,8},{10,9... | collective-permute-start | bytes 122888 | tf_op jit(solution)/shard_map/ppermute | solution.py:458

commit v3 on v2

--- a/solution.py
+++ b/solution.py
@@ -17,6 +17,7 @@
 CAP = 16
 TILE = 32
 HALO = 4
+CHUNKS = 4
 TILES = 8
 F32 = jnp.float32
 BF16 = jnp.bfloat16
@@ -39,6 +40,11 @@
 
 def flag(condition):
     return condition.astype(F32).astype(BF16)
+
+
+def marks(row, count):
+    places = iota((count, row.shape[1]), 0).astype(F32).astype(BF16)
+    return jnp.where(row.astype(F32).astype(BF16) == places, jnp.ones((), BF16), jnp.zeros((), BF16))
 
 
 def regroup(number):
@@ -106,33 +112,48 @@
     return copies
 
 
-def gather_rows(rows_ref, slots, scale_ref, out_ref, offset, stride):
+def start_copies(pairs, sem):
+    copies = [pltpu.make_async_copy(source, target, sem.at[i]) for i, (source, target) in enumerate(pairs)]
+    for copy in copies:
+        copy.start()
+    return copies
+
+
+def gather_rows(rows_ref, sides, out_ref, target_of, sem):
     low = low_half(1)
-
-    def body(i, carry):
-        for u in range(2):
-            d = 2 * i + u
+    copies = []
+    for chunk in range(CHUNKS):
+        count = DEVS // CHUNKS
+
+        def body(i, carry, chunk=chunk, count=count):
+            d = count * chunk + i
             scale_base = pl.multiple_of(d * 8, 8)
-            out_base = pl.multiple_of(d * stride, 8)
-            for p in range(8):
-                a = slots[p][0, d]
-                b = slots[p + 8][0, d]
-                row = jnp.where(low, rows_ref[pl.ds(a, 1), :], rows_ref[pl.ds(b, 1), :])
-                out_ref[pl.ds(out_base + (offset + p), 1), :] = row * scale_ref[pl.ds(scale_base + p, 1), :]
-        return carry
-
-    lax.fori_loop(0, DEVS // 2, body, 0)
+            for slots, scale_ref, first in sides:
+                for p in range(8):
+                    a = slots[p][0, d]
+                    b = slots[p + 8][0, d]
+                    row = jnp.where(low, rows_ref[pl.ds(a, 1), :], rows_ref[pl.ds(b, 1), :])
+                    out_ref[d, first + p : first + p + 1, :] = row * scale_ref[pl.ds(scale_base + p, 1), :]
+            return carry
+
+        lax.fori_loop(0, count, body, 0, unroll=2)
+        mine = pl.ds(count * chunk, count)
+        copy = pltpu.make_async_copy(out_ref.at[mine], target_of(mine), sem.at[chunk])
+        copy.start()
+        copies.append(copy)
+    return copies
 
 
 def gather_kernel(incoming, *refs):
     if incoming:
-        table_ref, volt_ref, sent_ref, out_ref = refs[:4]
+        table_ref, volt_any, _, out_any = refs[:4]
         refs = refs[4:]
     else:
-        table_ref, volt_ref, out_ref = refs[:3]
+        table_ref, volt_any, out_any = refs[:3]
         refs = refs[3:]
-    index_ref, number_ref, conduct_ref, scale_ref, rows_ref, scratch = refs[:6]
-    slots, sem = refs[6:22], refs[22]
+    index_ref, number_ref, conduct_ref, scale_any, rows_ref, scratch, volt_ref, out_ref, scale_ref = refs[:9]
+    slots, sem, data_sem, out_sem = refs[9:25], refs[25], refs[26], refs[27]
+    (volt_copy,) = start_copies([(volt_any, volt_ref)], data_sem)
     first = 0 if incoming else 32
     table = table_ref[...]
     numbers = 64.0 * table + pltpu.roll(table, 112, 1)
@@ -148,16 +169,16 @@
     scale = jnp.dot(table.astype(BF16), spread, preferred_element_type=F32)
     for p in range(8):
         scale_ref[pl.ds(p, DEVS, stride=8), :] = scale[:, 128 * p : 128 * p + 128]
+    scale_copy = pltpu.make_async_copy(scale_ref, scale_any, data_sem.at[1])
+    scale_copy.start()
+    volt_copy.wait()
     doubled(volt_ref[...], rows_ref)
-    if incoming:
-        for d in range(DEVS):
-            out_ref[16 * d : 16 * d + 8, :] = sent_ref[8 * d : 8 * d + 8, :]
     for copy in copies:
         copy.wait()
-    if incoming:
-        gather_rows(rows_ref, slots, scale_ref, out_ref, 8, 16)
-    else:
-        gather_rows(rows_ref, slots, scale_ref, out_ref, 0, 8)
+    at = pl.ds(8 if incoming else 0, 8)
+    done = gather_rows(rows_ref, ((slots, scale_ref, 0),), out_ref, lambda mine: out_any.at[mine, at], out_sem)
+    for copy in (scale_copy, *done):
+        copy.wait()
 
 
 def expander(rows, j):
@@ -183,7 +204,6 @@
     place_ref,
     found_ref,
 ):
-    cell = iota((CELLS, 128), 0)
     kind = iota((16, 128), 0)
     place_ref[...] = jnp.zeros_like(place_ref)
     place_ref[0:PER, :] = grid_row(point_ref[...]).astype(F32)
@@ -193,7 +213,7 @@
     for side, (index_ref, conduct_ref) in enumerate(((into_ref, into_conduct_ref), (own_ref, own_conduct_ref))):
         for s in range(16):
             number = index_ref[s : s + 1, :]
-            hit = flag((number & 255) == cell)
+            hit = marks(number & 255, CELLS)
             here = (number >> 8) == kind
             first, rest = split2(conduct_ref[s : s + 1, :])
             second, third = split2(rest)
@@ -229,10 +249,10 @@
 
 
 def deposited(total, row, column, mean):
-    hit = flag(row == iota((CELLS, CELLS), 0))
-    here = column == iota((128, CELLS), 0)
-    spread = jnp.concatenate([jnp.where(here, x, 0.0) for x in split2(mean)], axis=0)
-    return total + lax.dot_general(hit, spread.astype(BF16), NT, preferred_element_type=F32)
+    hit = marks(row, CELLS)
+    here = marks(column, 128)
+    spread = jnp.concatenate([here * x.astype(BF16) for x in split2(mean)], axis=0)
+    return total + lax.dot_general(hit, spread, NT, preferred_element_type=F32)
 
 
 def base_kernel(volt_ref, recov_ref, id_ref, degree_ref, point_ref, template_ref, out_ref, deposit_ref, volt_bf, held, sem):
@@ -262,16 +282,14 @@
     means = jnp.zeros((16, CELLS), F32)
     for j in range(PER // 2):
         weights = jnp.where(expander(16, j), 1.0 / BLOCK, 0.0).astype(BF16)
-        for part in split2(out_ref[:, 128 * j : 128 * j + 128]):
-            means = means + lax.dot_general(weights, part.astype(BF16), NT, preferred_element_type=F32)
+        parts = jnp.concatenate(split2(out_ref[:, 128 * j : 128 * j + 128]), axis=1).astype(BF16)
+        weights = jnp.concatenate([weights, weights], axis=1)
+        means = means + lax.dot_general(weights, parts, NT, preferred_element_type=F32)
     total = jnp.zeros((CELLS, 256), F32)
     for k in range(PER):
         point = point_ref[k : k + 1, :]
         total = deposited(total, grid_row(point), point & 127, means[k : k + 1, :])
     deposit_ref[...] = total[:, 0:128] + total[:, 128:256]
-
-
-CHUNKS = 4
 
 
 def deposit_kernel(
@@ -284,15 +302,16 @@
     ]
     for copy in copies:
         copy.start()
-    lane = iota((16, 128), 1)
-    weights = jnp.where(iota((16, 128), 0) == (lane >> 6), 1.0 / BLOCK, 0.0).astype(BF16)
+    half = (iota((16, 256), 1) >> 6) & 1
+    weights = jnp.where(iota((16, 256), 0) == half, 1.0 / BLOCK, 0.0).astype(BF16)
     total = jnp.zeros((CELLS, 256), F32)
     for r in range(16):
         if r % (16 // CHUNKS) == 0:
             copies[r // (16 // CHUNKS)].wait()
-        mean = jnp.zeros((16, 128), F32)
-        for part in split2(got_ref[128 * r : 128 * r + 128, :]):
-            mean = mean + lax.dot_general(weights, part.astype(BF16), NT, preferred_element_type=F32)
+        if r % 2 == 0:
+            parts = jnp.concatenate(split2(got_ref[128 * r : 128 * r + 256, :]), axis=1).astype(BF16)
+            pair = lax.dot_general(weights, parts, NT, preferred_element_type=F32)
+        mean = pair[:, 128 * (r % 2) : 128 * (r % 2) + 128]
 
         def both(at):
             return jnp.concatenate([slot_ref[at + r : at + r + 1, :], slot_ref[at + 16 + r : at + 17 + r, :]], axis=1)
@@ -308,34 +327,52 @@
         y_high_ref[across : across + TILE, :] = array[TILE * (TILES - 1) :, :]
 
 
-def collect_kernel(offset, index_ref, got_ref, base_ref, out_ref, *scratch):
-    lower, upper, slots, sem = scratch[0:2], scratch[2:4], scratch[4:20], scratch[20]
-    copies = start_slots(index_ref, slots, sem)
-    for ref in (*lower, *upper):
+def collect_kernel(into_ref, own_ref, got_any, base_any, out_any, *scratch):
+    sums, into_slots, own_slots = scratch[0:8], scratch[8:24], scratch[24:40]
+    got_ref, base_ref, into_sem, own_sem, data_sem, out_sem = scratch[40:]
+    copies = start_slots(into_ref, into_slots, into_sem) + start_slots(own_ref, own_slots, own_sem)
+    count = DEVS // CHUNKS
+    pieces = [pl.ds(16 * count * i, 16 * count) for i in range(CHUNKS)]
+    got_copies = start_copies(
+        [(got_any.at[piece], got_ref.at[piece]) for piece in pieces] + [(base_any, base_ref)], data_sem
+    )
+    for ref in sums:
         ref[...] = jnp.zeros_like(ref)
     for copy in copies:
         copy.wait()
-
-    def body(i, carry):
-        for u in range(2):
-            d = 2 * i + u
+    for chunk in range(CHUNKS):
+        got_copies[chunk].wait()
+
+        def body(i, carry, chunk=chunk):
+            d = count * chunk + i
             base = pl.multiple_of(d * 16, 16)
             for p in range(8):
-                row = got_ref[pl.ds(base + (offset + p), 1), :]
-                lower[p % 2][pl.ds(slots[p][0, d], 1), :] += row
-                upper[p % 2][pl.ds(slots[p + 8][0, d], 1), :] += row
-        return carry
-
-    lax.fori_loop(0, DEVS // 2, body, 0)
+                for side, slots in ((0, into_slots), (1, own_slots)):
+                    row = got_ref[pl.ds(base + (8 * side + p), 1), :]
+                    for half in (0, 1):
+                        ref = sums[4 * (p % 2) + 2 * side + half]
+                        ref[pl.ds(slots[p + 8 * half][0, d], 1), :] += row
+            return carry
+
+        lax.fori_loop(0, count, body, 0, unroll=2)
+    got_copies[CHUNKS].wait()
     low = low_half(CELLS)
+    out_copies = []
     for j in range(PER // 2):
-        sums = []
+        both = []
         for k in (2 * j, 2 * j + 1):
             cut = slice(CELLS * k, CELLS * k + CELLS)
-            both = jnp.where(low, lower[0][cut, :] + lower[1][cut, :], upper[0][cut, :] + upper[1][cut, :])
-            sums.append(both + pltpu.roll(both, 64, 1))
+            halves = [sum(ref[cut, :] for ref in sums[half::2]) for half in (0, 1)]
+            rows = jnp.where(low, *halves)
+            both.append(rows + pltpu.roll(rows, 64, 1))
         cut = slice(128 * j, 128 * j + 128)
-        out_ref[:, cut] = base_ref[:, cut] - jnp.where(low, sums[0], sums[1])
+        base_ref[:, cut] = base_ref[:, cut] - jnp.where(low, both[0], both[1])
+        cut = pl.ds(128 * j, 128)
+        copy = pltpu.make_async_copy(base_ref.at[:, cut], out_any.at[:, cut], out_sem.at[j])
+        copy.start()
+        out_copies.append(copy)
+    for copy in out_copies:
+        copy.wait()
 
 
 def frame_kernel(before_ref, after_ref, y_low_ref, y_high_ref, low_ref, high_ref):
@@ -351,14 +388,29 @@
 
 def sweep_kernel(last, *refs):
     place_ref, phi_ref, deposit_ref, x_before_ref, x_after_ref, y_before_ref, y_after_ref = refs[:7]
-    current_ref, volt_ref, point_ref = refs[7:10]
+    current_any, volt_any, point_ref = refs[7:10]
     if last:
-        volt_out, phi_out, wide_phi, wide_deposit, found_ref = refs[10:]
+        volt_out, phi_out, wide_phi, wide_deposit, found_ref, current_ref, volt_ref, phi_held = refs[10:18]
+        data_sem, out_sem = refs[18:]
+        fetched = start_copies([(current_any, current_ref), (volt_any, volt_ref)], data_sem)
     else:
-        recov_ref, into_ref, into_scale_ref, own_ref, own_scale_ref = refs[10:15]
-        volt_out, phi_out, recov_out, send_out, wide_phi, wide_deposit, found_ref, rows_ref = refs[15:23]
-        own_slots, into_slots, own_sem, into_sem = refs[23:39], refs[39:55], refs[55], refs[56]
+        recov_any, into_ref, into_scale_any, own_ref, own_scale_any = refs[10:15]
+        volt_out, phi_out, recov_out, send_any = refs[15:19]
+        wide_phi, wide_deposit, found_ref, current_ref, volt_ref, recov_ref = refs[19:25]
+        own_scale_ref, into_scale_ref, send_ref, rows_ref = refs[25:29]
+        own_slots, into_slots = refs[29:45], refs[45:61]
+        own_sem, into_sem, data_sem, out_sem = refs[61:]
         copies = start_slots(own_ref, own_slots, own_sem) + start_slots(into_ref, into_slots, into_sem)
+        fetched = start_copies(
+            [
+                (current_any, current_ref),
+                (volt_any, volt_ref),
+                (recov_any, recov_ref),
+                (own_scale_any, own_scale_ref),
+                (into_scale_any, into_scale_ref),
+            ],
+            data_sem,
+        )
     end = LEAD + ROWS
     high = LEAD + HALO + TILE
     for wide, array, at, across in ((wide_phi, phi_ref, 0, 0), (wide_deposit, deposit_ref, HALO, TILE)):
@@ -408,41 +460,56 @@
         for t in range(TILES):
             for y in range(4):
                 turned = tiles[t] if y == 0 else pltpu.roll(tiles[t], 128 - 32 * y, 1)
-                phi_out[pl.ds(4 * t + y, TILE, stride=TILE), :] = turned[:, 0:TILE]
+                phi_held[pl.ds(4 * t + y, TILE, stride=TILE), :] = turned[:, 0:TILE]
+        phi_copy = pltpu.make_async_copy(phi_held, phi_out, out_sem.at[PER // 2])
+        phi_copy.start()
     else:
         for t in range(TILES):
             phi_out[TILE * t : TILE * t + TILE, :] = tiles[t]
     turned = jnp.concatenate(tiles, axis=0).T
     pieces = jnp.concatenate(split2(turned), axis=0).astype(BF16)
-    row_of = iota((CELLS, CELLS), 0)
     column_of = iota((128, CELLS), 0)
     found_ref[...] = jnp.zeros_like(found_ref)
     for k in range(PER):
         point = point_ref[k : k + 1, :]
-        hit = flag(grid_row(point) == row_of)
+        hit = marks(grid_row(point), CELLS)
         found = jnp.dot(pieces, hit, preferred_element_type=F32)
         found = found[0:128, :] + found[128:256, :]
         here = (point & 127) == column_of
         found_ref[k : k + 1, :] = jnp.sum(jnp.where(here, found, 0.0), axis=0, keepdims=True)
     found = jnp.concatenate(split2(found_ref[...]), axis=0).astype(BF16)
     low = low_half(CELLS)
+    for copy in fetched:
+        copy.wait()
+    done = []
     for j in range(PER // 2):
         cut = slice(128 * j, 128 * j + 128)
         at_node = lax.dot_general(found, flag(expander(32, j)), TN, preferred_element_type=F32)
         volt = volt_ref[:, cut]
         fresh = volt - 0.05 * (current_ref[:, cut] + at_node)
-        volt_out[:, cut] = fresh
-        if not last:
+        volt_ref[:, cut] = fresh
+        if last:
+            part = pl.ds(128 * j, 128)
+            done.append(pltpu.make_async_copy(volt_ref.at[:, part], volt_out.at[:, part], out_sem.at[j]))
+            done[-1].start()
+        else:
             recov = recov_ref[:, cut]
-            recov_out[:, cut] = recov + 0.05 * 0.08 * (volt + 0.7 - 0.8 * recov)
+            recov_ref[:, cut] = recov + 0.05 * 0.08 * (volt + 0.7 - 0.8 * recov)
             turned = pltpu.roll(fresh, 64, 1)
             rows_ref[512 * j : 512 * j + 256, :] = jnp.where(low, fresh, turned)
             rows_ref[512 * j + 256 : 512 * j + 512, :] = jnp.where(low, turned, fresh)
-    if not last:
+    if last:
+        done.append(phi_copy)
+    else:
+        for i, (held, target) in enumerate(((volt_ref, volt_out), (recov_ref, recov_out))):
+            done.append(pltpu.make_async_copy(held, target, out_sem.at[CHUNKS + i]))
+            done[-1].start()
         for copy in copies:
             copy.wait()
-        gather_rows(rows_ref, own_slots, own_scale_ref, send_out, 0, 16)
-        gather_rows(rows_ref, into_slots, into_scale_ref, send_out, 8, 16)
+        sides = ((own_slots, own_scale_ref, 0), (into_slots, into_scale_ref, 8))
+        done += gather_rows(rows_ref, sides, send_ref, lambda mine: send_any.at[mine], out_sem)
+    for copy in done:
+        copy.wait()
 
 
 def shaped(*shape, dtype=F32):
@@ -490,25 +557,40 @@
     slot_sem = pltpu.SemaphoreType.DMA((CAP,))
     small = shaped(16, 128, dtype=I32)
     tables_out = (small, small, shaped(16, 128), shaped(DEVS * 8, 128))
-    gather_scratch = [rows_scratch, pltpu.VMEM((128, 128), F32)] + slot_scratch + [slot_sem]
-    sent, own, own_number, own_conduct, own_scale = pl.pallas_call(
+    plane = pltpu.VMEM((CELLS, NODES), F32)
+    scale_scratch = pltpu.VMEM((DEVS * 8, 128), F32)
+    gather_scratch = [
+        rows_scratch,
+        pltpu.VMEM((128, 128), F32),
+        plane,
+        pltpu.VMEM((DEVS, 8, 128), F32),
+        scale_scratch,
+        *slot_scratch,
+        slot_sem,
+        pltpu.SemaphoreType.DMA((2,)),
+        pltpu.SemaphoreType.DMA((CHUNKS,)),
+    ]
+    anywhere = pl.BlockSpec(memory_space=pl.ANY)
+    message = shaped(DEVS, 16, 128)
+    outgoing, own, own_number, own_conduct, own_scale = pl.pallas_call(
         functools.partial(gather_kernel, False),
-        out_shape=(shaped(DEVS * 8, 128),) + tables_out,
-        in_specs=[VMEM] * 2,
-        out_specs=(VMEM,) * 5,
+        out_shape=(message,) + tables_out,
+        in_specs=[VMEM, anywhere],
+        out_specs=(anywhere,) + (VMEM,) * 3 + (anywhere,),
         scratch_shapes=gather_scratch,
         compiler_params=PARAMS,
         name="gather_source",
     )(table, potential)
     outgoing, into, into_number, into_conduct, into_scale = pl.pallas_call(
         functools.partial(gather_kernel, True),
-        out_shape=(shaped(DEVS * 16, 128),) + tables_out,
-        in_specs=[VMEM] * 3,
-        out_specs=(VMEM,) * 5,
+        out_shape=(message,) + tables_out,
+        in_specs=[VMEM, anywhere, anywhere],
+        out_specs=(anywhere,) + (VMEM,) * 3 + (anywhere,),
         scratch_shapes=gather_scratch,
+        input_output_aliases={2: 0},
         compiler_params=PARAMS,
         name="gather_target",
-    )(got_table, potential, sent)
+    )(got_table, potential, outgoing)
     points = memb_point.reshape(CELLS, PER).T
     degree, id_wide, phi, slot_points = pl.pallas_call(
         prepare_kernel,
@@ -532,10 +614,9 @@
     place = place.astype(I32)
     volt = potential
     recov = gating
-    anywhere = pl.BlockSpec(memory_space=pl.ANY)
     for step in range(STEPS):
         last = step == STEPS - 1
-        got = exchange(outgoing.reshape(DEVS, 16, 128)).reshape(DEVS * 16, 128)
+        got = exchange(outgoing).reshape(DEVS * 16, 128)
         base, deposit_base = pl.pallas_call(
             base_kernel,
             out_shape=(shaped(CELLS, NODES), shaped(TILE * TILES, 128)),
@@ -560,21 +641,8 @@
             name="deposit",
         )(got, deposit_base, slot_points, phi)
 
-        def collect(offset, index, start):
-            return pl.pallas_call(
-                functools.partial(collect_kernel, offset),
-                out_shape=shaped(CELLS, NODES),
-                in_specs=[VMEM] * 3,
-                out_specs=VMEM,
-                scratch_shapes=[rows_scratch] * 4 + slot_scratch + [slot_sem],
-                cost_estimate=pl.CostEstimate(flops=1_000_000_000, bytes_accessed=10_000_000, transcendentals=0),
-                compiler_params=PARAMS,
-                name="collect_own" if offset else "collect_into",
-            )(index, got, start)
-
         x_before = shift(x_high, "tx", 1)
         x_after = shift(x_low, "tx", -1)
-        current = collect(0, into, base)
         y_low, y_high = pl.pallas_call(
             frame_kernel,
             out_shape=(shaped(80, 128),) * 2,
@@ -585,32 +653,61 @@
         )(x_before, x_after, y_low, y_high)
         y_before = shift(y_high, "ty", 1)
         y_after = shift(y_low, "ty", -1)
-        current = collect(8, own, current)
+        current = pl.pallas_call(
+            collect_kernel,
+            out_shape=shaped(CELLS, NODES),
+            in_specs=[VMEM] * 2 + [anywhere] * 2,
+            out_specs=anywhere,
+            scratch_shapes=[
+                *[rows_scratch] * 8,
+                *slot_scratch * 2,
+                pltpu.VMEM((DEVS * 16, 128), F32),
+                plane,
+                slot_sem,
+                slot_sem,
+                pltpu.SemaphoreType.DMA((CHUNKS + 1,)),
+                pltpu.SemaphoreType.DMA((PER // 2,)),
+            ],
+            cost_estimate=pl.CostEstimate(flops=1_000_000_000, bytes_accessed=10_000_000, transcendentals=0),
+            compiler_params=PARAMS,
+            name="collect",
+        )(into, own, got, base)
         operands = [place, phi, deposit, x_before, x_after, y_before, y_after, current, volt, points]
-        specs = [SMEM] + [VMEM] * 9
+        specs = [SMEM] + [VMEM] * 6 + [anywhere] * 2 + [VMEM]
         wide = [pltpu.VMEM((TILES + 2, LEAD + ROWS + 8, 128), F32)] * 2 + [pltpu.VMEM((16, CELLS), F32)]
         if last:
             volt, phi = pl.pallas_call(
                 functools.partial(sweep_kernel, True),
                 out_shape=(shaped(CELLS, NODES), shaped(TILE * TILE, TILE)),
                 in_specs=specs,
-                out_specs=(VMEM,) * 2,
-                scratch_shapes=wide,
+                out_specs=(anywhere,) * 2,
+                scratch_shapes=wide
+                + [plane] * 2
+                + [
+                    pltpu.VMEM((TILE * TILE, TILE), F32),
+                    pltpu.SemaphoreType.DMA((2,)),
+                    pltpu.SemaphoreType.DMA((PER // 2 + 1,)),
+                ],
                 compiler_params=PARAMS,
                 name="sweep_last",
             )(*operands)
         else:
             volt, phi, recov, outgoing = pl.pallas_call(
                 functools.partial(sweep_kernel, False),
-                out_shape=(
-                    shaped(CELLS, NODES),
-                    shaped(TILE * TILES, 128),
-                    shaped(CELLS, NODES),
-                    shaped(DEVS * 16, 128),
-                ),
-                in_specs=specs + [VMEM] * 5,
-                out_specs=(VMEM,) * 4,
-                scratch_shapes=wide + [rows_scratch] + slot_scratch * 2 + [slot_sem] * 2,
+                out_shape=(shaped(CELLS, NODES), shaped(TILE * TILES, 128), shaped(CELLS, NODES), message),
+                in_specs=specs + [anywhere, VMEM, anywhere, VMEM, anywhere],
+                out_specs=(anywhere, VMEM, anywhere, anywhere),
+                scratch_shapes=wide
+                + [plane] * 3
+                + [scale_scratch] * 2
+                + [pltpu.VMEM((DEVS, 16, 128), F32), rows_scratch]
+                + slot_scratch * 2
+                + [
+                    slot_sem,
+                    slot_sem,
+                    pltpu.SemaphoreType.DMA((5,)),
+                    pltpu.SemaphoreType.DMA((CHUNKS + 2,)),
+                ],
                 compiler_params=PARAMS,
                 name="sweep",
             )(*operands, recov, into, into_scale, own, own_scale)

time: 152 us -> 145 us (0.954)
  the two profiles are of different devices: /device:TPU:0 before, /device:TPU:30 now
where the time goes in v3:
time: 145 us; the launch traced here: 144 us
  Pallas kernels  77.3 us (53%)
  starting transfers between devices  41.1 us (28%)
  waiting for transfers between devices  22.7 us (16%)
  local copies, waits for them, and re-layouts  1.53 us (1%)
    all_to_all x3, starting transfers between devices, exchange(): return lax.all_to_all(x, AXES, split_axis=0, concat_axis=0, tiled=True)  26.9 us
    pallas_call x2, Pallas kernels, on_device(): pl.pallas_call(base_kernel, out_shape=(shaped(CELLS, NODES), shaped(TILE...  19.1 us
    pallas_call x2, Pallas kernels, on_device(): pl.pallas_call(collect_kernel, out_shape=shaped(CELLS, NODES), in_specs=[...  15.3 us
    ppermute x8, waiting for transfers between devices, shift(): return lax.ppermute(x, axis, [(i, (i + by) % size) for i in range(size)])  14.5 us
    ppermute x8, starting transfers between devices, shift(): return lax.ppermute(x, axis, [(i, (i + by) % size) for i in range(size)])  14.3 us
    pallas_call x2, Pallas kernels, on_device(): pl.pallas_call(deposit_kernel, out_shape=(shaped(TILE * TILES, 128),) + (...  10.4 us
    pallas_call x1, Pallas kernels, on_device(): pl.pallas_call(functools.partial(sweep_kernel, False), out_shape=(shaped(...  9.21 us
    all_to_all x3, waiting for transfers between devices, exchange(): return lax.all_to_all(x, AXES, split_axis=0, concat_axis=0, tiled=True)  8.17 us
  transfers between devices with their start and end apart: 11, of which 7 were waited for; matrix products, arithmetic and copies ran while one was open for 1% of the time, Pallas kernels for 30%

profile of v3, /device:TPU:30, one launch (start us, length us, event | category | flops | bytes accessed | tf_op | source)
XLA Modules:
  0.0 144.2 jit_solution(13187969281207743074)
XLA Ops:
  0.6 2.1 %setup.1.refs_0_ = f32[128,128]{1,0:T(8,128)} custom-call(s32[8,128]{1,0:T(8,128)} %bitcast.23, s32[8,128]{1,0:T(8,128)} %bitcast.24, s32[8,128]{1,0:T(8,128)} %bitcast.25, f32[8,128]{1,0:T(8,128)} %bitcast.26), custom_call_target="tpu_custom_call" | custom-call | tf_op jit(solution)/shard_map/setup/pallas_call | solution.py:541
  2.7 10.7 %all-to-all-start = ((f32[128,1,128]{2,1,0:T(1,128)}), f32[128,1,128]{2,1,0:T(1,128)}, u32[]{:S(2)}, u32[]{:S(2)}) async-start(f32[128,1,128]{2,1,0:T(1,128)} %bitcast.16), calls=%async_computation | async-start | bytes 131072 | tf_op jit(solution)/shard_map/all_to_all | solution.py:520
  13.4 5.4 %gather_source.1 = (f32[128,16,128]{2,1,0:T(8,128)}, s32[16,128]{1,0:T(8,128)}, s32[16,128]{1,0:T(8,128)}, f32[16,128]{1,0:T(8,128)}, f32[1024,128]{1,0:T(8,128)}) custom-call(f32[128,128]{1,0:T(8,128)} %setup.1.refs_0_, f32[256,768]{1,0:T(8,128)} %refs_8_.1), custom_call_target="tpu_custom_call" | custom-call | tf_op jit(solution)/shard_map/gather_source/pallas_call | solution.py:575
  19.7 5.4 %gather_target.1 = (f32[128,16,128]{2,1,0:T(8,128)}, s32[16,128]{1,0:T(8,128)}, s32[16,128]{1,0:T(8,128)}, f32[16,128]{1,0:T(8,128)}, f32[1024,128]{1,0:T(8,128)}) custom-call(f32[128,128]{1,0:T(8,128)} %bitcast.8.refs_0_, f32[256,768]{1,0:T(8,128)} %refs_8_.1, f32[128,16,128]{2,1,0:T(8,128)} %get-tuple-element.40.refs_2_), custom_call_target="tpu_custom_call", output_to_operand_aliasing={{0}: (2, {})} | custom-call | tf_op jit(solution)/shard_map/gather_target/pallas_call | solution.py:584
  25.0 9.4 %all-to-all-start.1 = ((f32[128,16,128]{2,1,0:T(8,128)}), f32[128,16,128]{2,1,0:T(8,128)}, u32[]{:S(2)}, u32[]{:S(2)}) async-start(f32[128,16,128]{2,1,0:T(8,128)} %get-tuple-element.46), calls=%async_computation.1 | async-start | bytes 2097152 | tf_op jit(solution)/shard_map/all_to_all | solution.py:520
  36.0 3.5 %prepare.1 = (f32[256,768]{1,0:T(8,128)}, f32[256,128]{1,0:T(8,128)}, f32[256,128]{1,0:T(8,128)}, s32[64,128]{1,0:T(8,128)}) custom-call(s32[16,128]{1,0:T(8,128)} %get-tuple-element.41.into_ref, f32[16,128]{1,0:T(8,128)} %get-tuple-element.42.into_conduct_ref, s32[16,128]{1,0:T(8,128)} %get-tuple-element.43.own_ref, ...), custom_call_target="tpu_custom_call" | custom-call | tf_op jit(solution)/shard_map/prepare/pallas_call | solution.py:595
  39.5 9.6 %base.2 = (f32[256,768]{1,0:T(8,128)}, f32[256,128]{1,0:T(8,128)}) custom-call(f32[256,768]{1,0:T(8,128)} %refs_8_.1, f32[256,768]{1,0:T(8,128)} %refs_10_.1, f32[256,128]{1,0:T(8,128)} %get-tuple-element.47.id_ref, f32[256,768]{1,0:T(8,128)} %get-tuple-element.48.degree_ref, s32[12,256]{1,0:T(8,128)} %bitcast.18, bf16[10,768,768]{2,1,0:T(8,128)(2,1)} %template_ref.3), custom_call_target="tpu_custom_call" | custom-call | flops 3000000000 | bytes 14000000 | tf_op jit(solution)/shard_map/base/pallas_call | solution.py:620
  50.2 5.2 %deposit.2 = (f32[256,128]{1,0:T(8,128)}, f32[64,128]{1,0:T(8,128)}, f32[64,128]{1,0:T(8,128)}, f32[64,128]{1,0:T(8,128)}, f32[64,128]{1,0:T(8,128)}) custom-call(f32[2048,128]{1,0:T(8,128)} %bitcast.12.got_any, f32[256,128]{1,0:T(8,128)} %get-tuple-element.49.base_ref, s32[64,128]{1,0:T(8,128)} %get-tuple-element.50.slot_ref, ...), custom_call_target="tpu_custom_call" | custom-call | tf_op jit(solution)/shard_map/deposit/pallas_call | solution.py:634
  55.4 4.2 %collective-permute-start = (f32[64,128]{1,0:T(8,128)}, f32[64,128]{1,0:T(8,128)}, u32[]{:S(2)}, u32[]{:S(2)}) collective-permute-start(f32[64,128]{1,0:T(8,128)} %get-tuple-element.52), channel_id=1, source_target_pairs={{0,8},{8,16},{16,24},{24,32},{32,40},{40,48},{48,56},{56,64},{64,7... | collective-permute-start | bytes 98312 | tf_op jit(solution)/shard_map/ppermute | solution.py:525
  61.5 5.6 %collective-permute-done.1.after_ref.refs_4_ = f32[64,128]{1,0:T(8,128)} collective-permute-done((f32[64,128]{1,0:T(8,128)}, f32[64,128]{1,0:T(8,128)}, u32[]{:S(2)}, u32[]{:S(2)}) %collective-permute-start.1) | collective-permute-done | bytes 32800 | tf_op jit(solution)/shard_map/ppermute | solution.py:525
  67.2 1.4 frame.2
  68.6 3.0 %collective-permute-start.3 = (f32[80,128]{1,0:T(8,128)}, f32[80,128]{1,0:T(8,128)}, u32[]{:S(2)}, u32[]{:S(2)}) collective-permute-start(f32[80,128]{1,0:T(8,128)} %get-tuple-element.57), channel_id=1, source_target_pairs={{0,7},{1,0},{2,1},{3,2},{4,3},{5,4},{6,5},{7,6},{8,15},{9,8},{10,9... | collective-permute-start | bytes 122888 | tf_op jit(solution)/shard_map/ppermute | solution.py:525
  71.6 7.6 %collect.2.refs_7_ = f32[256,768]{1,0:T(8,128)} custom-call(s32[16,128]{1,0:T(8,128)} %get-tuple-element.58.into_ref.refs_11_, s32[16,128]{1,0:T(8,128)} %get-tuple-element.59.own_ref.refs_13_, f32[2048,128]{1,0:T(8,128)} %bitcast.12.got_any, f32[256,768]{1,0:T(8,128)} %get-tuple-element.60.base_any), custom_call_target="tpu_custom_call" | custom-call | flops 1000000000 | bytes 10000000 | tf_op jit(solution)/shard_map/collect/pallas_call | solution.py:656
  79.2 9.2 %sweep.1 = (f32[256,768]{1,0:T(8,128)}, f32[256,128]{1,0:T(8,128)}, f32[256,768]{1,0:T(8,128)}, f32[128,16,128]{2,1,0:T(8,128)}) custom-call(s32[4]{0:T(128)} %pad_add_fusion.refs_0_, f32[256,128]{1,0:T(8,128)} %get-tuple-element.45.phi_ref.refs_1_, f32[256,128]{1,0:T(8,128)} %get-tuple-element.51.refs_2_, ...), custom_call_target="tpu_custom_call" | custom-call | tf_op jit(solution)/shard_map/sweep/pallas_call | solution.py:695
  88.5 6.8 %all-to-all-start.2 = ((f32[128,16,128]{2,1,0:T(8,128)}), f32[128,16,128]{2,1,0:T(8,128)}, u32[]{:S(2)}, u32[]{:S(2)}) async-start(f32[128,16,128]{2,1,0:T(8,128)} %get-tuple-element.64), calls=%async_computation.2 | async-start | bytes 2097152 | tf_op jit(solution)/shard_map/all_to_all | solution.py:520
  95.2 9.6 %base.3 = (f32[256,768]{1,0:T(8,128)}, f32[256,128]{1,0:T(8,128)}) custom-call(f32[256,768]{1,0:T(8,128)} %get-tuple-element.65.volt_ref.refs_8_, f32[256,768]{1,0:T(8,128)} %get-tuple-element.66.recov_ref, f32[256,128]{1,0:T(8,128)} %get-tuple-element.47.id_ref, f32[256,768]{1,0:T(8,128)} %get-tuple-element.48.degree_ref, s32[12,256]{1,0:T(8,128)} %bitcast.20, ...), custom_call_target="tpu_custom_call" | custom-call | flops 3000000000 | bytes 14000000 | tf_op jit(solution)/shard_map/base/pallas_call | solution.py:620
  104.8 6.2 %all-to-all-done.2 = f32[128,16,128]{2,1,0:T(8,128)} async-done(((f32[128,16,128]{2,1,0:T(8,128)}), f32[128,16,128]{2,1,0:T(8,128)}, u32[]{:S(2)}, u32[]{:S(2)}) %all-to-all-start.2) | async-done | bytes 1048608 | tf_op jit(solution)/shard_map/all_to_all | solution.py:520
  111.0 5.2 %deposit.3 = (f32[256,128]{1,0:T(8,128)}, f32[64,128]{1,0:T(8,128)}, f32[64,128]{1,0:T(8,128)}, f32[64,128]{1,0:T(8,128)}, f32[64,128]{1,0:T(8,128)}) custom-call(f32[2048,128]{1,0:T(8,128)} %bitcast.13.got_any, f32[256,128]{1,0:T(8,128)} %get-tuple-element.67.base_ref, s32[64,128]{1,0:T(8,128)} %get-tuple-element.50.slot_ref, ...), custom_call_target="tpu_custom_call" | custom-call | tf_op jit(solution)/shard_map/deposit/pallas_call | solution.py:634
  116.2 4.2 %collective-permute-start.4 = (f32[64,128]{1,0:T(8,128)}, f32[64,128]{1,0:T(8,128)}, u32[]{:S(2)}, u32[]{:S(2)}) collective-permute-start(f32[64,128]{1,0:T(8,128)} %get-tuple-element.69), channel_id=1, source_target_pairs={{0,8},{8,16},{16,24},{24,32},{32,40},{40,48},{48,56},{56,64},{64,7... | collective-permute-start | bytes 98312 | tf_op jit(solution)/shard_map/ppermute | solution.py:525
  120.4 1.9 %collective-permute-done.4.before_ref.refs_3_ = f32[64,128]{1,0:T(8,128)} collective-permute-done((f32[64,128]{1,0:T(8,128)}, f32[64,128]{1,0:T(8,128)}, u32[]{:S(2)}, u32[]{:S(2)}) %collective-permute-start.4) | collective-permute-done | bytes 32800 | tf_op jit(solution)/shard_map/ppermute | solution.py:525
  122.3 5.6 %collective-permute-done.5.after_ref.refs_4_ = f32[64,128]{1,0:T(8,128)} collective-permute-done((f32[64,128]{1,0:T(8,128)}, f32[64,128]{1,0:T(8,128)}, u32[]{:S(2)}, u32[]{:S(2)}) %collective-permute-start.5) | collective-permute-done | bytes 32800 | tf_op jit(solution)/shard_map/ppermute | solution.py:525
  129.4 3.0 %collective-permute-start.7 = (f32[80,128]{1,0:T(8,128)}, f32[80,128]{1,0:T(8,128)}, u32[]{:S(2)}, u32[]{:S(2)}) collective-permute-start(f32[80,128]{1,0:T(8,128)} %get-tuple-element.74), channel_id=1, source_target_pairs={{0,7},{1,0},{2,1},{3,2},{4,3},{5,4},{6,5},{7,6},{8,15},{9,8},{10,9... | collective-permute-start | bytes 122888 | tf_op jit(solution)/shard_map/ppermute | solution.py:525
  132.3 7.6 %collect.3.refs_7_ = f32[256,768]{1,0:T(8,128)} custom-call(s32[16,128]{1,0:T(8,128)} %get-tuple-element.58.into_ref.refs_11_, s32[16,128]{1,0:T(8,128)} %get-tuple-element.59.own_ref.refs_13_, f32[2048,128]{1,0:T(8,128)} %bitcast.13.got_any, f32[256,768]{1,0:T(8,128)} %get-tuple-element.75.base_any), custom_call_target="tpu_custom_call" | custom-call | flops 1000000000 | bytes 10000000 | tf_op jit(solution)/shard_map/collect/pallas_call | solution.py:656
  140.0 4.1 %sweep_last.1 = (f32[256,768]{1,0:T(8,128)}, f32[1024,32]{1,0:T(8,128)}) custom-call(s32[4]{0:T(128)} %pad_add_fusion.refs_0_, f32[256,128]{1,0:T(8,128)} %get-tuple-element.63.phi_ref.refs_1_, f32[256,128]{1,0:T(8,128)} %get-tuple-element.68.refs_2_, f32[64,128]{1,0:T(8,128)} %collective-permute-done.4.before_ref.refs_3_, ...), custom_call_target="tpu_custom_call" | custom-call | tf_op jit(solution)/shard_map/sweep_last/pallas_call | solution.py:679
  (15 shorter events, 6.9 us)
Async XLA Ops:
  2.7 16.9 %all-to-all-start = ((f32[128,1,128]{2,1,0:T(1,128)}), f32[128,1,128]{2,1,0:T(1,128)}, u32[]{:S(2)}, u32[]{:S(2)}) async-start(f32[128,1,128]{2,1,0:T(1,128)} %bitcast.16), calls=%async_computation | async-start | bytes 131072 | tf_op jit(solution)/shard_map/all_to_all | solution.py:520
  25.0 25.2 %all-to-all-start.1 = ((f32[128,16,128]{2,1,0:T(8,128)}), f32[128,16,128]{2,1,0:T(8,128)}, u32[]{:S(2)}, u32[]{:S(2)}) async-start(f32[128,16,128]{2,1,0:T(8,128)} %get-tuple-element.46), calls=%async_computation.1 | async-start | bytes 2097152 | tf_op jit(solution)/shard_map/all_to_all | solution.py:520
  55.4 6.1 %collective-permute-start = (f32[64,128]{1,0:T(8,128)}, f32[64,128]{1,0:T(8,128)}, u32[]{:S(2)}, u32[]{:S(2)}) collective-permute-start(f32[64,128]{1,0:T(8,128)} %get-tuple-element.52), channel_id=1, source_target_pairs={{0,8},{8,16},{16,24},{24,32},{32,40},{40,48},{48,56},{56,64},{64,7... | collective-permute-start | bytes 98312 | tf_op jit(solution)/shard_map/ppermute | solution.py:525
  59.6 7.6 %collective-permute-start.1 = (f32[64,128]{1,0:T(8,128)}, f32[64,128]{1,0:T(8,128)}, u32[]{:S(2)}, u32[]{:S(2)}) collective-permute-start(f32[64,128]{1,0:T(8,128)} %get-tuple-element.53), channel_id=1, source_target_pairs={{0,120},{8,0},{16,8},{24,16},{32,24},{40,32},{48,40},{56,48},{64,5... | collective-permute-start | bytes 98312 | tf_op jit(solution)/shard_map/ppermute | solution.py:525
  68.6 10.6 %collective-permute-start.2 = (f32[80,128]{1,0:T(8,128)}, f32[80,128]{1,0:T(8,128)}, u32[]{:S(2)}, u32[]{:S(2)}) collective-permute-start(f32[80,128]{1,0:T(8,128)} %get-tuple-element.56), channel_id=1, source_target_pairs={{0,1},{1,2},{2,3},{3,4},{4,5},{5,6},{6,7},{7,0},{8,9},{9,10},{10,1... | collective-permute-start | bytes 122888 | tf_op jit(solution)/shard_map/ppermute | solution.py:525
  68.6 10.6 %collective-permute-start.3 = (f32[80,128]{1,0:T(8,128)}, f32[80,128]{1,0:T(8,128)}, u32[]{:S(2)}, u32[]{:S(2)}) collective-permute-start(f32[80,128]{1,0:T(8,128)} %get-tuple-element.57), channel_id=1, source_target_pairs={{0,7},{1,0},{2,1},{3,2},{4,3},{5,4},{6,5},{7,6},{8,15},{9,8},{10,9... | collective-permute-start | bytes 122888 | tf_op jit(solution)/shard_map/ppermute | solution.py:525
  88.5 22.6 %all-to-all-start.2 = ((f32[128,16,128]{2,1,0:T(8,128)}), f32[128,16,128]{2,1,0:T(8,128)}, u32[]{:S(2)}, u32[]{:S(2)}) async-start(f32[128,16,128]{2,1,0:T(8,128)} %get-tuple-element.64), calls=%async_computation.2 | async-start | bytes 2097152 | tf_op jit(solution)/shard_map/all_to_all | solution.py:520
  116.2 6.1 %collective-permute-start.4 = (f32[64,128]{1,0:T(8,128)}, f32[64,128]{1,0:T(8,128)}, u32[]{:S(2)}, u32[]{:S(2)}) collective-permute-start(f32[64,128]{1,0:T(8,128)} %get-tuple-element.69), channel_id=1, source_target_pairs={{0,8},{8,16},{16,24},{24,32},{32,40},{40,48},{48,56},{56,64},{64,7... | collective-permute-start | bytes 98312 | tf_op jit(solution)/shard_map/ppermute | solution.py:525
  120.4 7.6 %collective-permute-start.5 = (f32[64,128]{1,0:T(8,128)}, f32[64,128]{1,0:T(8,128)}, u32[]{:S(2)}, u32[]{:S(2)}) collective-permute-start(f32[64,128]{1,0:T(8,128)} %get-tuple-element.70), channel_id=1, source_target_pairs={{0,120},{8,0},{16,8},{24,16},{32,24},{40,32},{48,40},{56,48},{64,5... | collective-permute-start | bytes 98312 | tf_op jit(solution)/shard_map/ppermute | solution.py:525
  129.4 10.6 %collective-permute-start.6 = (f32[80,128]{1,0:T(8,128)}, f32[80,128]{1,0:T(8,128)}, u32[]{:S(2)}, u32[]{:S(2)}) collective-permute-start(f32[80,128]{1,0:T(8,128)} %get-tuple-element.73), channel_id=1, source_target_pairs={{0,1},{1,2},{2,3},{3,4},{4,5},{5,6},{6,7},{7,0},{8,9},{9,10},{10,1... | collective-permute-start | bytes 122888 | tf_op jit(solution)/shard_map/ppermute | solution.py:525
  129.4 10.6 %collective-permute-start.7 = (f32[80,128]{1,0:T(8,128)}, f32[80,128]{1,0:T(8,128)}, u32[]{:S(2)}, u32[]{:S(2)}) collective-permute-start(f32[80,128]{1,0:T(8,128)} %get-tuple-element.74), channel_id=1, source_target_pairs={{0,7},{1,0},{2,1},{3,2},{4,3},{5,4},{6,5},{7,6},{8,15},{9,8},{10,9... | collective-permute-start | bytes 122888 | tf_op jit(solution)/shard_map/ppermute | solution.py:525

commit v4 on v3

--- a/solution.py
+++ b/solution.py
@@ -151,17 +151,14 @@
     else:
         table_ref, volt_any, out_any = refs[:3]
         refs = refs[3:]
-    index_ref, number_ref, conduct_ref, scale_any, rows_ref, scratch, volt_ref, out_ref, scale_ref = refs[:9]
-    slots, sem, data_sem, out_sem = refs[9:25], refs[25], refs[26], refs[27]
+    index_ref, scale_any, rows_ref, volt_ref, out_ref, scale_ref = refs[:6]
+    slots, sem, data_sem, out_sem = refs[6:22], refs[22], refs[23], refs[24]
     (volt_copy,) = start_copies([(volt_any, volt_ref)], data_sem)
     first = 0 if incoming else 32
     table = table_ref[...]
     numbers = 64.0 * table + pltpu.roll(table, 112, 1)
     index_ref[...] = numbers.T[first : first + 16, :].astype(I32)
     copies = start_slots(index_ref, slots, sem)
-    number_ref[...] = decode(numbers, first, scratch).astype(I32)
-    conducts = table + pltpu.roll(table, 112, 1) + pltpu.roll(table, 96, 1)
-    conduct_ref[...] = decode(conducts, 64, scratch)
     part = iota((128, 1024), 0)
     lane = iota((128, 1024), 1)
     slot = (lane >> 7) + 8 * ((lane >> 6) & 1)
@@ -190,10 +187,8 @@
 
 
 def prepare_kernel(
-    into_ref,
-    into_conduct_ref,
-    own_ref,
-    own_conduct_ref,
+    got_table_ref,
+    table_ref,
     id_ref,
     ecs_ref,
     point_ref,
@@ -203,6 +198,7 @@
     slot_out,
     place_ref,
     found_ref,
+    scratch,
 ):
     kind = iota((16, 128), 0)
     place_ref[...] = jnp.zeros_like(place_ref)
@@ -210,12 +206,15 @@
     place_ref[16 : 16 + PER, :] = (point_ref[...] & 127).astype(F32)
     places = place_ref[...].astype(BF16)
     total = jnp.zeros((48, CELLS), F32)
-    for side, (index_ref, conduct_ref) in enumerate(((into_ref, into_conduct_ref), (own_ref, own_conduct_ref))):
+    for side, ref in enumerate((got_table_ref, table_ref)):
+        table = ref[...]
+        index = decode(64.0 * table + pltpu.roll(table, 112, 1), 32 * side, scratch).astype(I32)
+        conducts = decode(table + pltpu.roll(table, 112, 1) + pltpu.roll(table, 96, 1), 64, scratch)
         for s in range(16):
-            number = index_ref[s : s + 1, :]
+            number = index[s : s + 1, :]
             hit = marks(number & 255, CELLS)
             here = (number >> 8) == kind
-            first, rest = split2(conduct_ref[s : s + 1, :])
+            first, rest = split2(conducts[s : s + 1, :])
             second, third = split2(rest)
             values = jnp.concatenate([jnp.where(here, x, 0.0) for x in (first, second, third)], axis=0)
             total = total + lax.dot_general(values.astype(BF16), hit, NT, preferred_element_type=F32)
@@ -292,22 +291,29 @@
     deposit_ref[...] = total[:, 0:128] + total[:, 128:256]
 
 
+def odd_of(place_ref, axis):
+    return place_ref[axis] & 1
+
+
 def deposit_kernel(
-    got_any, base_ref, slot_ref, phi_ref, deposit_ref, x_low_ref, x_high_ref, y_low_ref, y_high_ref, got_ref, sem
+    place_ref, got_any, base_any, slot_any, phi_any, deposit_ref, x_near_ref, x_far_ref, y_near_ref, y_far_ref, *scratch
 ):
+    got_ref, base_ref, slot_ref, phi_ref, sem = scratch
     rows = got_ref.shape[0] // CHUNKS
-    copies = [
-        pltpu.make_async_copy(got_any.at[pl.ds(rows * i, rows), :], got_ref.at[pl.ds(rows * i, rows), :], sem.at[i])
-        for i in range(CHUNKS)
-    ]
-    for copy in copies:
-        copy.start()
+    pieces = [pl.ds(rows * i, rows) for i in range(CHUNKS)]
+    copies = start_copies(
+        [(slot_any, slot_ref)]
+        + [(got_any.at[piece], got_ref.at[piece]) for piece in pieces]
+        + [(base_any, base_ref), (phi_any, phi_ref)],
+        sem,
+    )
+    copies[0].wait()
     half = (iota((16, 256), 1) >> 6) & 1
     weights = jnp.where(iota((16, 256), 0) == half, 1.0 / BLOCK, 0.0).astype(BF16)
     total = jnp.zeros((CELLS, 256), F32)
     for r in range(16):
         if r % (16 // CHUNKS) == 0:
-            copies[r // (16 // CHUNKS)].wait()
+            copies[1 + r // (16 // CHUNKS)].wait()
         if r % 2 == 0:
             parts = jnp.concatenate(split2(got_ref[128 * r : 128 * r + 256, :]), axis=1).astype(BF16)
             pair = lax.dot_general(weights, parts, NT, preferred_element_type=F32)
@@ -317,14 +323,22 @@
             return jnp.concatenate([slot_ref[at + r : at + r + 1, :], slot_ref[at + 16 + r : at + 17 + r, :]], axis=1)
 
         total = deposited(total, both(0), both(32), jnp.concatenate([mean[0:1, :], mean[1:2, :]], axis=1))
+    for copy in copies[1 + CHUNKS :]:
+        copy.wait()
     deposit_ref[...] = base_ref[...] - (total[:, 0:128] + total[:, 128:256])
+    odd_x = odd_of(place_ref, 0)
+    odd_y = odd_of(place_ref, 1)
     for array, at, across in ((phi_ref, 0, 0), (deposit_ref, HALO, TILE)):
         for t in range(TILES):
-            start = TILE * t
-            x_low_ref[8 * t + at : 8 * t + at + HALO, :] = array[start : start + HALO, :]
-            x_high_ref[8 * t + at : 8 * t + at + HALO, :] = array[start + TILE - HALO : start + TILE, :]
-        y_low_ref[across : across + TILE, :] = array[0:TILE, :]
-        y_high_ref[across : across + TILE, :] = array[TILE * (TILES - 1) :, :]
+            low = array[TILE * t : TILE * t + HALO, :]
+            high = array[TILE * t + TILE - HALO : TILE * t + TILE, :]
+            place = slice(8 * t + at, 8 * t + at + HALO)
+            x_near_ref[place, :] = jnp.where(jnp.full(low.shape, odd_x) == 0, high, low)
+            x_far_ref[place, :] = jnp.where(jnp.full(low.shape, odd_x) == 0, low, high)
+        near = pl.multiple_of((1 - odd_y) * (TILE * (TILES - 1)), TILE)
+        far = pl.multiple_of(odd_y * (TILE * (TILES - 1)), TILE)
+        y_near_ref[across : across + TILE, :] = array[pl.ds(near, TILE), :]
+        y_far_ref[across : across + TILE, :] = array[pl.ds(far, TILE), :]
 
 
 def collect_kernel(into_ref, own_ref, got_any, base_any, out_any, *scratch):
@@ -375,11 +389,19 @@
         copy.wait()
 
 
-def frame_kernel(before_ref, after_ref, y_low_ref, y_high_ref, low_ref, high_ref):
-    for middle_ref, out_ref, at in ((y_low_ref, low_ref, 0), (y_high_ref, high_ref, 8 * (TILES - 1))):
-        out_ref[0:8, :] = before_ref[at : at + 8, :]
+def ordered(odd, near, far):
+    is_even = jnp.full(near.shape, odd) == 0
+    return jnp.where(is_even, far, near), jnp.where(is_even, near, far)
+
+
+def frame_kernel(place_ref, x_near_ref, x_far_ref, y_near_ref, y_far_ref, near_ref, far_ref):
+    odd_y = odd_of(place_ref, 1)
+    for middle_ref, out_ref, at in ((y_near_ref, near_ref, 1 - odd_y), (y_far_ref, far_ref, odd_y)):
+        rows = pl.ds(pl.multiple_of(at * (8 * (TILES - 1)), 8), 8)
+        before, after = ordered(odd_of(place_ref, 0), x_near_ref[rows, :], x_far_ref[rows, :])
+        out_ref[0:8, :] = before
         out_ref[8:72, :] = middle_ref[...]
-        out_ref[72:80, :] = after_ref[at : at + 8, :]
+        out_ref[72:80, :] = after
 
 
 ROWS = TILE + 2 * HALO
@@ -387,7 +409,7 @@
 
 
 def sweep_kernel(last, *refs):
-    place_ref, phi_ref, deposit_ref, x_before_ref, x_after_ref, y_before_ref, y_after_ref = refs[:7]
+    place_ref, phi_ref, deposit_ref, x_near_ref, x_far_ref, y_near_ref, y_far_ref = refs[:7]
     current_any, volt_any, point_ref = refs[7:10]
     if last:
         volt_out, phi_out, wide_phi, wide_deposit, found_ref, current_ref, volt_ref, phi_held = refs[10:18]
@@ -413,12 +435,14 @@
         )
     end = LEAD + ROWS
     high = LEAD + HALO + TILE
+    x_before, x_after = ordered(odd_of(place_ref, 0), x_near_ref[...], x_far_ref[...])
+    y_before, y_after = ordered(odd_of(place_ref, 1), y_near_ref[...], y_far_ref[...])
     for wide, array, at, across in ((wide_phi, phi_ref, 0, 0), (wide_deposit, deposit_ref, HALO, TILE)):
         for t in range(TILES):
-            wide[t + 1, LEAD : LEAD + HALO, :] = x_before_ref[8 * t + at : 8 * t + at + HALO, :]
+            wide[t + 1, LEAD : LEAD + HALO, :] = x_before[8 * t + at : 8 * t + at + HALO, :]
             wide[t + 1, LEAD + HALO : high, :] = array[TILE * t : TILE * t + TILE, :]
-            wide[t + 1, high:end, :] = x_after_ref[8 * t + at : 8 * t + at + HALO, :]
-        for t, came in ((0, y_before_ref), (TILES + 1, y_after_ref)):
+            wide[t + 1, high:end, :] = x_after[8 * t + at : 8 * t + at + HALO, :]
+        for t, came in ((0, y_before), (TILES + 1, y_after)):
             wide[t, LEAD : LEAD + HALO, :] = came[at : at + HALO, :]
             wide[t, LEAD + HALO : high, :] = came[8 + across : 8 + across + TILE, :]
             wide[t, high:end, :] = came[72 + at : 72 + at + HALO, :]
@@ -520,9 +544,10 @@
     return lax.all_to_all(x, AXES, split_axis=0, concat_axis=0, tiled=True)
 
 
-def shift(x, axis, by):
+def swap(x, axis, first):
     size = lax.axis_size(axis)
-    return lax.ppermute(x, axis, [(i, (i + by) % size) for i in range(size)])
+    pairs = [((first + i) % size, (first + i + 1) % size) for i in range(0, size, 2)]
+    return lax.ppermute(x, axis, pairs + [(j, i) for i, j in pairs])
 
 
 def on_device(
@@ -556,12 +581,11 @@
     slot_scratch = [pltpu.SMEM((1, 128), I32)] * CAP
     slot_sem = pltpu.SemaphoreType.DMA((CAP,))
     small = shaped(16, 128, dtype=I32)
-    tables_out = (small, small, shaped(16, 128), shaped(DEVS * 8, 128))
+    tables_out = (small, shaped(DEVS * 8, 128))
     plane = pltpu.VMEM((CELLS, NODES), F32)
     scale_scratch = pltpu.VMEM((DEVS * 8, 128), F32)
     gather_scratch = [
         rows_scratch,
-        pltpu.VMEM((128, 128), F32),
         plane,
         pltpu.VMEM((DEVS, 8, 128), F32),
         scale_scratch,
@@ -572,20 +596,20 @@
     ]
     anywhere = pl.BlockSpec(memory_space=pl.ANY)
     message = shaped(DEVS, 16, 128)
-    outgoing, own, own_number, own_conduct, own_scale = pl.pallas_call(
+    outgoing, own, own_scale = pl.pallas_call(
         functools.partial(gather_kernel, False),
         out_shape=(message,) + tables_out,
         in_specs=[VMEM, anywhere],
-        out_specs=(anywhere,) + (VMEM,) * 3 + (anywhere,),
+        out_specs=(anywhere, VMEM, anywhere),
         scratch_shapes=gather_scratch,
         compiler_params=PARAMS,
         name="gather_source",
     )(table, potential)
-    outgoing, into, into_number, into_conduct, into_scale = pl.pallas_call(
+    outgoing, into, into_scale = pl.pallas_call(
         functools.partial(gather_kernel, True),
         out_shape=(message,) + tables_out,
         in_specs=[VMEM, anywhere, anywhere],
-        out_specs=(anywhere,) + (VMEM,) * 3 + (anywhere,),
+        out_specs=(anywhere, VMEM, anywhere),
         scratch_shapes=gather_scratch,
         input_output_aliases={2: 0},
         compiler_params=PARAMS,
@@ -595,16 +619,14 @@
     degree, id_wide, phi, slot_points = pl.pallas_call(
         prepare_kernel,
         out_shape=(shaped(CELLS, NODES), shaped(CELLS, 128), shaped(TILE * TILES, 128), shaped(64, 128, dtype=I32)),
-        in_specs=[VMEM] * 7,
+        in_specs=[VMEM] * 5,
         out_specs=(VMEM,) * 4,
-        scratch_shapes=[pltpu.VMEM((32, CELLS), F32), pltpu.VMEM((64, 128), F32)],
+        scratch_shapes=[pltpu.VMEM((32, CELLS), F32), pltpu.VMEM((64, 128), F32), pltpu.VMEM((128, 128), F32)],
         compiler_params=PARAMS,
         name="prepare",
     )(
-        into_number,
-        into_conduct,
-        own_number,
-        own_conduct,
+        got_table,
+        table,
         template_id.reshape(2, 128),
         ecs_start.reshape(TILE * TILE, TILE),
         points,
@@ -631,28 +653,34 @@
             compiler_params=PARAMS,
             name="base",
         )(volt, recov, id_wide, degree, points, templates)
-        deposit, x_low, x_high, y_low, y_high = pl.pallas_call(
+        deposit, x_near, x_far, y_near, y_far = pl.pallas_call(
             deposit_kernel,
             out_shape=(shaped(TILE * TILES, 128),) + (shaped(64, 128),) * 4,
-            in_specs=[anywhere] + [VMEM] * 3,
+            in_specs=[SMEM] + [anywhere] * 4,
             out_specs=(VMEM,) * 5,
-            scratch_shapes=[pltpu.VMEM((DEVS * 16, 128), F32), pltpu.SemaphoreType.DMA((CHUNKS,))],
+            scratch_shapes=[
+                pltpu.VMEM((DEVS * 16, 128), F32),
+                pltpu.VMEM((TILE * TILES, 128), F32),
+                pltpu.VMEM((64, 128), I32),
+                pltpu.VMEM((TILE * TILES, 128), F32),
+                pltpu.SemaphoreType.DMA((CHUNKS + 3,)),
+            ],
             compiler_params=PARAMS,
             name="deposit",
-        )(got, deposit_base, slot_points, phi)
-
-        x_before = shift(x_high, "tx", 1)
-        x_after = shift(x_low, "tx", -1)
-        y_low, y_high = pl.pallas_call(
+        )(place, got, deposit_base, slot_points, phi)
+
+        x_far = swap(x_far, "tx", 1)
+        x_near = swap(x_near, "tx", 0)
+        y_near, y_far = pl.pallas_call(
             frame_kernel,
             out_shape=(shaped(80, 128),) * 2,
-            in_specs=[VMEM] * 4,
+            in_specs=[SMEM] + [VMEM] * 4,
             out_specs=(VMEM,) * 2,
             compiler_params=PARAMS,
             name="frame",
-        )(x_before, x_after, y_low, y_high)
-        y_before = shift(y_high, "ty", 1)
-        y_after = shift(y_low, "ty", -1)
+        )(place, x_near, x_far, y_near, y_far)
+        y_far = swap(y_far, "ty", 1)
+        y_near = swap(y_near, "ty", 0)
         current = pl.pallas_call(
             collect_kernel,
             out_shape=shaped(CELLS, NODES),
@@ -672,7 +700,7 @@
             compiler_params=PARAMS,
             name="collect",
         )(into, own, got, base)
-        operands = [place, phi, deposit, x_before, x_after, y_before, y_after, current, volt, points]
+        operands = [place, phi, deposit, x_near, x_far, y_near, y_far, current, volt, points]
         specs = [SMEM] + [VMEM] * 6 + [anywhere] * 2 + [VMEM]
         wide = [pltpu.VMEM((TILES + 2, LEAD + ROWS + 8, 128), F32)] * 2 + [pltpu.VMEM((16, CELLS), F32)]
         if last:

time: 145 us -> 141 us (0.972)
  the two profiles are of different devices: /device:TPU:30 before, /device:TPU:1 now
where the time goes in v4:
time: 141 us; the launch traced here: 140 us
  Pallas kernels  76.3 us (54%)
  starting transfers between devices  34.5 us (24%)
  waiting for transfers between devices  26 us (18%)
  local copies, waits for them, and re-layouts  1.53 us (1%)
    all_to_all x3, starting transfers between devices, exchange(): return lax.all_to_all(x, AXES, split_axis=0, concat_axis=0, tiled=True)  25.1 us
    pallas_call x2, Pallas kernels, on_device(): pl.pallas_call(base_kernel, out_shape=(shaped(CELLS, NODES), shaped(TILE...  19.1 us
    all_to_all x3, waiting for transfers between devices, exchange(): return lax.all_to_all(x, AXES, split_axis=0, concat_axis=0, tiled=True)  16.3 us
    pallas_call x2, Pallas kernels, on_device(): pl.pallas_call(collect_kernel, out_shape=shaped(CELLS, NODES), in_specs=[...  14.6 us
    pallas_call x2, Pallas kernels, on_device(): pl.pallas_call(deposit_kernel, out_shape=(shaped(TILE * TILES, 128),) + (...  9.87 us
    ppermute x8, waiting for transfers between devices, swap(): return lax.ppermute(x, axis, pairs + [(j, i) for i, j in pairs])  9.75 us
    ppermute x8, starting transfers between devices, swap(): return lax.ppermute(x, axis, pairs + [(j, i) for i, j in pairs])  9.47 us
    pallas_call x1, Pallas kernels, on_device(): pl.pallas_call(functools.partial(sweep_kernel, False), out_shape=(shaped(...  9.23 us
  transfers between devices with their start and end apart: 11, of which 7 were waited for; matrix products, arithmetic and copies ran while one was open for 2% of the time, Pallas kernels for 31%

profile of v4, /device:TPU:1, one launch (start us, length us, event | category | flops | bytes accessed | tf_op | source)
XLA Modules:
  0.0 140.1 jit_solution(9230558355568598959)
XLA Ops:
  0.6 2.1 %setup.1.table_ref.refs_0_ = f32[128,128]{1,0:T(8,128)} custom-call(s32[8,128]{1,0:T(8,128)} %bitcast.23, s32[8,128]{1,0:T(8,128)} %bitcast.24, s32[8,128]{1,0:T(8,128)} %bitcast.25, f32[8,128]{1,0:T(8,128)} %bitcast.26), custom_call_target="tpu_custom_call" | custom-call | tf_op jit(solution)/shard_map/setup/pallas_call | solution.py:566
  2.7 11.9 %all-to-all-start = ((f32[128,1,128]{2,1,0:T(1,128)}), f32[128,1,128]{2,1,0:T(1,128)}, u32[]{:S(2)}, u32[]{:S(2)}) async-start(f32[128,1,128]{2,1,0:T(1,128)} %bitcast.16), calls=%async_computation | async-start | bytes 131072 | tf_op jit(solution)/shard_map/all_to_all | solution.py:544
  14.7 5.4 %gather_source.1 = (f32[128,16,128]{2,1,0:T(8,128)}, s32[16,128]{1,0:T(8,128)}, f32[1024,128]{1,0:T(8,128)}) custom-call(f32[128,128]{1,0:T(8,128)} %setup.1.table_ref.refs_0_, f32[256,768]{1,0:T(8,128)} %refs_8_.1), custom_call_target="tpu_custom_call" | custom-call | tf_op jit(solution)/shard_map/gather_source/pallas_call | solution.py:599
  20.1 4.0 %all-to-all-done = f32[128,1,128]{2,1,0:T(1,128)} async-done(((f32[128,1,128]{2,1,0:T(1,128)}), f32[128,1,128]{2,1,0:T(1,128)}, u32[]{:S(2)}, u32[]{:S(2)}) %all-to-all-start) | async-done | bytes 65568 | tf_op jit(solution)/shard_map/all_to_all | solution.py:544
  24.0 5.4 %gather_target.1 = (f32[128,16,128]{2,1,0:T(8,128)}, s32[16,128]{1,0:T(8,128)}, f32[1024,128]{1,0:T(8,128)}) custom-call(f32[128,128]{1,0:T(8,128)} %bitcast.8.got_table_ref.refs_0_, f32[256,768]{1,0:T(8,128)} %refs_8_.1, f32[128,16,128]{2,1,0:T(8,128)} %get-tuple-element.37.refs_2_), custom_call_target="tpu_custom_call", output_to_operand_aliasing={{0}: (2, {})} | custom-call | tf_op jit(solution)/shard_map/gather_target/pallas_call | solution.py:608
  29.4 6.3 %all-to-all-start.1 = ((f32[128,16,128]{2,1,0:T(8,128)}), f32[128,16,128]{2,1,0:T(8,128)}, u32[]{:S(2)}, u32[]{:S(2)}) async-start(f32[128,16,128]{2,1,0:T(8,128)} %get-tuple-element.38), calls=%async_computation.1 | async-start | bytes 2097152 | tf_op jit(solution)/shard_map/all_to_all | solution.py:544
  37.9 3.7 %prepare.1 = (f32[256,768]{1,0:T(8,128)}, f32[256,128]{1,0:T(8,128)}, f32[256,128]{1,0:T(8,128)}, s32[64,128]{1,0:T(8,128)}) custom-call(f32[128,128]{1,0:T(8,128)} %bitcast.8.got_table_ref.refs_0_, f32[128,128]{1,0:T(8,128)} %setup.1.table_ref.refs_0_, s32[2,128]{1,0:T(2,128)} %bitcast.27, f32[1024,32]{1,0:T(8,128)} %bitcast.22, s32[12,256]{1,0:T(8,128)} %bitcast.17), custom_call_target="tpu_custom_call" | custom-call | tf_op jit(solution)/shard_map/prepare/pallas_call | solution.py:619
  41.6 9.6 %base.2 = (f32[256,768]{1,0:T(8,128)}, f32[256,128]{1,0:T(8,128)}) custom-call(f32[256,768]{1,0:T(8,128)} %refs_8_.1, f32[256,768]{1,0:T(8,128)} %refs_10_.1, f32[256,128]{1,0:T(8,128)} %get-tuple-element.39.id_ref, f32[256,768]{1,0:T(8,128)} %get-tuple-element.40.degree_ref, s32[12,256]{1,0:T(8,128)} %bitcast.18, bf16[10,768,768]{2,1,0:T(8,128)(2,1)} %template_ref.3), custom_call_target="tpu_custom_call" | custom-call | flops 3000000000 | bytes 14000000 | tf_op jit(solution)/shard_map/base/pallas_call | solution.py:642
  51.1 3.2 %all-to-all-done.1 = f32[128,16,128]{2,1,0:T(8,128)} async-done(((f32[128,16,128]{2,1,0:T(8,128)}), f32[128,16,128]{2,1,0:T(8,128)}, u32[]{:S(2)}, u32[]{:S(2)}) %all-to-all-start.1) | async-done | bytes 1048608 | tf_op jit(solution)/shard_map/all_to_all | solution.py:544
  54.4 4.9 %deposit.2 = (f32[256,128]{1,0:T(8,128)}, f32[64,128]{1,0:T(8,128)}, f32[64,128]{1,0:T(8,128)}, f32[64,128]{1,0:T(8,128)}, f32[64,128]{1,0:T(8,128)}) custom-call(s32[4]{0:T(128)} %pad_add_fusion.place_ref.refs_0_, f32[2048,128]{1,0:T(8,128)} %bitcast.12.got_any, f32[256,128]{1,0:T(8,128)} %get-tuple-element.41.base_any, ...), custom_call_target="tpu_custom_call" | custom-call | tf_op jit(solution)/shard_map/deposit/pallas_call | solution.py:656
  59.8 1.7 %collective-permute-start.1 = (f32[64,128]{1,0:T(8,128)}, f32[64,128]{1,0:T(8,128)}, u32[]{:S(2)}, u32[]{:S(2)}) collective-permute-start(f32[64,128]{1,0:T(8,128)} %get-tuple-element.45), channel_id=1, source_target_pairs={{8,16},{24,32},{40,48},{56,64},{72,80},{88,96},{104,112},{120,0},{... | collective-permute-start | bytes 98312 | tf_op jit(solution)/shard_map/ppermute | solution.py:550
  62.5 3.8 %collective-permute-done.1.x_far_ref.refs_4_ = f32[64,128]{1,0:T(8,128)} collective-permute-done((f32[64,128]{1,0:T(8,128)}, f32[64,128]{1,0:T(8,128)}, u32[]{:S(2)}, u32[]{:S(2)}) %collective-permute-start.1) | collective-permute-done | bytes 32800 | tf_op jit(solution)/shard_map/ppermute | solution.py:550
  66.2 1.5 %frame.2 = (f32[80,128]{1,0:T(8,128)}, f32[80,128]{1,0:T(8,128)}) custom-call(s32[4]{0:T(128)} %pad_add_fusion.place_ref.refs_0_, f32[64,128]{1,0:T(8,128)} %collective-permute-done.x_near_ref.refs_3_, f32[64,128]{1,0:T(8,128)} %collective-permute-done.1.x_far_ref.refs_4_, f32[64,128]{1,0:T(8,128)} %get-tuple-element.46.y_near_ref, ...), custom_call_target="tpu_custom_call" | custom-call | tf_op jit(solution)/shard_map/frame/pallas_call | solution.py:674
  67.7 2.7 %collective-permute-start.2 = (f32[80,128]{1,0:T(8,128)}, f32[80,128]{1,0:T(8,128)}, u32[]{:S(2)}, u32[]{:S(2)}) collective-permute-start(f32[80,128]{1,0:T(8,128)} %get-tuple-element.48), channel_id=1, source_target_pairs={{0,1},{2,3},{4,5},{6,7},{1,0},{3,2},{5,4},{7,6},{8,9},{10,11},{12,... | collective-permute-start | bytes 122888 | tf_op jit(solution)/shard_map/ppermute | solution.py:550
  70.4 7.3 %collect.2.refs_7_ = f32[256,768]{1,0:T(8,128)} custom-call(s32[16,128]{1,0:T(8,128)} %get-tuple-element.50.into_ref.refs_11_, s32[16,128]{1,0:T(8,128)} %get-tuple-element.51.own_ref.refs_13_, f32[2048,128]{1,0:T(8,128)} %bitcast.12.got_any, f32[256,768]{1,0:T(8,128)} %get-tuple-element.52.base_any), custom_call_target="tpu_custom_call" | custom-call | flops 1000000000 | bytes 10000000 | tf_op jit(solution)/shard_map/collect/pallas_call | solution.py:684
  77.7 9.2 %sweep.1 = (f32[256,768]{1,0:T(8,128)}, f32[256,128]{1,0:T(8,128)}, f32[256,768]{1,0:T(8,128)}, f32[128,16,128]{2,1,0:T(8,128)}) custom-call(s32[4]{0:T(128)} %pad_add_fusion.place_ref.refs_0_, f32[256,128]{1,0:T(8,128)} %get-tuple-element.36.phi_any.refs_1_, f32[256,128]{1,0:T(8,128)} %get-tuple-element.43.refs_2_, ...), custom_call_target="tpu_custom_call" | custom-call | tf_op jit(solution)/shard_map/sweep/pallas_call | solution.py:723
  86.9 6.9 %all-to-all-start.2 = ((f32[128,16,128]{2,1,0:T(8,128)}), f32[128,16,128]{2,1,0:T(8,128)}, u32[]{:S(2)}, u32[]{:S(2)}) async-start(f32[128,16,128]{2,1,0:T(8,128)} %get-tuple-element.56), calls=%async_computation.2 | async-start | bytes 2097152 | tf_op jit(solution)/shard_map/all_to_all | solution.py:544
  93.8 9.6 %base.3 = (f32[256,768]{1,0:T(8,128)}, f32[256,128]{1,0:T(8,128)}) custom-call(f32[256,768]{1,0:T(8,128)} %get-tuple-element.57.volt_ref.refs_8_, f32[256,768]{1,0:T(8,128)} %get-tuple-element.58.recov_ref, f32[256,128]{1,0:T(8,128)} %get-tuple-element.39.id_ref, f32[256,768]{1,0:T(8,128)} %get-tuple-element.40.degree_ref, s32[12,256]{1,0:T(8,128)} %bitcast.20, ...), custom_call_target="tpu_custom_call" | custom-call | flops 3000000000 | bytes 14000000 | tf_op jit(solution)/shard_map/base/pallas_call | solution.py:642
  103.4 9.1 %all-to-all-done.2 = f32[128,16,128]{2,1,0:T(8,128)} async-done(((f32[128,16,128]{2,1,0:T(8,128)}), f32[128,16,128]{2,1,0:T(8,128)}, u32[]{:S(2)}, u32[]{:S(2)}) %all-to-all-start.2) | async-done | bytes 1048608 | tf_op jit(solution)/shard_map/all_to_all | solution.py:544
  112.5 4.9 %deposit.3 = (f32[256,128]{1,0:T(8,128)}, f32[64,128]{1,0:T(8,128)}, f32[64,128]{1,0:T(8,128)}, f32[64,128]{1,0:T(8,128)}, f32[64,128]{1,0:T(8,128)}) custom-call(s32[4]{0:T(128)} %pad_add_fusion.place_ref.refs_0_, f32[2048,128]{1,0:T(8,128)} %bitcast.13.got_any, f32[256,128]{1,0:T(8,128)} %get-tuple-element.59.base_any, ...), custom_call_target="tpu_custom_call" | custom-call | tf_op jit(solution)/shard_map/deposit/pallas_call | solution.py:656
  120.6 3.8 %collective-permute-done.5.x_far_ref.refs_4_ = f32[64,128]{1,0:T(8,128)} collective-permute-done((f32[64,128]{1,0:T(8,128)}, f32[64,128]{1,0:T(8,128)}, u32[]{:S(2)}, u32[]{:S(2)}) %collective-permute-start.5) | collective-permute-done | bytes 32800 | tf_op jit(solution)/shard_map/ppermute | solution.py:550
  125.8 2.7 %collective-permute-start.6 = (f32[80,128]{1,0:T(8,128)}, f32[80,128]{1,0:T(8,128)}, u32[]{:S(2)}, u32[]{:S(2)}) collective-permute-start(f32[80,128]{1,0:T(8,128)} %get-tuple-element.65), channel_id=1, source_target_pairs={{0,1},{2,3},{4,5},{6,7},{1,0},{3,2},{5,4},{7,6},{8,9},{10,11},{12,... | collective-permute-start | bytes 122888 | tf_op jit(solution)/shard_map/ppermute | solution.py:550
  128.5 7.3 %collect.3.refs_7_ = f32[256,768]{1,0:T(8,128)} custom-call(s32[16,128]{1,0:T(8,128)} %get-tuple-element.50.into_ref.refs_11_, s32[16,128]{1,0:T(8,128)} %get-tuple-element.51.own_ref.refs_13_, f32[2048,128]{1,0:T(8,128)} %bitcast.13.got_any, f32[256,768]{1,0:T(8,128)} %get-tuple-element.67.base_any), custom_call_target="tpu_custom_call" | custom-call | flops 1000000000 | bytes 10000000 | tf_op jit(solution)/shard_map/collect/pallas_call | solution.py:684
  135.8 4.0 %sweep_last.1 = (f32[256,768]{1,0:T(8,128)}, f32[1024,32]{1,0:T(8,128)}) custom-call(s32[4]{0:T(128)} %pad_add_fusion.place_ref.refs_0_, f32[256,128]{1,0:T(8,128)} %get-tuple-element.55.phi_any.refs_1_, f32[256,128]{1,0:T(8,128)} %get-tuple-element.60.refs_2_, f32[64,128]{1,0:T(8,128)} %collective-permute-done.4.x_near_ref.refs_3_, ...), custom_call_target="tpu_custom_call" | custom-call | tf_op jit(solution)/shard_map/sweep_last/pallas_call | solution.py:707
  (15 shorter events, 8.3 us)
Async XLA Ops:
  2.7 21.3 %all-to-all-start = ((f32[128,1,128]{2,1,0:T(1,128)}), f32[128,1,128]{2,1,0:T(1,128)}, u32[]{:S(2)}, u32[]{:S(2)}) async-start(f32[128,1,128]{2,1,0:T(1,128)} %bitcast.16), calls=%async_computation | async-start | bytes 131072 | tf_op jit(solution)/shard_map/all_to_all | solution.py:544
  29.4 24.9 %all-to-all-start.1 = ((f32[128,16,128]{2,1,0:T(8,128)}), f32[128,16,128]{2,1,0:T(8,128)}, u32[]{:S(2)}, u32[]{:S(2)}) async-start(f32[128,16,128]{2,1,0:T(8,128)} %get-tuple-element.38), calls=%async_computation.1 | async-start | bytes 2097152 | tf_op jit(solution)/shard_map/all_to_all | solution.py:544
  59.3 3.2 %collective-permute-start = (f32[64,128]{1,0:T(8,128)}, f32[64,128]{1,0:T(8,128)}, u32[]{:S(2)}, u32[]{:S(2)}) collective-permute-start(f32[64,128]{1,0:T(8,128)} %get-tuple-element.44), channel_id=1, source_target_pairs={{0,8},{16,24},{32,40},{48,56},{64,72},{80,88},{96,104},{112,120},{... | collective-permute-start | bytes 98312 | tf_op jit(solution)/shard_map/ppermute | solution.py:550
  59.8 6.4 %collective-permute-start.1 = (f32[64,128]{1,0:T(8,128)}, f32[64,128]{1,0:T(8,128)}, u32[]{:S(2)}, u32[]{:S(2)}) collective-permute-start(f32[64,128]{1,0:T(8,128)} %get-tuple-element.45), channel_id=1, source_target_pairs={{8,16},{24,32},{40,48},{56,64},{72,80},{88,96},{104,112},{120,0},{... | collective-permute-start | bytes 98312 | tf_op jit(solution)/shard_map/ppermute | solution.py:550
  67.7 10.0 %collective-permute-start.2 = (f32[80,128]{1,0:T(8,128)}, f32[80,128]{1,0:T(8,128)}, u32[]{:S(2)}, u32[]{:S(2)}) collective-permute-start(f32[80,128]{1,0:T(8,128)} %get-tuple-element.48), channel_id=1, source_target_pairs={{0,1},{2,3},{4,5},{6,7},{1,0},{3,2},{5,4},{7,6},{8,9},{10,11},{12,... | collective-permute-start | bytes 122888 | tf_op jit(solution)/shard_map/ppermute | solution.py:550
  70.4 7.3 %collective-permute-start.3 = (f32[80,128]{1,0:T(8,128)}, f32[80,128]{1,0:T(8,128)}, u32[]{:S(2)}, u32[]{:S(2)}) collective-permute-start(f32[80,128]{1,0:T(8,128)} %get-tuple-element.49), channel_id=1, source_target_pairs={{1,2},{3,4},{5,6},{7,0},{2,1},{4,3},{6,5},{0,7},{9,10},{11,12},{13... | collective-permute-start | bytes 122888 | tf_op jit(solution)/shard_map/ppermute | solution.py:550
  86.9 25.5 %all-to-all-start.2 = ((f32[128,16,128]{2,1,0:T(8,128)}), f32[128,16,128]{2,1,0:T(8,128)}, u32[]{:S(2)}, u32[]{:S(2)}) async-start(f32[128,16,128]{2,1,0:T(8,128)} %get-tuple-element.56), calls=%async_computation.2 | async-start | bytes 2097152 | tf_op jit(solution)/shard_map/all_to_all | solution.py:544
  117.4 3.2 %collective-permute-start.4 = (f32[64,128]{1,0:T(8,128)}, f32[64,128]{1,0:T(8,128)}, u32[]{:S(2)}, u32[]{:S(2)}) collective-permute-start(f32[64,128]{1,0:T(8,128)} %get-tuple-element.61), channel_id=1, source_target_pairs={{0,8},{16,24},{32,40},{48,56},{64,72},{80,88},{96,104},{112,120},{... | collective-permute-start | bytes 98312 | tf_op jit(solution)/shard_map/ppermute | solution.py:550
  117.9 6.4 %collective-permute-start.5 = (f32[64,128]{1,0:T(8,128)}, f32[64,128]{1,0:T(8,128)}, u32[]{:S(2)}, u32[]{:S(2)}) collective-permute-start(f32[64,128]{1,0:T(8,128)} %get-tuple-element.62), channel_id=1, source_target_pairs={{8,16},{24,32},{40,48},{56,64},{72,80},{88,96},{104,112},{120,0},{... | collective-permute-start | bytes 98312 | tf_op jit(solution)/shard_map/ppermute | solution.py:550
  125.8 10.0 %collective-permute-start.6 = (f32[80,128]{1,0:T(8,128)}, f32[80,128]{1,0:T(8,128)}, u32[]{:S(2)}, u32[]{:S(2)}) collective-permute-start(f32[80,128]{1,0:T(8,128)} %get-tuple-element.65), channel_id=1, source_target_pairs={{0,1},{2,3},{4,5},{6,7},{1,0},{3,2},{5,4},{7,6},{8,9},{10,11},{12,... | collective-permute-start | bytes 122888 | tf_op jit(solution)/shard_map/ppermute | solution.py:550
  128.5 7.3 %collective-permute-start.7 = (f32[80,128]{1,0:T(8,128)}, f32[80,128]{1,0:T(8,128)}, u32[]{:S(2)}, u32[]{:S(2)}) collective-permute-start(f32[80,128]{1,0:T(8,128)} %get-tuple-element.66), channel_id=1, source_target_pairs={{1,2},{3,4},{5,6},{7,0},{2,1},{4,3},{6,5},{0,7},{9,10},{11,12},{13... | collective-permute-start | bytes 122888 | tf_op jit(solution)/shard_map/ppermute | solution.py:550

commit v5 on v4

--- a/solution.py
+++ b/solution.py
@@ -24,7 +24,6 @@
 I32 = jnp.int32
 AXES = ("tx", "ty")
 VMEM = pl.BlockSpec(memory_space=pltpu.VMEM)
-SMEM = pl.BlockSpec(memory_space=pltpu.SMEM)
 NT = (((1,), (1,)), ((), ()))
 TN = (((0,), (0,)), ((), ()))
 PARAMS = pltpu.CompilerParams(vmem_limit_bytes=67_043_328)
@@ -291,12 +290,12 @@
     deposit_ref[...] = total[:, 0:128] + total[:, 128:256]
 
 
-def odd_of(place_ref, axis):
-    return place_ref[axis] & 1
+def odd_of(axis):
+    return lax.axis_index(axis) & 1
 
 
 def deposit_kernel(
-    place_ref, got_any, base_any, slot_any, phi_any, deposit_ref, x_near_ref, x_far_ref, y_near_ref, y_far_ref, *scratch
+    got_any, base_any, slot_any, phi_any, deposit_ref, x_near_ref, x_far_ref, y_near_ref, y_far_ref, *scratch
 ):
     got_ref, base_ref, slot_ref, phi_ref, sem = scratch
     rows = got_ref.shape[0] // CHUNKS
@@ -326,8 +325,8 @@
     for copy in copies[1 + CHUNKS :]:
         copy.wait()
     deposit_ref[...] = base_ref[...] - (total[:, 0:128] + total[:, 128:256])
-    odd_x = odd_of(place_ref, 0)
-    odd_y = odd_of(place_ref, 1)
+    odd_x = odd_of("tx")
+    odd_y = odd_of("ty")
     for array, at, across in ((phi_ref, 0, 0), (deposit_ref, HALO, TILE)):
         for t in range(TILES):
             low = array[TILE * t : TILE * t + HALO, :]
@@ -394,14 +393,15 @@
     return jnp.where(is_even, far, near), jnp.where(is_even, near, far)
 
 
-def frame_kernel(place_ref, x_near_ref, x_far_ref, y_near_ref, y_far_ref, near_ref, far_ref):
-    odd_y = odd_of(place_ref, 1)
-    for middle_ref, out_ref, at in ((y_near_ref, near_ref, 1 - odd_y), (y_far_ref, far_ref, odd_y)):
-        rows = pl.ds(pl.multiple_of(at * (8 * (TILES - 1)), 8), 8)
-        before, after = ordered(odd_of(place_ref, 0), x_near_ref[rows, :], x_far_ref[rows, :])
-        out_ref[0:8, :] = before
-        out_ref[8:72, :] = middle_ref[...]
-        out_ref[72:80, :] = after
+def frame_kernel(y_near_ref, y_far_ref, x_near_ref, x_far_ref, near_ref, far_ref):
+    odd_x = odd_of("tx")
+    for middle_ref, out_ref, high in ((x_near_ref, near_ref, 1 - odd_x), (x_far_ref, far_ref, odd_x)):
+        out_ref[0:64, :] = middle_ref[...]
+        for at, across in ((0, 0), (HALO, TILE)):
+            rows = pl.ds(pl.multiple_of(high * (TILE - HALO) + across, HALO), HALO)
+            before, after = ordered(odd_of("ty"), y_near_ref[rows, :], y_far_ref[rows, :])
+            out_ref[64 + at : 64 + at + HALO, :] = before
+            out_ref[72 + at : 72 + at + HALO, :] = after
 
 
 ROWS = TILE + 2 * HALO
@@ -409,19 +409,20 @@
 
 
 def sweep_kernel(last, *refs):
-    place_ref, phi_ref, deposit_ref, x_near_ref, x_far_ref, y_near_ref, y_far_ref = refs[:7]
-    current_any, volt_any, point_ref = refs[7:10]
+    phi_ref, deposit_ref, x_near_ref, x_far_ref, y_near_ref, y_far_ref = refs[:6]
+    current_any, volt_any, point_ref = refs[6:9]
+    refs = refs[9:]
     if last:
-        volt_out, phi_out, wide_phi, wide_deposit, found_ref, current_ref, volt_ref, phi_held = refs[10:18]
-        data_sem, out_sem = refs[18:]
+        volt_out, phi_out, wide_phi, wide_deposit, found_ref, current_ref, volt_ref, phi_held = refs[:8]
+        data_sem, out_sem = refs[8:]
         fetched = start_copies([(current_any, current_ref), (volt_any, volt_ref)], data_sem)
     else:
-        recov_any, into_ref, into_scale_any, own_ref, own_scale_any = refs[10:15]
-        volt_out, phi_out, recov_out, send_any = refs[15:19]
-        wide_phi, wide_deposit, found_ref, current_ref, volt_ref, recov_ref = refs[19:25]
-        own_scale_ref, into_scale_ref, send_ref, rows_ref = refs[25:29]
-        own_slots, into_slots = refs[29:45], refs[45:61]
-        own_sem, into_sem, data_sem, out_sem = refs[61:]
+        recov_any, into_ref, into_scale_any, own_ref, own_scale_any = refs[:5]
+        volt_out, phi_out, recov_out, send_any = refs[5:9]
+        wide_phi, wide_deposit, found_ref, current_ref, volt_ref, recov_ref = refs[9:15]
+        own_scale_ref, into_scale_ref, send_ref, rows_ref = refs[15:19]
+        own_slots, into_slots = refs[19:35], refs[35:51]
+        own_sem, into_sem, data_sem, out_sem = refs[51:]
         copies = start_slots(own_ref, own_slots, own_sem) + start_slots(into_ref, into_slots, into_sem)
         fetched = start_copies(
             [
@@ -435,26 +436,26 @@
         )
     end = LEAD + ROWS
     high = LEAD + HALO + TILE
-    x_before, x_after = ordered(odd_of(place_ref, 0), x_near_ref[...], x_far_ref[...])
-    y_before, y_after = ordered(odd_of(place_ref, 1), y_near_ref[...], y_far_ref[...])
+    x_before, x_after = ordered(odd_of("tx"), x_near_ref[...], x_far_ref[...])
+    y_before, y_after = ordered(odd_of("ty"), y_near_ref[...], y_far_ref[...])
     for wide, array, at, across in ((wide_phi, phi_ref, 0, 0), (wide_deposit, deposit_ref, HALO, TILE)):
         for t in range(TILES):
             wide[t + 1, LEAD : LEAD + HALO, :] = x_before[8 * t + at : 8 * t + at + HALO, :]
             wide[t + 1, LEAD + HALO : high, :] = array[TILE * t : TILE * t + TILE, :]
             wide[t + 1, high:end, :] = x_after[8 * t + at : 8 * t + at + HALO, :]
-        for t, came in ((0, y_before), (TILES + 1, y_after)):
-            wide[t, LEAD : LEAD + HALO, :] = came[at : at + HALO, :]
-            wide[t, LEAD + HALO : high, :] = came[8 + across : 8 + across + TILE, :]
-            wide[t, high:end, :] = came[72 + at : 72 + at + HALO, :]
+        for t, came, corner in ((0, y_before, 64 + at), (TILES + 1, y_after, 72 + at)):
+            wide[t, LEAD : LEAD + HALO, :] = x_before[corner : corner + HALO, :]
+            wide[t, LEAD + HALO : high, :] = came[across : across + TILE, :]
+            wide[t, high:end, :] = x_after[corner : corner + HALO, :]
     shape = (ROWS, 128)
     row = iota(shape, 0)
     lane = iota(shape, 1)
     depth = lane & (TILE - 1)
-    first_row = jnp.where(place_ref[0] == 0, HALO, 0)
-    last_row = jnp.where(place_ref[0] == place_ref[2] - 1, HALO + TILE, ROWS)
+    first_row = jnp.where(lax.axis_index("tx") == 0, HALO, 0)
+    last_row = jnp.where(lax.axis_index("tx") == lax.axis_size("tx") - 1, HALO + TILE, ROWS)
     inside = (row >= first_row) & (row < last_row)
-    first_tile = jnp.where(place_ref[1] == 0, 1, 0)
-    last_tile = jnp.where(place_ref[1] == place_ref[3] - 1, TILES + 1, TILES + 2)
+    first_tile = jnp.where(lax.axis_index("ty") == 0, 1, 0)
+    last_tile = jnp.where(lax.axis_index("ty") == lax.axis_size("ty") - 1, TILES + 1, TILES + 2)
     scale = jnp.where(inside, 1.0 / 6.5, 0.0)
     side = [jnp.where((t >= first_tile) & (t < last_tile), 1.0, 0.0) for t in (0, TILES + 1)]
     edge = {0: scale * side[0], TILES + 1: scale * side[1]}
@@ -546,8 +547,9 @@
 
 def swap(x, axis, first):
     size = lax.axis_size(axis)
-    pairs = [((first + i) % size, (first + i + 1) % size) for i in range(0, size, 2)]
-    return lax.ppermute(x, axis, pairs + [(j, i) for i, j in pairs])
+    pairs = [(i, i + 1) for i in range(first, size - 1, 2)]
+    ends = [(i, i) for i in range(size) if not any(i in pair for pair in pairs)]
+    return lax.ppermute(x, axis, pairs + [(j, i) for i, j in pairs] + ends)
 
 
 def on_device(
@@ -632,8 +634,6 @@
         points,
     )
 
-    place = jnp.stack([lax.axis_index("tx"), lax.axis_index("ty"), lax.axis_size("tx"), lax.axis_size("ty")])
-    place = place.astype(I32)
     volt = potential
     recov = gating
     for step in range(STEPS):
@@ -656,7 +656,7 @@
         deposit, x_near, x_far, y_near, y_far = pl.pallas_call(
             deposit_kernel,
             out_shape=(shaped(TILE * TILES, 128),) + (shaped(64, 128),) * 4,
-            in_specs=[SMEM] + [anywhere] * 4,
+            in_specs=[anywhere] * 4,
             out_specs=(VMEM,) * 5,
             scratch_shapes=[
                 pltpu.VMEM((DEVS * 16, 128), F32),
@@ -667,20 +667,20 @@
             ],
             compiler_params=PARAMS,
             name="deposit",
-        )(place, got, deposit_base, slot_points, phi)
-
-        x_far = swap(x_far, "tx", 1)
-        x_near = swap(x_near, "tx", 0)
-        y_near, y_far = pl.pallas_call(
+        )(got, deposit_base, slot_points, phi)
+
+        y_far = swap(y_far, "ty", 1)
+        y_near = swap(y_near, "ty", 0)
+        x_near, x_far = pl.pallas_call(
             frame_kernel,
             out_shape=(shaped(80, 128),) * 2,
-            in_specs=[SMEM] + [VMEM] * 4,
+            in_specs=[VMEM] * 4,
             out_specs=(VMEM,) * 2,
             compiler_params=PARAMS,
             name="frame",
-        )(place, x_near, x_far, y_near, y_far)
-        y_far = swap(y_far, "ty", 1)
-        y_near = swap(y_near, "ty", 0)
+        )(y_near, y_far, x_near, x_far)
+        x_far = swap(x_far, "tx", 1)
+        x_near = swap(x_near, "tx", 0)
         current = pl.pallas_call(
             collect_kernel,
             out_shape=shaped(CELLS, NODES),
@@ -700,8 +700,8 @@
             compiler_params=PARAMS,
             name="collect",
         )(into, own, got, base)
-        operands = [place, phi, deposit, x_near, x_far, y_near, y_far, current, volt, points]
-        specs = [SMEM] + [VMEM] * 6 + [anywhere] * 2 + [VMEM]
+        operands = [phi, deposit, x_near, x_far, y_near, y_far, current, volt, points]
+        specs = [VMEM] * 6 + [anywhere] * 2 + [VMEM]
         wide = [pltpu.VMEM((TILES + 2, LEAD + ROWS + 8, 128), F32)] * 2 + [pltpu.VMEM((16, CELLS), F32)]
         if last:
             volt, phi = pl.pallas_call(

time: 141 us -> 140 us (level)
  starting transfers between devices: 34.5 us -> 37 us
  waiting for transfers between devices: 26 us -> 24.3 us
    ppermute x8, waiting for transfers between devices: 9.75 us -> 7.24 us  [swap(): return lax.ppermute(x, axis, pairs + [(j, i) for i, j in pairs] + ends)]
    ppermute x8, starting transfers between devices: 9.47 us -> 11.4 us  [swap(): return lax.ppermute(x, axis, pairs + [(j, i) for i, j in pairs] + ends)]
  transfers between devices with their start and end apart: 11 -> 11, of which waited for: 7 -> 5; matrix products, arithmetic and copies ran while one was open for 2% -> 1% of each run, Pallas kernels for 31% -> 31%
where the time goes in v5:
time: 140 us; the launch traced here: 139 us
  Pallas kernels  74.9 us (54%)
  starting transfers between devices  37 us (26%)
  waiting for transfers between devices  24.3 us (17%)
  local copies, waits for them, and re-layouts  1.53 us (1%)
    all_to_all x3, starting transfers between devices, exchange(): return lax.all_to_all(x, AXES, split_axis=0, concat_axis=0, tiled=True)  25.5 us
    pallas_call x2, Pallas kernels, on_device(): pl.pallas_call(base_kernel, out_shape=(shaped(CELLS, NODES), shaped(TILE...  19.1 us
    all_to_all x3, waiting for transfers between devices, exchange(): return lax.all_to_all(x, AXES, split_axis=0, concat_axis=0, tiled=True)  17.1 us
    pallas_call x2, Pallas kernels, on_device(): pl.pallas_call(collect_kernel, out_shape=shaped(CELLS, NODES), in_specs=[...  14.7 us
    ppermute x8, starting transfers between devices, swap(): return lax.ppermute(x, axis, pairs + [(j, i) for i, j in pairs] + ends)  11.4 us
    pallas_call x1, Pallas kernels, on_device(): pl.pallas_call(functools.partial(sweep_kernel, False), out_shape=(shaped(...  9.24 us
    pallas_call x2, Pallas kernels, on_device(): pl.pallas_call(deposit_kernel, out_shape=(shaped(TILE * TILES, 128),) + (...  8.55 us
    ppermute x8, waiting for transfers between devices, swap(): return lax.ppermute(x, axis, pairs + [(j, i) for i, j in pairs] + ends)  7.24 us
  transfers between devices with their start and end apart: 11, of which 5 were waited for; matrix products, arithmetic and copies ran while one was open for 1% of the time, Pallas kernels for 31%

profile of v5, /device:TPU:1, one launch (start us, length us, event | category | flops | bytes accessed | tf_op | source)
XLA Modules:
  0.0 138.7 jit_solution(2543997342204832909)
XLA Ops:
  0.6 2.1 %setup.1.table_ref.refs_0_ = f32[128,128]{1,0:T(8,128)} custom-call(s32[8,128]{1,0:T(8,128)} %bitcast.21, s32[8,128]{1,0:T(8,128)} %bitcast.22, s32[8,128]{1,0:T(8,128)} %bitcast.23, f32[8,128]{1,0:T(8,128)} %bitcast.24), custom_call_target="tpu_custom_call" | custom-call | tf_op jit(solution)/shard_map/setup/pallas_call | solution.py:568
  2.7 11.9 %all-to-all-start = ((f32[128,1,128]{2,1,0:T(1,128)}), f32[128,1,128]{2,1,0:T(1,128)}, u32[]{:S(2)}, u32[]{:S(2)}) async-start(f32[128,1,128]{2,1,0:T(1,128)} %bitcast.14), calls=%async_computation | async-start | bytes 131072 | tf_op jit(solution)/shard_map/all_to_all | solution.py:545
  14.7 5.4 %gather_source.1 = (f32[128,16,128]{2,1,0:T(8,128)}, s32[16,128]{1,0:T(8,128)}, f32[1024,128]{1,0:T(8,128)}) custom-call(f32[128,128]{1,0:T(8,128)} %setup.1.table_ref.refs_0_, f32[256,768]{1,0:T(8,128)} %refs_7_.1), custom_call_target="tpu_custom_call" | custom-call | tf_op jit(solution)/shard_map/gather_source/pallas_call | solution.py:601
  20.1 4.1 %all-to-all-done = f32[128,1,128]{2,1,0:T(1,128)} async-done(((f32[128,1,128]{2,1,0:T(1,128)}), f32[128,1,128]{2,1,0:T(1,128)}, u32[]{:S(2)}, u32[]{:S(2)}) %all-to-all-start) | async-done | bytes 65568 | tf_op jit(solution)/shard_map/all_to_all | solution.py:545
  24.1 5.3 %gather_target.1 = (f32[128,16,128]{2,1,0:T(8,128)}, s32[16,128]{1,0:T(8,128)}, f32[1024,128]{1,0:T(8,128)}) custom-call(f32[128,128]{1,0:T(8,128)} %bitcast.6.got_table_ref.refs_0_, f32[256,768]{1,0:T(8,128)} %refs_7_.1, f32[128,16,128]{2,1,0:T(8,128)} %get-tuple-element.37.refs_2_), custom_call_target="tpu_custom_call", output_to_operand_aliasing={{0}: (2, {})} | custom-call | tf_op jit(solution)/shard_map/gather_target/pallas_call | solution.py:610
  29.5 6.2 %all-to-all-start.1 = ((f32[128,16,128]{2,1,0:T(8,128)}), f32[128,16,128]{2,1,0:T(8,128)}, u32[]{:S(2)}, u32[]{:S(2)}) async-start(f32[128,16,128]{2,1,0:T(8,128)} %get-tuple-element.38), calls=%async_computation.1 | async-start | bytes 2097152 | tf_op jit(solution)/shard_map/all_to_all | solution.py:545
  37.2 3.7 %prepare.1 = (f32[256,768]{1,0:T(8,128)}, f32[256,128]{1,0:T(8,128)}, f32[256,128]{1,0:T(8,128)}, s32[64,128]{1,0:T(8,128)}) custom-call(f32[128,128]{1,0:T(8,128)} %bitcast.6.got_table_ref.refs_0_, f32[128,128]{1,0:T(8,128)} %setup.1.table_ref.refs_0_, s32[2,128]{1,0:T(2,128)} %bitcast.25, f32[1024,32]{1,0:T(8,128)} %bitcast.20, s32[12,256]{1,0:T(8,128)} %bitcast.15), custom_call_target="tpu_custom_call" | custom-call | tf_op jit(solution)/shard_map/prepare/pallas_call | solution.py:621
  40.9 9.5 %base.2 = (f32[256,768]{1,0:T(8,128)}, f32[256,128]{1,0:T(8,128)}) custom-call(f32[256,768]{1,0:T(8,128)} %refs_7_.1, f32[256,768]{1,0:T(8,128)} %refs_9_.1, f32[256,128]{1,0:T(8,128)} %get-tuple-element.39.id_ref, f32[256,768]{1,0:T(8,128)} %get-tuple-element.40.degree_ref, s32[12,256]{1,0:T(8,128)} %bitcast.16, bf16[10,768,768]{2,1,0:T(8,128)(2,1)} %template_ref.3), custom_call_target="tpu_custom_call" | custom-call | flops 3000000000 | bytes 14000000 | tf_op jit(solution)/shard_map/base/pallas_call | solution.py:642
  50.4 3.9 %all-to-all-done.1 = f32[128,16,128]{2,1,0:T(8,128)} async-done(((f32[128,16,128]{2,1,0:T(8,128)}), f32[128,16,128]{2,1,0:T(8,128)}, u32[]{:S(2)}, u32[]{:S(2)}) %all-to-all-start.1) | async-done | bytes 1048608 | tf_op jit(solution)/shard_map/all_to_all | solution.py:545
  54.3 4.3 %deposit.2 = (f32[256,128]{1,0:T(8,128)}, f32[64,128]{1,0:T(8,128)}, f32[64,128]{1,0:T(8,128)}, f32[64,128]{1,0:T(8,128)}, f32[64,128]{1,0:T(8,128)}) custom-call(f32[2048,128]{1,0:T(8,128)} %bitcast.10.got_any, f32[256,128]{1,0:T(8,128)} %get-tuple-element.41.base_any, s32[64,128]{1,0:T(8,128)} %get-tuple-element.42.slot_any, ...), custom_call_target="tpu_custom_call" | custom-call | tf_op jit(solution)/shard_map/deposit/pallas_call | solution.py:656
  60.0 1.9 %collective-permute-start.1 = (f32[64,128]{1,0:T(8,128)}, f32[64,128]{1,0:T(8,128)}, u32[]{:S(2)}, u32[]{:S(2)}) collective-permute-start(f32[64,128]{1,0:T(8,128)} %get-tuple-element.45), channel_id=1, source_target_pairs={{1,2},{3,4},{5,6},{2,1},{4,3},{6,5},{0,0},{7,7},{9,10},{11,12},{13... | collective-permute-start | bytes 98312 | tf_op jit(solution)/shard_map/ppermute | solution.py:552
  61.9 3.6 %collective-permute-done.1.y_far_ref.refs_5_ = f32[64,128]{1,0:T(8,128)} collective-permute-done((f32[64,128]{1,0:T(8,128)}, f32[64,128]{1,0:T(8,128)}, u32[]{:S(2)}, u32[]{:S(2)}) %collective-permute-start.1) | collective-permute-done | bytes 32800 | tf_op jit(solution)/shard_map/ppermute | solution.py:552
  67.4 2.0 %collective-permute-start.3 = (f32[80,128]{1,0:T(8,128)}, f32[80,128]{1,0:T(8,128)}, u32[]{:S(2)}, u32[]{:S(2)}) collective-permute-start(f32[80,128]{1,0:T(8,128)} %get-tuple-element.49), channel_id=1, source_target_pairs={{8,16},{24,32},{40,48},{56,64},{72,80},{88,96},{104,112},{16,8},{3... | collective-permute-start | bytes 122888 | tf_op jit(solution)/shard_map/ppermute | solution.py:552
  69.4 7.3 %collect.2.refs_6_ = f32[256,768]{1,0:T(8,128)} custom-call(s32[16,128]{1,0:T(8,128)} %get-tuple-element.50.into_ref.refs_10_, s32[16,128]{1,0:T(8,128)} %get-tuple-element.51.own_ref.refs_12_, f32[2048,128]{1,0:T(8,128)} %bitcast.10.got_any, f32[256,768]{1,0:T(8,128)} %get-tuple-element.52.base_any), custom_call_target="tpu_custom_call" | custom-call | flops 1000000000 | bytes 10000000 | tf_op jit(solution)/shard_map/collect/pallas_call | solution.py:684
  76.7 9.2 %sweep.1 = (f32[256,768]{1,0:T(8,128)}, f32[256,128]{1,0:T(8,128)}, f32[256,768]{1,0:T(8,128)}, f32[128,16,128]{2,1,0:T(8,128)}) custom-call(f32[256,128]{1,0:T(8,128)} %get-tuple-element.36.phi_any.refs_0_, f32[256,128]{1,0:T(8,128)} %get-tuple-element.43.refs_1_, f32[80,128]{1,0:T(8,128)} %collective-permute-done.2.refs_2_, ...), custom_call_target="tpu_custom_call" | custom-call | tf_op jit(solution)/shard_map/sweep/pallas_call | solution.py:723
  86.0 7.4 %all-to-all-start.2 = ((f32[128,16,128]{2,1,0:T(8,128)}), f32[128,16,128]{2,1,0:T(8,128)}, u32[]{:S(2)}, u32[]{:S(2)}) async-start(f32[128,16,128]{2,1,0:T(8,128)} %get-tuple-element.56), calls=%async_computation.2 | async-start | bytes 2097152 | tf_op jit(solution)/shard_map/all_to_all | solution.py:545
  93.4 9.6 %base.3 = (f32[256,768]{1,0:T(8,128)}, f32[256,128]{1,0:T(8,128)}) custom-call(f32[256,768]{1,0:T(8,128)} %get-tuple-element.57.volt_ref.refs_7_, f32[256,768]{1,0:T(8,128)} %get-tuple-element.58.recov_ref, f32[256,128]{1,0:T(8,128)} %get-tuple-element.39.id_ref, f32[256,768]{1,0:T(8,128)} %get-tuple-element.40.degree_ref, s32[12,256]{1,0:T(8,128)} %bitcast.18, ...), custom_call_target="tpu_custom_call" | custom-call | flops 3000000000 | bytes 14000000 | tf_op jit(solution)/shard_map/base/pallas_call | solution.py:642
  103.0 9.1 %all-to-all-done.2 = f32[128,16,128]{2,1,0:T(8,128)} async-done(((f32[128,16,128]{2,1,0:T(8,128)}), f32[128,16,128]{2,1,0:T(8,128)}, u32[]{:S(2)}, u32[]{:S(2)}) %all-to-all-start.2) | async-done | bytes 1048608 | tf_op jit(solution)/shard_map/all_to_all | solution.py:545
  112.1 4.3 %deposit.3 = (f32[256,128]{1,0:T(8,128)}, f32[64,128]{1,0:T(8,128)}, f32[64,128]{1,0:T(8,128)}, f32[64,128]{1,0:T(8,128)}, f32[64,128]{1,0:T(8,128)}) custom-call(f32[2048,128]{1,0:T(8,128)} %bitcast.11.got_any, f32[256,128]{1,0:T(8,128)} %get-tuple-element.59.base_any, s32[64,128]{1,0:T(8,128)} %get-tuple-element.42.slot_any, ...), custom_call_target="tpu_custom_call" | custom-call | tf_op jit(solution)/shard_map/deposit/pallas_call | solution.py:656
  117.7 1.9 %collective-permute-start.5 = (f32[64,128]{1,0:T(8,128)}, f32[64,128]{1,0:T(8,128)}, u32[]{:S(2)}, u32[]{:S(2)}) collective-permute-start(f32[64,128]{1,0:T(8,128)} %get-tuple-element.62), channel_id=1, source_target_pairs={{1,2},{3,4},{5,6},{2,1},{4,3},{6,5},{0,0},{7,7},{9,10},{11,12},{13... | collective-permute-start | bytes 98312 | tf_op jit(solution)/shard_map/ppermute | solution.py:552
  119.6 3.6 %collective-permute-done.5.y_far_ref.refs_5_ = f32[64,128]{1,0:T(8,128)} collective-permute-done((f32[64,128]{1,0:T(8,128)}, f32[64,128]{1,0:T(8,128)}, u32[]{:S(2)}, u32[]{:S(2)}) %collective-permute-start.5) | collective-permute-done | bytes 32800 | tf_op jit(solution)/shard_map/ppermute | solution.py:552
  125.1 2.1 %collective-permute-start.7 = (f32[80,128]{1,0:T(8,128)}, f32[80,128]{1,0:T(8,128)}, u32[]{:S(2)}, u32[]{:S(2)}) collective-permute-start(f32[80,128]{1,0:T(8,128)} %get-tuple-element.66), channel_id=1, source_target_pairs={{8,16},{24,32},{40,48},{56,64},{72,80},{88,96},{104,112},{16,8},{3... | collective-permute-start | bytes 122888 | tf_op jit(solution)/shard_map/ppermute | solution.py:552
  127.1 7.3 %collect.3.refs_6_ = f32[256,768]{1,0:T(8,128)} custom-call(s32[16,128]{1,0:T(8,128)} %get-tuple-element.50.into_ref.refs_10_, s32[16,128]{1,0:T(8,128)} %get-tuple-element.51.own_ref.refs_12_, f32[2048,128]{1,0:T(8,128)} %bitcast.11.got_any, f32[256,768]{1,0:T(8,128)} %get-tuple-element.67.base_any), custom_call_target="tpu_custom_call" | custom-call | flops 1000000000 | bytes 10000000 | tf_op jit(solution)/shard_map/collect/pallas_call | solution.py:684
  134.5 4.0 %sweep_last.1 = (f32[256,768]{1,0:T(8,128)}, f32[1024,32]{1,0:T(8,128)}) custom-call(f32[256,128]{1,0:T(8,128)} %get-tuple-element.55.phi_any.refs_0_, f32[256,128]{1,0:T(8,128)} %get-tuple-element.60.refs_1_, f32[80,128]{1,0:T(8,128)} %collective-permute-done.6.refs_2_, f32[80,128]{1,0:T(8,128)} %collective-permute-done.7.refs_3_, ...), custom_call_target="tpu_custom_call" | custom-call | tf_op jit(solution)/shard_map/sweep_last/pallas_call | solution.py:707
  (14 shorter events, 8.0 us)
Async XLA Ops:
  2.7 21.4 %all-to-all-start = ((f32[128,1,128]{2,1,0:T(1,128)}), f32[128,1,128]{2,1,0:T(1,128)}, u32[]{:S(2)}, u32[]{:S(2)}) async-start(f32[128,1,128]{2,1,0:T(1,128)} %bitcast.14), calls=%async_computation | async-start | bytes 131072 | tf_op jit(solution)/shard_map/all_to_all | solution.py:545
  29.5 24.8 %all-to-all-start.1 = ((f32[128,16,128]{2,1,0:T(8,128)}), f32[128,16,128]{2,1,0:T(8,128)}, u32[]{:S(2)}, u32[]{:S(2)}) async-start(f32[128,16,128]{2,1,0:T(8,128)} %get-tuple-element.38), calls=%async_computation.1 | async-start | bytes 2097152 | tf_op jit(solution)/shard_map/all_to_all | solution.py:545
  58.6 3.3 %collective-permute-start = (f32[64,128]{1,0:T(8,128)}, f32[64,128]{1,0:T(8,128)}, u32[]{:S(2)}, u32[]{:S(2)}) collective-permute-start(f32[64,128]{1,0:T(8,128)} %get-tuple-element.44), channel_id=1, source_target_pairs={{0,1},{2,3},{4,5},{6,7},{1,0},{3,2},{5,4},{7,6},{8,9},{10,11},{12,... | collective-permute-start | bytes 98312 | tf_op jit(solution)/shard_map/ppermute | solution.py:552
  60.0 5.5 %collective-permute-start.1 = (f32[64,128]{1,0:T(8,128)}, f32[64,128]{1,0:T(8,128)}, u32[]{:S(2)}, u32[]{:S(2)}) collective-permute-start(f32[64,128]{1,0:T(8,128)} %get-tuple-element.45), channel_id=1, source_target_pairs={{1,2},{3,4},{5,6},{2,1},{4,3},{6,5},{0,0},{7,7},{9,10},{11,12},{13... | collective-permute-start | bytes 98312 | tf_op jit(solution)/shard_map/ppermute | solution.py:552
  67.0 9.7 %collective-permute-start.2 = (f32[80,128]{1,0:T(8,128)}, f32[80,128]{1,0:T(8,128)}, u32[]{:S(2)}, u32[]{:S(2)}) collective-permute-start(f32[80,128]{1,0:T(8,128)} %get-tuple-element.48), channel_id=1, source_target_pairs={{0,8},{16,24},{32,40},{48,56},{64,72},{80,88},{96,104},{112,120},{... | collective-permute-start | bytes 122888 | tf_op jit(solution)/shard_map/ppermute | solution.py:552
  67.4 9.4 %collective-permute-start.3 = (f32[80,128]{1,0:T(8,128)}, f32[80,128]{1,0:T(8,128)}, u32[]{:S(2)}, u32[]{:S(2)}) collective-permute-start(f32[80,128]{1,0:T(8,128)} %get-tuple-element.49), channel_id=1, source_target_pairs={{8,16},{24,32},{40,48},{56,64},{72,80},{88,96},{104,112},{16,8},{3... | collective-permute-start | bytes 122888 | tf_op jit(solution)/shard_map/ppermute | solution.py:552
  86.0 26.1 %all-to-all-start.2 = ((f32[128,16,128]{2,1,0:T(8,128)}), f32[128,16,128]{2,1,0:T(8,128)}, u32[]{:S(2)}, u32[]{:S(2)}) async-start(f32[128,16,128]{2,1,0:T(8,128)} %get-tuple-element.56), calls=%async_computation.2 | async-start | bytes 2097152 | tf_op jit(solution)/shard_map/all_to_all | solution.py:545
  116.3 3.3 %collective-permute-start.4 = (f32[64,128]{1,0:T(8,128)}, f32[64,128]{1,0:T(8,128)}, u32[]{:S(2)}, u32[]{:S(2)}) collective-permute-start(f32[64,128]{1,0:T(8,128)} %get-tuple-element.61), channel_id=1, source_target_pairs={{0,1},{2,3},{4,5},{6,7},{1,0},{3,2},{5,4},{7,6},{8,9},{10,11},{12,... | collective-permute-start | bytes 98312 | tf_op jit(solution)/shard_map/ppermute | solution.py:552
  117.7 5.5 %collective-permute-start.5 = (f32[64,128]{1,0:T(8,128)}, f32[64,128]{1,0:T(8,128)}, u32[]{:S(2)}, u32[]{:S(2)}) collective-permute-start(f32[64,128]{1,0:T(8,128)} %get-tuple-element.62), channel_id=1, source_target_pairs={{1,2},{3,4},{5,6},{2,1},{4,3},{6,5},{0,0},{7,7},{9,10},{11,12},{13... | collective-permute-start | bytes 98312 | tf_op jit(solution)/shard_map/ppermute | solution.py:552
  124.7 9.8 %collective-permute-start.6 = (f32[80,128]{1,0:T(8,128)}, f32[80,128]{1,0:T(8,128)}, u32[]{:S(2)}, u32[]{:S(2)}) collective-permute-start(f32[80,128]{1,0:T(8,128)} %get-tuple-element.65), channel_id=1, source_target_pairs={{0,8},{16,24},{32,40},{48,56},{64,72},{80,88},{96,104},{112,120},{... | collective-permute-start | bytes 122888 | tf_op jit(solution)/shard_map/ppermute | solution.py:552
  125.1 9.4 %collective-permute-start.7 = (f32[80,128]{1,0:T(8,128)}, f32[80,128]{1,0:T(8,128)}, u32[]{:S(2)}, u32[]{:S(2)}) collective-permute-start(f32[80,128]{1,0:T(8,128)} %get-tuple-element.66), channel_id=1, source_target_pairs={{8,16},{24,32},{40,48},{56,64},{72,80},{88,96},{104,112},{16,8},{3... | collective-permute-start | bytes 122888 | tf_op jit(solution)/shard_map/ppermute | solution.py:552

commit v6 on v5

--- a/solution.py
+++ b/solution.py
@@ -547,9 +547,8 @@
 
 def swap(x, axis, first):
     size = lax.axis_size(axis)
-    pairs = [(i, i + 1) for i in range(first, size - 1, 2)]
-    ends = [(i, i) for i in range(size) if not any(i in pair for pair in pairs)]
-    return lax.ppermute(x, axis, pairs + [(j, i) for i, j in pairs] + ends)
+    pairs = [((first + i) % size, (first + i + 1) % size) for i in range(0, size, 2)]
+    return lax.ppermute(x, axis, pairs + [(j, i) for i, j in pairs])
 
 
 def on_device(

time: 140 us -> 134 us (0.957)
  the two profiles are of different devices: /device:TPU:1 before, /device:TPU:0 now
where the time goes in v6:
time: 134 us; the launch traced here: 133 us
  Pallas kernels  75 us (56%)
  starting transfers between devices  28.7 us (21%)
  waiting for transfers between devices  26.9 us (20%)
  local copies, waits for them, and re-layouts  1.53 us (1%)
    all_to_all x3, starting transfers between devices, exchange(): return lax.all_to_all(x, AXES, split_axis=0, concat_axis=0, tiled=True)  24.9 us
    pallas_call x2, Pallas kernels, on_device(): pl.pallas_call(base_kernel, out_shape=(shaped(CELLS, NODES), shaped(TILE...  19.1 us
    all_to_all x3, waiting for transfers between devices, exchange(): return lax.all_to_all(x, AXES, split_axis=0, concat_axis=0, tiled=True)  17.5 us
    pallas_call x2, Pallas kernels, on_device(): pl.pallas_call(collect_kernel, out_shape=shaped(CELLS, NODES), in_specs=[...  14.7 us
    ppermute x8, waiting for transfers between devices, swap(): return lax.ppermute(x, axis, pairs + [(j, i) for i, j in pairs])  9.41 us
    pallas_call x1, Pallas kernels, on_device(): pl.pallas_call(functools.partial(sweep_kernel, False), out_shape=(shaped(...  9.24 us
    pallas_call x2, Pallas kernels, on_device(): pl.pallas_call(deposit_kernel, out_shape=(shaped(TILE * TILES, 128),) + (...  8.55 us
    pallas_call x1, Pallas kernels, on_device(): pl.pallas_call(functools.partial(gather_kernel, False), out_shape=(messag...  5.37 us
  transfers between devices with their start and end apart: 11, of which 7 were waited for; matrix products, arithmetic and copies ran while one was open for 1% of the time, Pallas kernels for 32%

profile of v6, /device:TPU:0, one launch (start us, length us, event | category | flops | bytes accessed | tf_op | source)
XLA Modules:
  0.0 133.1 jit_solution(938436584296540634)
XLA Ops:
  0.6 2.1 %setup.1.table_ref.refs_0_ = f32[128,128]{1,0:T(8,128)} custom-call(s32[8,128]{1,0:T(8,128)} %bitcast.21, s32[8,128]{1,0:T(8,128)} %bitcast.22, s32[8,128]{1,0:T(8,128)} %bitcast.23, f32[8,128]{1,0:T(8,128)} %bitcast.24), custom_call_target="tpu_custom_call" | custom-call | tf_op jit(solution)/shard_map/setup/pallas_call | solution.py:567
  2.7 11.7 %all-to-all-start = ((f32[128,1,128]{2,1,0:T(1,128)}), f32[128,1,128]{2,1,0:T(1,128)}, u32[]{:S(2)}, u32[]{:S(2)}) async-start(f32[128,1,128]{2,1,0:T(1,128)} %bitcast.14), calls=%async_computation | async-start | bytes 131072 | tf_op jit(solution)/shard_map/all_to_all | solution.py:545
  14.4 5.4 %gather_source.1 = (f32[128,16,128]{2,1,0:T(8,128)}, s32[16,128]{1,0:T(8,128)}, f32[1024,128]{1,0:T(8,128)}) custom-call(f32[128,128]{1,0:T(8,128)} %setup.1.table_ref.refs_0_, f32[256,768]{1,0:T(8,128)} %refs_7_.1), custom_call_target="tpu_custom_call" | custom-call | tf_op jit(solution)/shard_map/gather_source/pallas_call | solution.py:600
  19.8 4.2 %all-to-all-done = f32[128,1,128]{2,1,0:T(1,128)} async-done(((f32[128,1,128]{2,1,0:T(1,128)}), f32[128,1,128]{2,1,0:T(1,128)}, u32[]{:S(2)}, u32[]{:S(2)}) %all-to-all-start) | async-done | bytes 65568 | tf_op jit(solution)/shard_map/all_to_all | solution.py:545
  24.0 5.3 %gather_target.1 = (f32[128,16,128]{2,1,0:T(8,128)}, s32[16,128]{1,0:T(8,128)}, f32[1024,128]{1,0:T(8,128)}) custom-call(f32[128,128]{1,0:T(8,128)} %bitcast.6.got_table_ref.refs_0_, f32[256,768]{1,0:T(8,128)} %refs_7_.1, f32[128,16,128]{2,1,0:T(8,128)} %get-tuple-element.37.refs_2_), custom_call_target="tpu_custom_call", output_to_operand_aliasing={{0}: (2, {})} | custom-call | tf_op jit(solution)/shard_map/gather_target/pallas_call | solution.py:609
  29.3 6.1 %all-to-all-start.1 = ((f32[128,16,128]{2,1,0:T(8,128)}), f32[128,16,128]{2,1,0:T(8,128)}, u32[]{:S(2)}, u32[]{:S(2)}) async-start(f32[128,16,128]{2,1,0:T(8,128)} %get-tuple-element.38), calls=%async_computation.1 | async-start | bytes 2097152 | tf_op jit(solution)/shard_map/all_to_all | solution.py:545
  36.9 3.7 %prepare.1 = (f32[256,768]{1,0:T(8,128)}, f32[256,128]{1,0:T(8,128)}, f32[256,128]{1,0:T(8,128)}, s32[64,128]{1,0:T(8,128)}) custom-call(f32[128,128]{1,0:T(8,128)} %bitcast.6.got_table_ref.refs_0_, f32[128,128]{1,0:T(8,128)} %setup.1.table_ref.refs_0_, s32[2,128]{1,0:T(2,128)} %bitcast.25, f32[1024,32]{1,0:T(8,128)} %bitcast.20, s32[12,256]{1,0:T(8,128)} %bitcast.15), custom_call_target="tpu_custom_call" | custom-call | tf_op jit(solution)/shard_map/prepare/pallas_call | solution.py:620
  40.6 9.5 %base.2 = (f32[256,768]{1,0:T(8,128)}, f32[256,128]{1,0:T(8,128)}) custom-call(f32[256,768]{1,0:T(8,128)} %refs_7_.1, f32[256,768]{1,0:T(8,128)} %refs_9_.1, f32[256,128]{1,0:T(8,128)} %get-tuple-element.39.id_ref, f32[256,768]{1,0:T(8,128)} %get-tuple-element.40.degree_ref, s32[12,256]{1,0:T(8,128)} %bitcast.16, bf16[10,768,768]{2,1,0:T(8,128)(2,1)} %template_ref.3), custom_call_target="tpu_custom_call" | custom-call | flops 3000000000 | bytes 14000000 | tf_op jit(solution)/shard_map/base/pallas_call | solution.py:641
  50.2 4.1 %all-to-all-done.1 = f32[128,16,128]{2,1,0:T(8,128)} async-done(((f32[128,16,128]{2,1,0:T(8,128)}), f32[128,16,128]{2,1,0:T(8,128)}, u32[]{:S(2)}, u32[]{:S(2)}) %all-to-all-start.1) | async-done | bytes 1048608 | tf_op jit(solution)/shard_map/all_to_all | solution.py:545
  54.2 4.3 %deposit.2 = (f32[256,128]{1,0:T(8,128)}, f32[64,128]{1,0:T(8,128)}, f32[64,128]{1,0:T(8,128)}, f32[64,128]{1,0:T(8,128)}, f32[64,128]{1,0:T(8,128)}) custom-call(f32[2048,128]{1,0:T(8,128)} %bitcast.10.got_any, f32[256,128]{1,0:T(8,128)} %get-tuple-element.41.base_any, s32[64,128]{1,0:T(8,128)} %get-tuple-element.42.slot_any, ...), custom_call_target="tpu_custom_call" | custom-call | tf_op jit(solution)/shard_map/deposit/pallas_call | solution.py:655
  58.9 1.3 collective-permute-done.y_near_ref.refs_4_
  60.2 3.4 %collective-permute-done.1.y_far_ref.refs_5_ = f32[64,128]{1,0:T(8,128)} collective-permute-done((f32[64,128]{1,0:T(8,128)}, f32[64,128]{1,0:T(8,128)}, u32[]{:S(2)}, u32[]{:S(2)}) %collective-permute-start.1) | collective-permute-done | bytes 32800 | tf_op jit(solution)/shard_map/ppermute | solution.py:551
  63.6 1.4 %frame.2 = (f32[80,128]{1,0:T(8,128)}, f32[80,128]{1,0:T(8,128)}) custom-call(f32[64,128]{1,0:T(8,128)} %collective-permute-done.y_near_ref.refs_4_, f32[64,128]{1,0:T(8,128)} %collective-permute-done.1.y_far_ref.refs_5_, f32[64,128]{1,0:T(8,128)} %get-tuple-element.46.x_near_ref, f32[64,128]{1,0:T(8,128)} %get-tuple-element.47.x_far_ref), custom_call_target="tpu_custom_call" | custom-call | tf_op jit(solution)/shard_map/frame/pallas_call | solution.py:673
  66.7 7.3 %collect.2.refs_6_ = f32[256,768]{1,0:T(8,128)} custom-call(s32[16,128]{1,0:T(8,128)} %get-tuple-element.50.into_ref.refs_10_, s32[16,128]{1,0:T(8,128)} %get-tuple-element.51.own_ref.refs_12_, f32[2048,128]{1,0:T(8,128)} %bitcast.10.got_any, f32[256,768]{1,0:T(8,128)} %get-tuple-element.52.base_any), custom_call_target="tpu_custom_call" | custom-call | flops 1000000000 | bytes 10000000 | tf_op jit(solution)/shard_map/collect/pallas_call | solution.py:683
  74.0 9.2 %sweep.1 = (f32[256,768]{1,0:T(8,128)}, f32[256,128]{1,0:T(8,128)}, f32[256,768]{1,0:T(8,128)}, f32[128,16,128]{2,1,0:T(8,128)}) custom-call(f32[256,128]{1,0:T(8,128)} %get-tuple-element.36.phi_any.refs_0_, f32[256,128]{1,0:T(8,128)} %get-tuple-element.43.refs_1_, f32[80,128]{1,0:T(8,128)} %collective-permute-done.2.refs_2_, ...), custom_call_target="tpu_custom_call" | custom-call | tf_op jit(solution)/shard_map/sweep/pallas_call | solution.py:722
  83.3 7.1 %all-to-all-start.2 = ((f32[128,16,128]{2,1,0:T(8,128)}), f32[128,16,128]{2,1,0:T(8,128)}, u32[]{:S(2)}, u32[]{:S(2)}) async-start(f32[128,16,128]{2,1,0:T(8,128)} %get-tuple-element.56), calls=%async_computation.2 | async-start | bytes 2097152 | tf_op jit(solution)/shard_map/all_to_all | solution.py:545
  90.4 9.6 %base.3 = (f32[256,768]{1,0:T(8,128)}, f32[256,128]{1,0:T(8,128)}) custom-call(f32[256,768]{1,0:T(8,128)} %get-tuple-element.57.volt_ref.refs_7_, f32[256,768]{1,0:T(8,128)} %get-tuple-element.58.recov_ref, f32[256,128]{1,0:T(8,128)} %get-tuple-element.39.id_ref, f32[256,768]{1,0:T(8,128)} %get-tuple-element.40.degree_ref, s32[12,256]{1,0:T(8,128)} %bitcast.18, ...), custom_call_target="tpu_custom_call" | custom-call | flops 3000000000 | bytes 14000000 | tf_op jit(solution)/shard_map/base/pallas_call | solution.py:641
  100.0 9.3 %all-to-all-done.2 = f32[128,16,128]{2,1,0:T(8,128)} async-done(((f32[128,16,128]{2,1,0:T(8,128)}), f32[128,16,128]{2,1,0:T(8,128)}, u32[]{:S(2)}, u32[]{:S(2)}) %all-to-all-start.2) | async-done | bytes 1048608 | tf_op jit(solution)/shard_map/all_to_all | solution.py:545
  109.2 4.3 %deposit.3 = (f32[256,128]{1,0:T(8,128)}, f32[64,128]{1,0:T(8,128)}, f32[64,128]{1,0:T(8,128)}, f32[64,128]{1,0:T(8,128)}, f32[64,128]{1,0:T(8,128)}) custom-call(f32[2048,128]{1,0:T(8,128)} %bitcast.11.got_any, f32[256,128]{1,0:T(8,128)} %get-tuple-element.59.base_any, s32[64,128]{1,0:T(8,128)} %get-tuple-element.42.slot_any, ...), custom_call_target="tpu_custom_call" | custom-call | tf_op jit(solution)/shard_map/deposit/pallas_call | solution.py:655
  113.9 1.3 collective-permute-done.4.y_near_ref.refs_4_
  115.1 3.4 %collective-permute-done.5.y_far_ref.refs_5_ = f32[64,128]{1,0:T(8,128)} collective-permute-done((f32[64,128]{1,0:T(8,128)}, f32[64,128]{1,0:T(8,128)}, u32[]{:S(2)}, u32[]{:S(2)}) %collective-permute-start.5) | collective-permute-done | bytes 32800 | tf_op jit(solution)/shard_map/ppermute | solution.py:551
  118.6 1.4 %frame.3 = (f32[80,128]{1,0:T(8,128)}, f32[80,128]{1,0:T(8,128)}) custom-call(f32[64,128]{1,0:T(8,128)} %collective-permute-done.4.y_near_ref.refs_4_, f32[64,128]{1,0:T(8,128)} %collective-permute-done.5.y_far_ref.refs_5_, f32[64,128]{1,0:T(8,128)} %get-tuple-element.63.x_near_ref, f32[64,128]{1,0:T(8,128)} %get-tuple-element.64.x_far_ref), custom_call_target="tpu_custom_call" | custom-call | tf_op jit(solution)/shard_map/frame/pallas_call | solution.py:673
  121.5 7.4 %collect.3.refs_6_ = f32[256,768]{1,0:T(8,128)} custom-call(s32[16,128]{1,0:T(8,128)} %get-tuple-element.50.into_ref.refs_10_, s32[16,128]{1,0:T(8,128)} %get-tuple-element.51.own_ref.refs_12_, f32[2048,128]{1,0:T(8,128)} %bitcast.11.got_any, f32[256,768]{1,0:T(8,128)} %get-tuple-element.67.base_any), custom_call_target="tpu_custom_call" | custom-call | flops 1000000000 | bytes 10000000 | tf_op jit(solution)/shard_map/collect/pallas_call | solution.py:683
  128.9 4.0 %sweep_last.1 = (f32[256,768]{1,0:T(8,128)}, f32[1024,32]{1,0:T(8,128)}) custom-call(f32[256,128]{1,0:T(8,128)} %get-tuple-element.55.phi_any.refs_0_, f32[256,128]{1,0:T(8,128)} %get-tuple-element.60.refs_1_, f32[80,128]{1,0:T(8,128)} %collective-permute-done.6.refs_2_, f32[80,128]{1,0:T(8,128)} %collective-permute-done.7.refs_3_, ...), custom_call_target="tpu_custom_call" | custom-call | tf_op jit(solution)/shard_map/sweep_last/pallas_call | solution.py:706
  (14 shorter events, 5.3 us)
Async XLA Ops:
  2.7 21.3 %all-to-all-start = ((f32[128,1,128]{2,1,0:T(1,128)}), f32[128,1,128]{2,1,0:T(1,128)}, u32[]{:S(2)}, u32[]{:S(2)}) async-start(f32[128,1,128]{2,1,0:T(1,128)} %bitcast.14), calls=%async_computation | async-start | bytes 131072 | tf_op jit(solution)/shard_map/all_to_all | solution.py:545
  29.3 24.9 %all-to-all-start.1 = ((f32[128,16,128]{2,1,0:T(8,128)}), f32[128,16,128]{2,1,0:T(8,128)}, u32[]{:S(2)}, u32[]{:S(2)}) async-start(f32[128,16,128]{2,1,0:T(8,128)} %get-tuple-element.38), calls=%async_computation.1 | async-start | bytes 2097152 | tf_op jit(solution)/shard_map/all_to_all | solution.py:545
  58.5 1.6 %collective-permute-start = (f32[64,128]{1,0:T(8,128)}, f32[64,128]{1,0:T(8,128)}, u32[]{:S(2)}, u32[]{:S(2)}) collective-permute-start(f32[64,128]{1,0:T(8,128)} %get-tuple-element.44), channel_id=1, source_target_pairs={{0,1},{2,3},{4,5},{6,7},{1,0},{3,2},{5,4},{7,6},{8,9},{10,11},{12,... | collective-permute-start | bytes 98312 | tf_op jit(solution)/shard_map/ppermute | solution.py:551
  58.6 4.9 %collective-permute-start.1 = (f32[64,128]{1,0:T(8,128)}, f32[64,128]{1,0:T(8,128)}, u32[]{:S(2)}, u32[]{:S(2)}) collective-permute-start(f32[64,128]{1,0:T(8,128)} %get-tuple-element.45), channel_id=1, source_target_pairs={{1,2},{3,4},{5,6},{7,0},{2,1},{4,3},{6,5},{0,7},{9,10},{11,12},{13... | collective-permute-start | bytes 98312 | tf_op jit(solution)/shard_map/ppermute | solution.py:551
  65.0 9.0 %collective-permute-start.2 = (f32[80,128]{1,0:T(8,128)}, f32[80,128]{1,0:T(8,128)}, u32[]{:S(2)}, u32[]{:S(2)}) collective-permute-start(f32[80,128]{1,0:T(8,128)} %get-tuple-element.48), channel_id=1, source_target_pairs={{0,8},{16,24},{32,40},{48,56},{64,72},{80,88},{96,104},{112,120},{... | collective-permute-start | bytes 122888 | tf_op jit(solution)/shard_map/ppermute | solution.py:551
  65.7 8.3 %collective-permute-start.3 = (f32[80,128]{1,0:T(8,128)}, f32[80,128]{1,0:T(8,128)}, u32[]{:S(2)}, u32[]{:S(2)}) collective-permute-start(f32[80,128]{1,0:T(8,128)} %get-tuple-element.49), channel_id=1, source_target_pairs={{8,16},{24,32},{40,48},{56,64},{72,80},{88,96},{104,112},{120,0},{... | collective-permute-start | bytes 122888 | tf_op jit(solution)/shard_map/ppermute | solution.py:551
  83.3 26.0 %all-to-all-start.2 = ((f32[128,16,128]{2,1,0:T(8,128)}), f32[128,16,128]{2,1,0:T(8,128)}, u32[]{:S(2)}, u32[]{:S(2)}) async-start(f32[128,16,128]{2,1,0:T(8,128)} %get-tuple-element.56), calls=%async_computation.2 | async-start | bytes 2097152 | tf_op jit(solution)/shard_map/all_to_all | solution.py:545
  113.5 1.6 %collective-permute-start.4 = (f32[64,128]{1,0:T(8,128)}, f32[64,128]{1,0:T(8,128)}, u32[]{:S(2)}, u32[]{:S(2)}) collective-permute-start(f32[64,128]{1,0:T(8,128)} %get-tuple-element.61), channel_id=1, source_target_pairs={{0,1},{2,3},{4,5},{6,7},{1,0},{3,2},{5,4},{7,6},{8,9},{10,11},{12,... | collective-permute-start | bytes 98312 | tf_op jit(solution)/shard_map/ppermute | solution.py:551
  113.6 4.9 %collective-permute-start.5 = (f32[64,128]{1,0:T(8,128)}, f32[64,128]{1,0:T(8,128)}, u32[]{:S(2)}, u32[]{:S(2)}) collective-permute-start(f32[64,128]{1,0:T(8,128)} %get-tuple-element.62), channel_id=1, source_target_pairs={{1,2},{3,4},{5,6},{7,0},{2,1},{4,3},{6,5},{0,7},{9,10},{11,12},{13... | collective-permute-start | bytes 98312 | tf_op jit(solution)/shard_map/ppermute | solution.py:551
  120.0 8.8 %collective-permute-start.6 = (f32[80,128]{1,0:T(8,128)}, f32[80,128]{1,0:T(8,128)}, u32[]{:S(2)}, u32[]{:S(2)}) collective-permute-start(f32[80,128]{1,0:T(8,128)} %get-tuple-element.65), channel_id=1, source_target_pairs={{0,8},{16,24},{32,40},{48,56},{64,72},{80,88},{96,104},{112,120},{... | collective-permute-start | bytes 122888 | tf_op jit(solution)/shard_map/ppermute | solution.py:551
  120.7 8.2 %collective-permute-start.7 = (f32[80,128]{1,0:T(8,128)}, f32[80,128]{1,0:T(8,128)}, u32[]{:S(2)}, u32[]{:S(2)}) collective-permute-start(f32[80,128]{1,0:T(8,128)} %get-tuple-element.66), channel_id=1, source_target_pairs={{8,16},{24,32},{40,48},{56,64},{72,80},{88,96},{104,112},{120,0},{... | collective-permute-start | bytes 122888 | tf_op jit(solution)/shard_map/ppermute | solution.py:551
